TPU v7x, 512 devices: a whole 4x4x16 slice. The times are simulated.
512 devices in a mesh: tok: 32 (over z, core), feat: 16 (over y, x).
Axes of the slice: x: 4, y: 4, z: 16, core: 2. Of those that a mesh axis runs over, the one named last changes fastest.
Arguments:
- tokens: bfloat16 [12288, 1408], P(('tok', 'feat')), may hold values from -24 to 24
- segment_ids: int32 [12288], P('tok'), may hold values from 0 to 1023, as said below
- owners: int32 [1024], P('tok'), may hold values from 0 to 31, as said below
- project_in: bfloat16 [1408, 3, 1408], P(None, None, 'feat'), may hold values from -2 to 2
- project_out: bfloat16 [1408, 1408], P('feat'), may hold values from -0.15625 to 0.15625
- weight_up: bfloat16 [1408, 6144], P('tok', 'feat'), may hold values from -0.15625 to 0.15625
- weight_down: bfloat16 [6144, 1408], P('feat', 'tok'), may hold values from -0.078125 to 0.078125
- weight_merge: bfloat16 [5632, 4096], P(None, 'feat'), may hold values from -0.078125 to 0.078125
- gain_attend: bfloat16 [1408], replicated, may hold values from 0.25 to 1.75
- gain_hidden: bfloat16 [1408], replicated, may hold values from 0.25 to 1.75
- gain_final: bfloat16 [1408], replicated, may hold values from 0.25 to 1.75
Outputs:
- routed: bfloat16 [16384, 4096], P('tok', 'feat')
Inputs may be any that keep to these rules, and one draw needn't show every extreme that they name: `segment_ids`: patches 384 * s to 384 * s + 383 form shard s; their ids never fall, run without gaps and lie in 32 * s to 32 * s + 31; in every shard but the last they start at 32 * s, in the last they end at 1023. Every segment has 16 to 64 patches, a multiple of 4, and every shard holds one of 64 patches. Each 2x2 window of an image is four consecutive patches. owners[g] is the tok index that owns segment g; the 32 entries from 32 * s to 32 * s + 31 are distinct.
All inputs are finite; a program needn't handle non-finite values.
Results may differ from a plain program's by a relative error of at most 0.025.
Values may be sent and summed in bfloat16 or wider, within the bound.
A program may use at most 64 MiB of HBM per device.

v0:
```python
import jax
import jax.numpy as jnp
from jax import lax
from jax.sharding import PartitionSpec as P

LEAST_UNITS = 4
MOST_UNITS = 16
HEAD_DIM = 88


epsilon = 1e-06


def layer_norm(row_block, gain_row):
    as_float = row_block.astype(jnp.float32)
    center = jnp.mean(as_float, axis=-1, keepdims=True)
    spread = jnp.mean(jnp.square(as_float - center), axis=-1, keepdims=True)
    scaled = (as_float - center) * lax.rsqrt(spread + epsilon) * gain_row.astype(jnp.float32)
    return scaled.astype(jnp.bfloat16)


def project_rows(row_block, weight_block):
    return jnp.dot(
        lax.all_gather(row_block, "feat", axis=0, tiled=True),
        weight_block,
        preferred_element_type=jnp.float32,
    )


def scatter_rows(left_rows, right_rows):
    return lax.psum_scatter(
        jnp.dot(left_rows, right_rows, preferred_element_type=jnp.float32).astype(jnp.bfloat16),
        "feat",
        scatter_dimension=0,
        tiled=True,
    ).astype(jnp.float32)


def early_weights(weight_up, weight_down):
    return (weight_up, weight_down)


def upper_weight(fetched):
    return lax.all_gather(fetched[0], "tok", axis=0, tiled=True)


def lower_weight(fetched):
    return lax.all_gather(fetched[1], "tok", axis=1, tiled=True)


def attend(projected, segment_ids, head_count):
    token_count = projected.shape[0]
    parts_all = projected.reshape(token_count, 3, head_count, HEAD_DIM)
    queries = (parts_all[:, 0] * HEAD_DIM ** (-0.5)).astype(jnp.bfloat16)
    keys_here = parts_all[:, 1].astype(jnp.bfloat16)
    values_here = parts_all[:, 2].astype(jnp.bfloat16)
    scores = jnp.einsum("qhd,khd->hqk", queries, keys_here, preferred_element_type=jnp.float32)
    same_segment = segment_ids[:, None] == segment_ids[None, :]
    scores = jnp.where(same_segment[None, :, :], scores, -1e30)
    highest = jnp.max(scores, axis=-1, keepdims=True)
    raised = jnp.exp(scores - highest)
    weights_soft = (raised / jnp.sum(raised, axis=-1, keepdims=True)).astype(jnp.bfloat16)
    attended = jnp.einsum(
        "hqk,khd->qhd", weights_soft, values_here, preferred_element_type=jnp.float32
    )
    return attended.astype(jnp.bfloat16).reshape(token_count, head_count * HEAD_DIM)


def route_rows(embedded, segment_ids, owners):
    merged_count = embedded.shape[0]
    peer_count = owners.shape[0]
    least_units = max(LEAST_UNITS, (merged_count + peer_count - 1) // peer_count)
    slot_count = max(MOST_UNITS, 2 * least_units)
    first_ids = segment_ids.reshape(merged_count, 4)[:, 0]
    id_base = lax.axis_index("tok") * peer_count
    local_index = first_ids - id_base
    owner_pick = local_index[:, None] == jnp.arange(peer_count, dtype=jnp.int32)[None, :]
    owner_of = jnp.sum(jnp.where(owner_pick, owners[None, :], 0), axis=1)
    row_index = jnp.arange(merged_count, dtype=jnp.int32)
    earlier = (row_index[None, :] < row_index[:, None]) & (first_ids[None, :] == first_ids[:, None])
    within = jnp.sum(earlier.astype(jnp.int32), axis=1)
    target = owner_of * slot_count + within
    select = (
        jnp.arange(peer_count * slot_count, dtype=jnp.int32)[:, None] == target[None, :]
    ).astype(jnp.bfloat16)
    packed = jnp.dot(select, embedded, preferred_element_type=jnp.float32).astype(jnp.bfloat16)
    packed = packed.reshape(peer_count, slot_count, embedded.shape[1])
    received = lax.all_to_all(packed, "tok", split_axis=0, concat_axis=0, tiled=True)
    return received.reshape(peer_count * slot_count, embedded.shape[1])


def body(
    tokens,
    segment_ids,
    owners,
    project_in,
    project_out,
    weight_up,
    weight_down,
    weight_merge,
    gain_attend,
    gain_hidden,
    gain_final,
):
    model_width = tokens.shape[1]
    head_count = project_in.shape[2] // HEAD_DIM
    fetched = early_weights(weight_up, weight_down)
    flat_in = project_in.reshape(model_width, 3 * project_in.shape[2])
    local_count = tokens.shape[0]
    normed = layer_norm(tokens, gain_attend)
    projected = project_rows(normed, flat_in)
    attended = attend(projected, segment_ids, head_count)
    second = (tokens.astype(jnp.float32) + scatter_rows(attended, project_out)).astype(jnp.bfloat16)
    normed_hidden = layer_norm(second, gain_hidden)
    hidden = jax.nn.gelu(
        project_rows(normed_hidden, upper_weight(fetched)), approximate=False
    ).astype(jnp.bfloat16)
    residual_out = (
        second.astype(jnp.float32) + scatter_rows(hidden, lower_weight(fetched))
    ).astype(jnp.bfloat16)
    normed_final = layer_norm(residual_out, gain_final)
    merged = normed_final.reshape(local_count // 4, 4 * model_width)
    embedded = project_rows(merged, weight_merge).astype(jnp.bfloat16)
    return route_rows(embedded, segment_ids, owners)


def solution(mesh):
    return jax.shard_map(
        body,
        mesh=mesh,
        in_specs=(
            P(("tok", "feat"), None),
            P("tok"),
            P("tok"),
            P(None, None, "feat"),
            P("feat", None),
            P("tok", "feat"),
            P("feat", "tok"),
            P(None, "feat"),
            P(),
            P(),
            P(),
        ),
        out_specs=P("tok", "feat"),
        check_vma=False,
    )
```

profile of v0, /device:TPU:1, one launch (start us, length us, event | category | flops | bytes accessed | tf_op | source)
XLA Modules:
  0.0 485.8 jit_solution(15327780551669928933)
XLA Ops:
  7.4 1.2 convert_reduce_fusion.1
  8.5 1.1 fusion.58
  9.6 0.7 convert_element_type.98
  10.3 1.6 fusion.60
  12.0 62.1 %all-gather.9.cloned.1.call-done = bf16[384,1408]{1,0:T(8,128)(2,1)} async-done(((bf16[24,1408]{1,0:T(8,128)(2,1)}), bf16[384,1408]{1,0:T(8,128)(2,1)}) %all-gather.9.cloned.1.call-update) | async-done | bytes 1081360 | tf_op jit(solution)/shard_map/all_gather | solution.py:24
  74.1 2.0 fusion.104
  76.9 2.6 convolution_convert_fusion.1
  80.8 86.1 %reduce-scatter.7.cloned.1.call-done = bf16[24,1408]{1,0:T(8,128)(2,1)} async-done(((bf16[384,1408]{1,0:T(8,128)(2,1)}), bf16[24,1408]{1,0:T(8,128)(2,1)}) %reduce-scatter.7.cloned.1.call-update) | async-done | bytes 67600
  167.0 1.0 convert_reduce_fusion
  168.2 0.7 fusion.57
  169.0 2.2 reshape.121
  171.2 53.8 %all-gather.15.cloned.1.call-done = bf16[32,44,384]{2,1,0:T(8,128)(2,1)} async-done(((bf16[1,44,384]{2,1,0:T(8,128)(2,1)}), bf16[32,44,384]{2,1,0:T(8,128)(2,1)}) %all-gather.15.cloned.1.call-update) | async-done | bytes 1081360 | tf_op jit(solution)/shard_map/all_gather | solution.py:48
  225.1 2.2 reshape.123
  227.3 53.9 %all-gather.11.cloned.1.call-done = bf16[384,1408]{1,0:T(8,128)(2,1)} async-done(((bf16[24,1408]{1,0:T(8,128)(2,1)}), bf16[384,1408]{1,0:T(8,128)(2,1)}) %all-gather.11.cloned.1.call-update) | async-done | bytes 1081360 | tf_op jit(solution)/shard_map/all_gather | solution.py:24
  281.2 5.5 %convolution_convert_fusion = bf16[384,1408]{1,0:T(8,128)(2,1)} fusion(bf16[1408,384]{1,0:T(8,128)(2,1)} %reshape.123, bf16[384,1408]{1,0:T(8,128)(2,1)} %all-gather.11.cloned.1.call-done, bf16[1408,384]{1,0:T(8,128)(2,1)} %reshape.121), kind=kOutput, calls=%fused_computation | convolution fusion | flops 840597504 | bytes 4325376 | tf_op jit(solution)/shard_map/dot_general | solution.py:32
  287.4 87.0 %reduce-scatter.9.cloned.1.call-done = bf16[24,1408]{1,0:T(8,128)(2,1)} async-done(((bf16[384,1408]{1,0:T(8,128)(2,1)}), bf16[24,1408]{1,0:T(8,128)(2,1)}) %reduce-scatter.9.cloned.1.call-update) | async-done | bytes 67600
  374.4 1.0 convert_reduce_fusion.2
  375.5 1.1 fusion.61
  376.6 1.0 fusion.63
  378.8 57.7 %all-gather.17.cloned.1.call-done = bf16[16,6,5632]{2,1,0:T(8,128)(2,1)} async-done(((bf16[1,6,5632]{2,1,0:T(8,128)(2,1)}), bf16[16,6,5632]{2,1,0:T(8,128)(2,1)}) %all-gather.17.cloned.1.call-update) | async-done | bytes 1081360 | tf_op jit(solution)/shard_map/all_gather | solution.py:24
  436.5 2.3 reshape.125
  438.8 2.1 convolution_convert_fusion.2
  441.0 36.8 %all_to_all.5 = bf16[32,16,256]{2,1,0:T(8,128)(2,1)S(1)} all-to-all(bf16[32,16,256]{2,1,0:T(8,128)(2,1)S(1)} %bitcast.51), channel_id=1, replica_groups=mesh['tok'=32,'feat'=16] {'tok'}, dimensions={0} | all-to-all | bytes 524288 | tf_op jit(solution)/shard_map/all_to_all | solution.py:88
  477.8 0.7 copy.13
  (46 shorter events, 4.3 us)
Async XLA Ops:
  7.4 431.5 %copy-start = (bf16[5632,256]{1,0:T(8,128)(2,1)S(1)}, bf16[5632,256]{1,0:T(8,128)(2,1)}, u32[]{:S(2)}) copy-start(bf16[5632,256]{1,0:T(8,128)(2,1)} %param.18) | copy-start | bytes 8650756
  7.4 66.7 %all-gather.9.cloned.1.call-start = ((), (), s32[]{:S(2)}) async-start(), calls=%async_computation.3 | async-start | bytes 1148928 | tf_op jit(solution)/shard_map/all_gather | solution.py:24
  11.9 64.2 %copy-start.3 = (s32[384]{0:T(512)S(1)}, s32[384]{0:T(512)}, u32[]{:S(2)}) copy-start(s32[384]{0:T(512)} %param.12) | copy-start | bytes 4612
  12.0 155.0 %reduce-scatter.7.cloned.1.call-start = ((), (), s32[]{:S(2)}) async-start(), calls=%async_computation.8 | async-start | bytes 1148928
  76.1 0.7 copy-start.2
  79.6 1.2 copy-start.4
  79.6 87.4 %copy-start.1 = (bf16[24,1408]{1,0:T(8,128)(2,1)S(1)}, bf16[24,1408]{1,0:T(8,128)(2,1)}, u32[]{:S(2)}) copy-start(bf16[24,1408]{1,0:T(8,128)(2,1)} %param.11) | copy-start | bytes 202756
  79.6 89.4 %all-gather.13.cloned.1.call-start = ((), (), s32[]{:S(2)}) async-start(), calls=%async_computation.5 | async-start | bytes 1216512 | tf_op jit(solution)/shard_map/all_gather | solution.py:44
  80.2 144.9 %all-gather.15.cloned.1.call-start = ((), (), s32[]{:S(2)}) async-start(), calls=%async_computation.6 | async-start | bytes 1216512 | tf_op jit(solution)/shard_map/all_gather | solution.py:48
  80.8 200.4 %all-gather.11.cloned.1.call-start = ((), (), s32[]{:S(2)}) async-start(), calls=%async_computation.4 | async-start | bytes 1148928 | tf_op jit(solution)/shard_map/all_gather | solution.py:24
  169.0 205.5 %reduce-scatter.9.cloned.1.call-start = ((), (), s32[]{:S(2)}) async-start(), calls=%async_computation.9 | async-start | bytes 1148928
  286.7 0.7 copy-start.5
  286.7 91.9 %copy-start.6 = (s32[32]{0:T(128)S(1)}, s32[32]{0:T(128)}, u32[]{:S(2)}) copy-start(s32[32]{0:T(128)} %param.13) | copy-start | bytes 388
  286.8 149.8 %all-gather.17.cloned.1.call-start = ((), (), s32[]{:S(2)}) async-start(), calls=%async_computation.7 | async-start | bytes 1531904 | tf_op jit(solution)/shard_map/all_gather | solution.py:24
Sparse Core Ops, SparseCore 0:
  12.1 61.9 all-gather.8
  79.7 87.1 reduce-scatter.6
  286.9 87.5 reduce-scatter.8
Sparse Core Ops, SparseCore 1:
  82.2 72.5 all-gather.12
  156.7 68.3 all-gather.14
  228.0 53.2 all-gather.10
  378.3 58.1 all-gather.16
where the time goes:
time: 486 us
  waiting for transfers between devices  402 us (83%)
  blocking collectives  36.8 us (8%)
  between operations  14.9 us (3%)
  matrix products  12.6 us (3%)
  other arithmetic  10.1 us (2%)
  local copies, waits for them, and re-layouts  9.2 us (2%)
    unnamed x9, waiting for transfers between devices  174 us
    all_gather x3, waiting for transfers between devices, project_rows(): lax.all_gather(row_block, 'feat', axis=0, tiled=True)  174 us
    all_gather x1, waiting for transfers between devices, lower_weight(): return lax.all_gather(fetched[1], 'tok', axis=1, tiled=True)  53.8 us
    all_to_all x1, blocking collectives, route_rows(): lax.all_to_all(packed, 'tok', split_axis=0, concat_axis=0, tiled=True)  36.8 us
  transfers between devices with their start and end apart: 7, of which 6 were waited for; matrix products, arithmetic and copies ran while one was open for 1% of the time, Pallas kernels for 0%

commit v1 on v0

--- a/solution.py
+++ b/solution.py
@@ -1,8 +1,95 @@
+import functools
 import jax
 import jax.numpy as jnp
 from jax import lax
+from jax.experimental import pallas as pl
+from jax.experimental.pallas import tpu as pltpu
 from jax.sharding import PartitionSpec as P
 
+
+def _greet(peers, tok_index):
+    barrier = pltpu.get_barrier_semaphore()
+    for peer in peers:
+        pl.semaphore_signal(barrier, inc=1, device_id=(tok_index, peer), device_id_type=MESH)
+    pl.semaphore_wait(barrier, len(peers))
+
+
+def _gather_kernel(n, row_ref, out_ref, send_sem, recv_sem):
+    me = lax.axis_index("feat")
+    tok_index = lax.axis_index("tok")
+    peers = [lax.rem(me + d, n) for d in range(1, n)]
+    _greet(peers, tok_index)
+    for peer in peers:
+        pltpu.make_async_remote_copy(
+            src_ref=row_ref, dst_ref=out_ref.at[me], send_sem=send_sem.at[peer],
+            recv_sem=recv_sem.at[me], device_id=(tok_index, peer), device_id_type=MESH,
+        ).start()
+    out_ref[me] = row_ref[...]
+    for peer in peers:
+        pltpu.make_async_remote_copy(
+            src_ref=row_ref, dst_ref=out_ref.at[peer], send_sem=send_sem.at[peer],
+            recv_sem=recv_sem.at[peer], device_id=(tok_index, peer), device_id_type=MESH,
+        ).wait_recv()
+    for peer in peers:
+        pltpu.make_async_remote_copy(
+            src_ref=row_ref, dst_ref=out_ref.at[me], send_sem=send_sem.at[peer],
+            recv_sem=recv_sem.at[me], device_id=(tok_index, peer), device_id_type=MESH,
+        ).wait_send()
+
+
+def gather_feat(row_block, n, collective_id):
+    rows, width = row_block.shape
+    return pl.pallas_call(
+        functools.partial(_gather_kernel, n),
+        out_shape=jax.ShapeDtypeStruct((n, rows, width), row_block.dtype),
+        in_specs=[pl.BlockSpec(memory_space=pltpu.VMEM)],
+        out_specs=pl.BlockSpec(memory_space=pltpu.VMEM),
+        scratch_shapes=[pltpu.SemaphoreType.DMA((n,)), pltpu.SemaphoreType.DMA((n,))],
+        compiler_params=pltpu.CompilerParams(collective_id=collective_id, has_side_effects=True),
+    )(row_block).reshape(n * rows, width)
+
+
+def _scatter_kernel(n, part_ref, out_ref, held, send_sem, recv_sem):
+    me = lax.axis_index("feat")
+    tok_index = lax.axis_index("tok")
+    peers = [lax.rem(me + d, n) for d in range(1, n)]
+    _greet(peers, tok_index)
+    for peer in peers:
+        pltpu.make_async_remote_copy(
+            src_ref=part_ref.at[peer], dst_ref=held.at[me], send_sem=send_sem.at[peer],
+            recv_sem=recv_sem.at[me], device_id=(tok_index, peer), device_id_type=MESH,
+        ).start()
+    total = part_ref[me].astype(jnp.float32)
+    for peer in peers:
+        pltpu.make_async_remote_copy(
+            src_ref=part_ref.at[peer], dst_ref=held.at[peer], send_sem=send_sem.at[peer],
+            recv_sem=recv_sem.at[peer], device_id=(tok_index, peer), device_id_type=MESH,
+        ).wait_recv()
+        total = total + held[peer].astype(jnp.float32)
+    out_ref[...] = total
+    for peer in peers:
+        pltpu.make_async_remote_copy(
+            src_ref=part_ref.at[peer], dst_ref=held.at[me], send_sem=send_sem.at[peer],
+            recv_sem=recv_sem.at[me], device_id=(tok_index, peer), device_id_type=MESH,
+        ).wait_send()
+
+
+def scatter_feat(parts, n, collective_id):
+    _, rows, width = parts.shape
+    return pl.pallas_call(
+        functools.partial(_scatter_kernel, n),
+        out_shape=jax.ShapeDtypeStruct((rows, width), jnp.float32),
+        in_specs=[pl.BlockSpec(memory_space=pltpu.VMEM)],
+        out_specs=pl.BlockSpec(memory_space=pltpu.VMEM),
+        scratch_shapes=[
+            pltpu.VMEM((n, rows, width), parts.dtype),
+            pltpu.SemaphoreType.DMA((n,)),
+            pltpu.SemaphoreType.DMA((n,)),
+        ],
+        compiler_params=pltpu.CompilerParams(collective_id=collective_id, has_side_effects=True),
+    )(parts)
+
+MESH = pl.DeviceIdType.MESH
 LEAST_UNITS = 4
 MOST_UNITS = 16
 HEAD_DIM = 88
@@ -19,21 +106,19 @@
     return scaled.astype(jnp.bfloat16)
 
 
-def project_rows(row_block, weight_block):
+def project_rows(row_block, weight_block, collective_id):
+    n = lax.axis_size("feat")
     return jnp.dot(
-        lax.all_gather(row_block, "feat", axis=0, tiled=True),
+        gather_feat(row_block, n, collective_id),
         weight_block,
         preferred_element_type=jnp.float32,
     )
 
 
-def scatter_rows(left_rows, right_rows):
-    return lax.psum_scatter(
-        jnp.dot(left_rows, right_rows, preferred_element_type=jnp.float32).astype(jnp.bfloat16),
-        "feat",
-        scatter_dimension=0,
-        tiled=True,
-    ).astype(jnp.float32)
+def scatter_rows(left_rows, right_rows, collective_id):
+    n = lax.axis_size("feat")
+    parts = jnp.dot(left_rows, right_rows, preferred_element_type=jnp.float32).astype(jnp.bfloat16)
+    return scatter_feat(parts.reshape(n, parts.shape[0] // n, parts.shape[1]), n, collective_id)
 
 
 def early_weights(weight_up, weight_down):
@@ -108,19 +193,19 @@
     flat_in = project_in.reshape(model_width, 3 * project_in.shape[2])
     local_count = tokens.shape[0]
     normed = layer_norm(tokens, gain_attend)
-    projected = project_rows(normed, flat_in)
+    projected = project_rows(normed, flat_in, 0)
     attended = attend(projected, segment_ids, head_count)
-    second = (tokens.astype(jnp.float32) + scatter_rows(attended, project_out)).astype(jnp.bfloat16)
+    second = (tokens.astype(jnp.float32) + scatter_rows(attended, project_out, 1)).astype(jnp.bfloat16)
     normed_hidden = layer_norm(second, gain_hidden)
     hidden = jax.nn.gelu(
-        project_rows(normed_hidden, upper_weight(fetched)), approximate=False
+        project_rows(normed_hidden, upper_weight(fetched), 2), approximate=False
     ).astype(jnp.bfloat16)
     residual_out = (
-        second.astype(jnp.float32) + scatter_rows(hidden, lower_weight(fetched))
+        second.astype(jnp.float32) + scatter_rows(hidden, lower_weight(fetched), 3)
     ).astype(jnp.bfloat16)
     normed_final = layer_norm(residual_out, gain_final)
     merged = normed_final.reshape(local_count // 4, 4 * model_width)
-    embedded = project_rows(merged, weight_merge).astype(jnp.bfloat16)
+    embedded = project_rows(merged, weight_merge, 4).astype(jnp.bfloat16)
     return route_rows(embedded, segment_ids, owners)
 
 

time: 486 us -> 258 us (0.53)
  waiting for transfers between devices: 402 us -> 72 us
  Pallas kernels: 0 us -> 111 us
  blocking collectives: 36.8 us -> 30.9 us
    all_gather x3 -> x0, waiting for transfers between devices: 174 us -> none  [project_rows(): lax.all_gather(row_block, 'feat', axis=0, tiled=True)]
    unnamed x9 -> x2, waiting for transfers between devices: 174 us -> 1.41 us
    pallas_call x0 -> x5, Pallas kernels: none -> 111 us  [the longest x3 66.2 us: gather_feat(): pl.pallas_call(functools.partial(_gather_kernel, n), out_shape=jax.ShapeD...]
    all_gather x1, waiting for transfers between devices: 53.8 us -> 68 us  [lower_weight(): return lax.all_gather(fetched[1], 'tok', axis=1, tiled=True)]
    all_to_all x1, blocking collectives: 36.8 us -> 30.9 us  [route_rows(): lax.all_to_all(packed, 'tok', split_axis=0, concat_axis=0, tiled=True)]
  transfers between devices with their start and end apart: 7 -> 2, of which waited for: 6 -> 2; matrix products, arithmetic and copies ran while one was open for 1% -> 6% of each run, Pallas kernels for 0% -> 25%
where the time goes in v1:
time: 258 us; the launch traced here: 257 us
  Pallas kernels  111 us (43%)
  waiting for transfers between devices  72 us (28%)
  blocking collectives  30.9 us (12%)
  between operations  13.6 us (5%)
  matrix products  12.6 us (5%)
  local copies, waits for them, and re-layouts  8.43 us (3%)
  other arithmetic  8.25 us (3%)
    all_gather x1, waiting for transfers between devices, lower_weight(): return lax.all_gather(fetched[1], 'tok', axis=1, tiled=True)  68 us
    pallas_call x3, Pallas kernels, gather_feat(): pl.pallas_call(functools.partial(_gather_kernel, n), out_shape=jax.ShapeD...  66.2 us
    pallas_call x2, Pallas kernels, scatter_feat(): pl.pallas_call(functools.partial(_scatter_kernel, n), out_shape=jax.Shape...  44.9 us
    all_to_all x1, blocking collectives, route_rows(): lax.all_to_all(packed, 'tok', split_axis=0, concat_axis=0, tiled=True)  30.9 us
    dot_general x2, matrix products, scatter_rows(): jnp.dot(left_rows, right_rows, preferred_element_type=jnp.float32)  8.15 us
    unnamed x17, local copies, waits for them, and re-layouts  5.31 us
  transfers between devices with their start and end apart: 2, of which 2 were waited for; matrix products, arithmetic and copies ran while one was open for 6% of the time, Pallas kernels for 25%

profile of v1, /device:TPU:1, one launch (start us, length us, event | category | flops | bytes accessed | tf_op | source)
XLA Modules:
  0.0 257.0 jit_solution(13933670506810984862)
XLA Ops:
  6.5 0.7 all-gather.5.cloned.1.call-update
  8.0 1.0 convert_reduce_fusion.1
  9.0 1.1 fusion.57
  10.1 0.7 convert_element_type.92
  10.8 1.6 fusion.59.row_ref
  12.4 22.2 %shard_map.109 = bf16[16,24,1408]{2,1,0:T(8,128)(2,1)} custom-call(bf16[24,1408]{1,0:T(8,128)(2,1)} %fusion.59.row_ref), custom_call_target="tpu_custom_call" | custom-call | tf_op jit(solution)/shard_map/pallas_call | solution.py:42
  34.6 2.1 fusion.104
  37.5 2.6 %convolution_convert_fusion.1 = bf16[384,1408]{1,0:T(8,128)(2,1)} fusion(bf16[88,1408]{1,0:T(8,128)(2,1)} %param.15, f32[384,384]{0,1:T(8,128)S(1)} %get-tuple-element.14, f32[384]{0:T(512)S(1)} %fusion.12, f32[384]{0:T(512)S(1)} %get-tuple-element.13, bf16[384,3,1,88]{0,3,1,2:T(8,128)(2,1)} %copy-done.2), kind=kOutput, calls=%fused_computation.1 | convolution fusion | flops 122127360 | bytes 1989632 | tf_op jit(solution)/shard_map/dot_general | solution.py:120
  40.1 22.2 %shard_map.110 = f32[24,1408]{1,0:T(8,128)} custom-call(bf16[16,24,1408]{2,1,0:T(8,128)(2,1)} %bitcast.52), custom_call_target="tpu_custom_call" | custom-call | tf_op jit(solution)/shard_map/pallas_call | solution.py:79
  62.3 1.0 convert_reduce_fusion
  63.6 0.7 fusion.56.row_ref
  64.3 18.9 %shard_map.111 = bf16[16,24,1408]{2,1,0:T(8,128)(2,1)} custom-call(bf16[24,1408]{1,0:T(8,128)(2,1)} %fusion.56.row_ref), custom_call_target="tpu_custom_call" | custom-call | tf_op jit(solution)/shard_map/pallas_call | solution.py:42
  83.6 2.6 %all-gather.5.cloned.1.call-done = bf16[32,44,384]{2,1,0:T(8,128)(2,1)} async-done(((bf16[1,44,384]{2,1,0:T(8,128)(2,1)}), bf16[32,44,384]{2,1,0:T(8,128)(2,1)}) %all-gather.5.cloned.1.call-update) | async-done | bytes 1081360 | tf_op jit(solution)/shard_map/all_gather | solution.py:129
  86.3 2.2 reshape.141
  88.4 68.0 %all-gather.7.cloned.1.call-done = bf16[32,44,384]{2,1,0:T(8,128)(2,1)} async-done(((bf16[1,44,384]{2,1,0:T(8,128)(2,1)}), bf16[32,44,384]{2,1,0:T(8,128)(2,1)}) %all-gather.7.cloned.1.call-update) | async-done | bytes 1081360 | tf_op jit(solution)/shard_map/all_gather | solution.py:133
  156.5 2.2 reshape.143
  158.6 5.5 %convolution_convert_fusion = bf16[384,1408]{1,0:T(8,128)(2,1)} fusion(bf16[1408,384]{1,0:T(8,128)(2,1)} %reshape.143, bf16[384,1408]{1,0:T(8,128)(2,1)} %bitcast.54, bf16[1408,384]{1,0:T(8,128)(2,1)} %reshape.141), kind=kOutput, calls=%fused_computation | convolution fusion | flops 840597504 | bytes 4325376 | tf_op jit(solution)/shard_map/dot_general | solution.py:120
  164.2 22.7 %shard_map.112 = f32[24,1408]{1,0:T(8,128)} custom-call(bf16[16,24,1408]{2,1,0:T(8,128)(2,1)} %bitcast.53), custom_call_target="tpu_custom_call" | custom-call | tf_op jit(solution)/shard_map/pallas_call | solution.py:79
  186.9 1.0 convert_reduce_fusion.2
  188.9 25.1 %shard_map.113 = bf16[16,6,5632]{2,1,0:T(8,128)(2,1)} custom-call(bf16[6,5632]{1,0:T(8,128)(2,1)} %reshape.136.row_ref), custom_call_target="tpu_custom_call" | custom-call | tf_op jit(solution)/shard_map/pallas_call | solution.py:42
  214.1 2.3 reshape.137
  216.4 2.1 convolution_convert_fusion.2
  218.6 30.9 %all_to_all.5 = bf16[32,16,256]{2,1,0:T(8,128)(2,1)S(1)} all-to-all(bf16[32,16,256]{2,1,0:T(8,128)(2,1)S(1)} %bitcast.56), channel_id=1, replica_groups=mesh['tok'=32,'feat'=16] {'tok'}, dimensions={0} | all-to-all | bytes 524288 | tf_op jit(solution)/shard_map/all_to_all | solution.py:173
  249.4 0.7 copy.13
  (36 shorter events, 3.1 us)
Async XLA Ops:
  6.5 209.9 %copy-start = (bf16[5632,256]{1,0:T(8,128)(2,1)S(1)}, bf16[5632,256]{1,0:T(8,128)(2,1)}, u32[]{:S(2)}) copy-start(bf16[5632,256]{1,0:T(8,128)(2,1)} %param.18) | copy-start | bytes 8650756
  6.5 79.7 %all-gather.5.cloned.1.call-start = ((), (), s32[]{:S(2)}) async-start(), calls=%async_computation.1 | async-start | bytes 1216512 | tf_op jit(solution)/shard_map/all_gather | solution.py:129
  7.3 149.2 %all-gather.7.cloned.1.call-start = ((), (), s32[]{:S(2)}) async-start(), calls=%async_computation.2 | async-start | bytes 1216512 | tf_op jit(solution)/shard_map/all_gather | solution.py:133
  34.6 2.1 copy-start.3
  36.6 0.7 copy-start.2
  36.6 0.8 copy-start.4
  36.7 0.8 copy-start.5
  40.1 22.2 %copy-start.1 = (bf16[24,1408]{1,0:T(8,128)(2,1)S(1)}, bf16[24,1408]{1,0:T(8,128)(2,1)}, u32[]{:S(2)}) copy-start(bf16[24,1408]{1,0:T(8,128)(2,1)} %param.11) | copy-start | bytes 202756
  62.3 21.2 %copy-start.6 = (s32[32]{0:T(128)S(1)}, s32[32]{0:T(128)}, u32[]{:S(2)}) copy-start(s32[32]{0:T(128)} %param.13) | copy-start | bytes 388
Sparse Core Ops, SparseCore 0:
  9.5 76.7 all-gather.4
  88.4 68.0 all-gather.6

commit v2 on v1

--- a/solution.py
+++ b/solution.py
@@ -47,6 +47,134 @@
         scratch_shapes=[pltpu.SemaphoreType.DMA((n,)), pltpu.SemaphoreType.DMA((n,))],
         compiler_params=pltpu.CompilerParams(collective_id=collective_id, has_side_effects=True),
     )(row_block).reshape(n * rows, width)
+
+
+def _ring_gather(x_ref, out_ref, send_right, send_left, send_partner, recv_sem, feat_index):
+    tok_count = out_ref.shape[0]
+    chips = tok_count // 2
+    right_steps = chips // 2
+    left_steps = chips - 1 - right_steps
+    me = lax.axis_index("tok")
+    chip = me // 2
+    core = me % 2
+    right = lax.rem(chip + 1, chips) * 2 + core
+    left = lax.rem(chip + chips - 1, chips) * 2 + core
+    partner = chip * 2 + (1 - core)
+
+    def slot_of(offset):
+        return lax.rem(chip + offset + 2 * chips, chips) * 2 + core
+
+    def remote(src, slot, sem, target):
+        return pltpu.make_async_remote_copy(
+            src_ref=src, dst_ref=out_ref.at[slot], send_sem=sem, recv_sem=recv_sem.at[slot],
+            device_id=(target, feat_index), device_id_type=MESH,
+        )
+
+    sends = []
+
+    def forward_partner(src, slot):
+        copy = remote(src, slot, send_partner.at[len(sends_partner)], partner)
+        copy.start()
+        sends_partner.append(copy)
+
+    sends_partner = []
+    out_ref[me] = x_ref[...]
+    forward_partner(x_ref, me)
+    for step in range(1, right_steps + 1):
+        if step == 1:
+            src_right = x_ref
+            src_left = x_ref
+        else:
+            from_left = slot_of(-(step - 1))
+            remote(x_ref, from_left, send_right.at[0], right).wait_recv()
+            forward_partner(out_ref.at[from_left], from_left)
+            src_right = out_ref.at[from_left]
+            if step - 1 <= left_steps:
+                from_right = slot_of(step - 1)
+                remote(x_ref, from_right, send_left.at[0], left).wait_recv()
+                forward_partner(out_ref.at[from_right], from_right)
+                src_left = out_ref.at[from_right]
+        copy = remote(src_right, slot_of(-(step - 1)), send_right.at[step - 1], right)
+        copy.start()
+        sends.append(copy)
+        if step <= left_steps:
+            copy = remote(src_left, slot_of(step - 1), send_left.at[step - 1], left)
+            copy.start()
+            sends.append(copy)
+    last_left = slot_of(-right_steps)
+    remote(x_ref, last_left, send_right.at[0], right).wait_recv()
+    forward_partner(out_ref.at[last_left], last_left)
+    if left_steps >= 1 and left_steps + 1 > right_steps:
+        last_right = slot_of(left_steps)
+        remote(x_ref, last_right, send_left.at[0], left).wait_recv()
+        forward_partner(out_ref.at[last_right], last_right)
+    for other_chip in range(chips):
+        remote(x_ref, other_chip * 2 + (1 - core), send_partner.at[0], partner).wait_recv()
+    for copy in sends + sends_partner:
+        copy.wait_send()
+
+
+def _first_kernel(n, row_ref, weight_ref, out_ref, weight_out, send_sem, recv_sem,
+                  send_right, send_left, send_partner, weight_recv):
+    me = lax.axis_index("feat")
+    tok_index = lax.axis_index("tok")
+    chips = weight_out.shape[0] // 2
+    chip = tok_index // 2
+    core = tok_index % 2
+    peers = [lax.rem(me + d, n) for d in range(1, n)]
+    barrier = pltpu.get_barrier_semaphore()
+    for peer in peers:
+        pl.semaphore_signal(barrier, inc=1, device_id=(tok_index, peer), device_id_type=MESH)
+    ring_peers = [
+        lax.rem(chip + 1, chips) * 2 + core,
+        lax.rem(chip + chips - 1, chips) * 2 + core,
+        chip * 2 + (1 - core),
+    ]
+    for peer in ring_peers:
+        pl.semaphore_signal(barrier, inc=1, device_id=(peer, me), device_id_type=MESH)
+    pl.semaphore_wait(barrier, len(peers) + len(ring_peers))
+    for peer in peers:
+        pltpu.make_async_remote_copy(
+            src_ref=row_ref, dst_ref=out_ref.at[me], send_sem=send_sem.at[peer],
+            recv_sem=recv_sem.at[me], device_id=(tok_index, peer), device_id_type=MESH,
+        ).start()
+    out_ref[me] = row_ref[...]
+    _ring_gather(weight_ref, weight_out, send_right, send_left, send_partner, weight_recv, me)
+    for peer in peers:
+        pltpu.make_async_remote_copy(
+            src_ref=row_ref, dst_ref=out_ref.at[peer], send_sem=send_sem.at[peer],
+            recv_sem=recv_sem.at[peer], device_id=(tok_index, peer), device_id_type=MESH,
+        ).wait_recv()
+    for peer in peers:
+        pltpu.make_async_remote_copy(
+            src_ref=row_ref, dst_ref=out_ref.at[me], send_sem=send_sem.at[peer],
+            recv_sem=recv_sem.at[me], device_id=(tok_index, peer), device_id_type=MESH,
+        ).wait_send()
+
+
+def first_exchange(row_block, weight_block, n, tok_count, collective_id):
+    rows, width = row_block.shape
+    weight_rows, weight_width = weight_block.shape
+    chips = tok_count // 2
+    gathered, weights = pl.pallas_call(
+        functools.partial(_first_kernel, n),
+        out_shape=(
+            jax.ShapeDtypeStruct((n, rows, width), row_block.dtype),
+            jax.ShapeDtypeStruct((tok_count, weight_rows, weight_width), weight_block.dtype),
+        ),
+        in_specs=[pl.BlockSpec(memory_space=pltpu.VMEM)] * 2,
+        out_specs=(pl.BlockSpec(memory_space=pltpu.VMEM),) * 2,
+        scratch_shapes=[
+            pltpu.SemaphoreType.DMA((n,)),
+            pltpu.SemaphoreType.DMA((n,)),
+            pltpu.SemaphoreType.DMA((chips,)),
+            pltpu.SemaphoreType.DMA((chips,)),
+            pltpu.SemaphoreType.DMA((chips,)),
+            pltpu.SemaphoreType.DMA((tok_count,)),
+        ],
+        compiler_params=pltpu.CompilerParams(collective_id=collective_id, has_side_effects=True),
+    )(row_block, weight_block)
+    return gathered.reshape(n * rows, width), weights
 
 
 def _scatter_kernel(n, part_ref, out_ref, held, send_sem, recv_sem):
@@ -189,20 +317,32 @@
 ):
     model_width = tokens.shape[1]
     head_count = project_in.shape[2] // HEAD_DIM
-    fetched = early_weights(weight_up, weight_down)
+    units = weight_up.shape[1]
+    feat_count = lax.axis_size("feat")
+    tok_count = lax.axis_size("tok")
     flat_in = project_in.reshape(model_width, 3 * project_in.shape[2])
     local_count = tokens.shape[0]
     normed = layer_norm(tokens, gain_attend)
-    projected = project_rows(normed, flat_in, 0)
+    stacked = jnp.concatenate([weight_up, weight_down.T], axis=1)
+    gathered, weights = first_exchange(normed, stacked, feat_count, tok_count, 0)
+    upper = weights[:, :, :units].reshape(tok_count * weight_up.shape[0], units)
+    lower_t = weights[:, :, units:].reshape(tok_count * weight_up.shape[0], units)
+    projected = jnp.dot(gathered, flat_in, preferred_element_type=jnp.float32)
     attended = attend(projected, segment_ids, head_count)
     second = (tokens.astype(jnp.float32) + scatter_rows(attended, project_out, 1)).astype(jnp.bfloat16)
     normed_hidden = layer_norm(second, gain_hidden)
     hidden = jax.nn.gelu(
-        project_rows(normed_hidden, upper_weight(fetched), 2), approximate=False
+        project_rows(normed_hidden, upper, 2), approximate=False
     ).astype(jnp.bfloat16)
-    residual_out = (
-        second.astype(jnp.float32) + scatter_rows(hidden, lower_weight(fetched), 3)
+    down_parts = lax.dot_general(
+        hidden, lower_t, (((1,), (1,)), ((), ())), preferred_element_type=jnp.float32
     ).astype(jnp.bfloat16)
+    mlp_sum = scatter_feat(
+        down_parts.reshape(feat_count, down_parts.shape[0] // feat_count, down_parts.shape[1]),
+        feat_count,
+        3,
+    )
+    residual_out = (second.astype(jnp.float32) + mlp_sum).astype(jnp.bfloat16)
     normed_final = layer_norm(residual_out, gain_final)
     merged = normed_final.reshape(local_count // 4, 4 * model_width)
     embedded = project_rows(merged, weight_merge, 4).astype(jnp.bfloat16)

time: 258 us -> 207 us (0.80)
  waiting for transfers between devices: 72 us -> 0 us
  Pallas kernels: 111 us -> 138 us
  between operations: 13.6 us -> 0.17 us
  local copies, waits for them, and re-layouts: 8.43 us -> 11.8 us
    all_gather x2 -> x0, waiting for transfers between devices: 70.6 us -> none  [the longest x1 68 us: lower_weight(): return lax.all_gather(fetched[1], 'tok', axis=1, tiled=True)]
    pallas_call x0 -> x1, Pallas kernels: none -> 52 us  [first_exchange(): pl.pallas_call(functools.partial(_first_kernel, n), out_shape=(jax.ShapeD...]
    pallas_call x3 -> x2, Pallas kernels: 66.2 us -> 44.6 us  [gather_feat(): pl.pallas_call(functools.partial(_gather_kernel, n), out_shape=jax.ShapeD...]
    dot_general x1 -> x2, matrix products: 2.05 us -> 7.57 us  [the longest x1 5.52 us: body(): lax.dot_general(hidden, lower_t, (((1,), (1,)), ((), ())), preferred_elem...]
    dot_general x2 -> x1, matrix products: 8.15 us -> 2.7 us  [scatter_rows(): jnp.dot(left_rows, right_rows, preferred_element_type=jnp.float32)]
    reshape x0 -> x2, local copies, waits for them, and re-layouts: none -> 4.31 us  [the longest x1 2.17 us: body(): weights[:, :, units:].reshape(tok_count * weight_up.shape[0], units)]
    unnamed x17 -> x15, local copies, waits for them, and re-layouts: 5.31 us -> 1.1 us
    slice x0 -> x1, local copies, waits for them, and re-layouts: none -> 3.25 us  [body(): upper = weights[:, :, :units].reshape(tok_count * weight_up.shape[0], units)]
  transfers between devices with their start and end apart: 2 -> 0, of which waited for: 2 -> 0; matrix products, arithmetic and copies ran while one was open for 6% -> 0% of each run, Pallas kernels for 25% -> 0%
where the time goes in v2:
time: 207 us; the launch traced here: 206 us
  Pallas kernels  138 us (67%)
  blocking collectives  32.9 us (16%)
  matrix products  12.7 us (6%)
  local copies, waits for them, and re-layouts  11.8 us (6%)
  other arithmetic  9.81 us (5%)
    pallas_call x1, Pallas kernels, first_exchange(): pl.pallas_call(functools.partial(_first_kernel, n), out_shape=(jax.ShapeD...  52 us
    pallas_call x2, Pallas kernels, gather_feat(): pl.pallas_call(functools.partial(_gather_kernel, n), out_shape=jax.ShapeD...  44.6 us
    pallas_call x2, Pallas kernels, scatter_feat(): pl.pallas_call(functools.partial(_scatter_kernel, n), out_shape=jax.Shape...  41.8 us
    all_to_all x1, blocking collectives, route_rows(): lax.all_to_all(packed, 'tok', split_axis=0, concat_axis=0, tiled=True)  32.9 us
    dot_general x1, matrix products, body(): lax.dot_general(hidden, lower_t, (((1,), (1,)), ((), ())), preferred_elem...  5.52 us

profile of v2, /device:TPU:1, one launch (start us, length us, event | category | flops | bytes accessed | tf_op | source)
XLA Modules:
  0.0 205.8 jit_solution(183947280267784111)
XLA Ops:
  0.0 0.8 convert_element_type.92
  0.8 1.0 convert_reduce_fusion.1
  1.9 1.1 fusion.57
  3.0 1.6 fusion.59.row_ref
  4.6 1.4 pad_maximum_fusion.weight_ref
  6.0 52.0 %shard_map.109 = (bf16[16,24,1408]{2,1,0:T(8,128)(2,1)}, bf16[32,44,768]{2,1,0:T(8,128)(2,1)}) custom-call(bf16[24,1408]{1,0:T(8,128)(2,1)} %fusion.59.row_ref, bf16[44,768]{1,0:T(8,128)(2,1)} %pad_maximum_fusion.weight_ref), custom_call_target="tpu_custom_call" | custom-call | tf_op jit(solution)/shard_map/pallas_call | solution.py:159
  58.0 3.3 %fusion.104 = (bf16[32,44,384]{2,1,0:T(8,128)(2,1)}, bf16[32,44,384]{2,1,0:T(8,128)(2,1)}) fusion(bf16[32,44,768]{2,1,0:T(8,128)(2,1)} %get-tuple-element.8), kind=kLoop, calls=%fused_computation.142 | loop fusion | bytes 4325376 | tf_op jit(solution)/shard_map/slice | solution.py:328
  61.3 2.2 %reshape.142 = bf16[1408,384]{1,0:T(8,128)(2,1)} reshape(bf16[32,44,384]{2,1,0:T(8,128)(2,1)} %get-tuple-element.16) | data formatting | bytes 2162688 | tf_op jit(solution)/shard_map/reshape | solution.py:329
  63.5 2.0 fusion.105
  66.4 2.7 %convolution_convert_fusion.1 = bf16[384,1408]{1,0:T(8,128)(2,1)} fusion(bf16[88,1408]{1,0:T(8,128)(2,1)} %param.15, f32[384,384]{0,1:T(8,128)S(1)} %get-tuple-element.20, f32[384]{0:T(512)S(1)} %fusion.12, f32[384]{0:T(512)S(1)} %get-tuple-element.19, bf16[384,3,1,88]{0,3,1,2:T(8,128)(2,1)} %copy-done.2), kind=kOutput, calls=%fused_computation.1 | convolution fusion | flops 122127360 | bytes 1989632 | tf_op jit(solution)/shard_map/dot_general | solution.py:248
  69.1 21.3 %shard_map.110 = f32[24,1408]{1,0:T(8,128)} custom-call(bf16[16,24,1408]{2,1,0:T(8,128)(2,1)} %bitcast.49), custom_call_target="tpu_custom_call" | custom-call | tf_op jit(solution)/shard_map/pallas_call | solution.py:207
  90.4 1.0 convert_reduce_fusion
  91.7 0.7 fusion.56.row_ref
  92.4 20.6 %shard_map.111 = bf16[16,24,1408]{2,1,0:T(8,128)(2,1)} custom-call(bf16[24,1408]{1,0:T(8,128)(2,1)} %fusion.56.row_ref), custom_call_target="tpu_custom_call" | custom-call | tf_op jit(solution)/shard_map/pallas_call | solution.py:42
  113.1 2.1 %reshape.141 = bf16[1408,384]{1,0:T(8,128)(2,1)} reshape(bf16[32,44,384]{2,1,0:T(8,128)(2,1)} %get-tuple-element.15) | data formatting | bytes 2162688 | tf_op jit(solution)/shard_map/reshape | solution.py:328
  115.2 5.5 %convolution_convert_fusion = bf16[384,1408]{1,0:T(8,128)(2,1)} fusion(bf16[1408,384]{1,0:T(8,128)(2,1)} %reshape.142, bf16[384,1408]{1,0:T(8,128)(2,1)} %bitcast.51, bf16[1408,384]{1,0:T(8,128)(2,1)} %reshape.141), kind=kOutput, calls=%fused_computation | convolution fusion | flops 840597504 | bytes 4325376 | tf_op jit(solution)/shard_map/dot_general | solution.py:337
  120.7 20.5 %shard_map.112 = f32[24,1408]{1,0:T(8,128)} custom-call(bf16[16,24,1408]{2,1,0:T(8,128)(2,1)} %bitcast.50), custom_call_target="tpu_custom_call" | custom-call | tf_op jit(solution)/shard_map/pallas_call | solution.py:207
  141.3 1.0 convert_reduce_fusion.2
  142.6 0.7 reshape.144.row_ref
  143.3 24.0 %shard_map.113 = bf16[16,6,5632]{2,1,0:T(8,128)(2,1)} custom-call(bf16[6,5632]{1,0:T(8,128)(2,1)} %reshape.144.row_ref), custom_call_target="tpu_custom_call" | custom-call | tf_op jit(solution)/shard_map/pallas_call | solution.py:42
  167.3 2.3 %reshape.145 = bf16[96,5632]{1,0:T(8,128)(2,1)} reshape(bf16[16,6,5632]{2,1,0:T(8,128)(2,1)} %shard_map.113) | data formatting | bytes 2162688 | tf_op jit(solution)/shard_map/reshape | solution.py:49
  170.1 2.1 %convolution_convert_fusion.2 = bf16[512,256]{1,0:T(8,128)(2,1)S(1)} fusion(bf16[96,5632]{1,0:T(8,128)(2,1)} %reshape.145, bf16[5632,256]{1,0:T(8,128)(2,1)S(1)} %copy-done, s32[96]{0:T(128)S(1)} %multiply_add_fusion), kind=kOutput, calls=%fused_computation.4 | convolution fusion | flops 302194688 | bytes 4227456 | tf_op jit(solution)/shard_map/dot_general | solution.py:299
  172.2 32.9 %all_to_all.5 = bf16[32,16,256]{2,1,0:T(8,128)(2,1)S(1)} all-to-all(bf16[32,16,256]{2,1,0:T(8,128)(2,1)S(1)} %bitcast.52), channel_id=1, replica_groups=mesh['tok'=32,'feat'=16] {'tok'}, dimensions={0} | all-to-all | bytes 524288 | tf_op jit(solution)/shard_map/all_to_all | solution.py:301
  205.1 0.7 copy.13
  (32 shorter events, 1.8 us)
Async XLA Ops:
  0.0 170.0 %copy-start = (bf16[5632,256]{1,0:T(8,128)(2,1)S(1)}, bf16[5632,256]{1,0:T(8,128)(2,1)}, u32[]{:S(2)}) copy-start(bf16[5632,256]{1,0:T(8,128)(2,1)} %param.18) | copy-start | bytes 8650756
  61.3 2.2 %copy-start.3 = (s32[384]{0:T(512)S(1)}, s32[384]{0:T(512)}, u32[]{:S(2)}) copy-start(s32[384]{0:T(512)} %param.12) | copy-start | bytes 4612
  65.6 0.7 copy-start.2
  69.1 21.3 %copy-start.1 = (bf16[24,1408]{1,0:T(8,128)(2,1)S(1)}, bf16[24,1408]{1,0:T(8,128)(2,1)}, u32[]{:S(2)}) copy-start(bf16[24,1408]{1,0:T(8,128)(2,1)} %param.11) | copy-start | bytes 202756
  69.1 22.4 %copy-start.4 = (bf16[1408]{0:T(1024)(128)(2,1)S(1)}, bf16[1408]{0:T(1024)(128)(2,1)}, u32[]{:S(2)}) copy-start(bf16[1408]{0:T(1024)(128)(2,1)} %param.20) | copy-start | bytes 8452
  120.7 21.6 %copy-start.5 = (bf16[1408]{0:T(1024)(128)(2,1)S(1)}, bf16[1408]{0:T(1024)(128)(2,1)}, u32[]{:S(2)}) copy-start(bf16[1408]{0:T(1024)(128)(2,1)} %param.21) | copy-start | bytes 8452
  167.3 2.6 %copy-start.6 = (s32[32]{0:T(128)S(1)}, s32[32]{0:T(128)}, u32[]{:S(2)}) copy-start(s32[32]{0:T(128)} %param.13) | copy-start | bytes 388

commit v3 on v2

--- a/solution.py
+++ b/solution.py
@@ -323,10 +323,9 @@
     flat_in = project_in.reshape(model_width, 3 * project_in.shape[2])
     local_count = tokens.shape[0]
     normed = layer_norm(tokens, gain_attend)
-    stacked = jnp.concatenate([weight_up, weight_down.T], axis=1)
-    gathered, weights = first_exchange(normed, stacked, feat_count, tok_count, 0)
-    upper = weights[:, :, :units].reshape(tok_count * weight_up.shape[0], units)
-    lower_t = weights[:, :, units:].reshape(tok_count * weight_up.shape[0], units)
+    lower = lax.all_gather(weight_down, "tok", axis=1, tiled=True)
+    gathered, weights = first_exchange(normed, weight_up, feat_count, tok_count, 0)
+    upper = weights.reshape(tok_count * weight_up.shape[0], units)
     projected = jnp.dot(gathered, flat_in, preferred_element_type=jnp.float32)
     attended = attend(projected, segment_ids, head_count)
     second = (tokens.astype(jnp.float32) + scatter_rows(attended, project_out, 1)).astype(jnp.bfloat16)
@@ -334,9 +333,7 @@
     hidden = jax.nn.gelu(
         project_rows(normed_hidden, upper, 2), approximate=False
     ).astype(jnp.bfloat16)
-    down_parts = lax.dot_general(
-        hidden, lower_t, (((1,), (1,)), ((), ())), preferred_element_type=jnp.float32
-    ).astype(jnp.bfloat16)
+    down_parts = jnp.dot(hidden, lower, preferred_element_type=jnp.float32).astype(jnp.bfloat16)
     mlp_sum = scatter_feat(
         down_parts.reshape(feat_count, down_parts.shape[0] // feat_count, down_parts.shape[1]),
         feat_count,

time: 207 us -> 211 us (1.019)
  between operations: 0.17 us -> 13.6 us
  local copies, waits for them, and re-layouts: 11.8 us -> 8.59 us
  blocking collectives: 32.9 us -> 30.5 us
    pallas_call x1, Pallas kernels: 52 us -> 47.9 us  [first_exchange(): pl.pallas_call(functools.partial(_first_kernel, n), out_shape=(jax.ShapeD...]
    slice x1 -> x0, local copies, waits for them, and re-layouts: 3.25 us -> none  [body(): upper = weights[:, :, :units].reshape(tok_count * weight_up.shape[0], units)]
    all_to_all x1, blocking collectives: 32.9 us -> 30.5 us  [route_rows(): lax.all_to_all(packed, 'tok', split_axis=0, concat_axis=0, tiled=True)]
    unnamed x15 -> x16, local copies, waits for them, and re-layouts: 1.1 us -> 3.29 us
    reshape x2 -> x1, local copies, waits for them, and re-layouts: 4.31 us -> 2.18 us  [body(): upper = weights.reshape(tok_count * weight_up.shape[0], units)]
  transfers between devices with their start and end apart: 0 -> 1, of which waited for: 0 -> 0; matrix products, arithmetic and copies ran while one was open for 0% -> 7% of each run, Pallas kernels for 0% -> 43%
where the time goes in v3:
time: 211 us; the launch traced here: 210 us
  Pallas kernels  136 us (64%)
  blocking collectives  30.5 us (14%)
  between operations  13.6 us (6%)
  matrix products  12.7 us (6%)
  local copies, waits for them, and re-layouts  8.59 us (4%)
  other arithmetic  8.37 us (4%)
    pallas_call x1, Pallas kernels, first_exchange(): pl.pallas_call(functools.partial(_first_kernel, n), out_shape=(jax.ShapeD...  47.9 us
    pallas_call x2, Pallas kernels, gather_feat(): pl.pallas_call(functools.partial(_gather_kernel, n), out_shape=jax.ShapeD...  46.7 us
    pallas_call x2, Pallas kernels, scatter_feat(): pl.pallas_call(functools.partial(_scatter_kernel, n), out_shape=jax.Shape...  41.4 us
    all_to_all x1, blocking collectives, route_rows(): lax.all_to_all(packed, 'tok', split_axis=0, concat_axis=0, tiled=True)  30.5 us
    dot_general x1, matrix products, body(): jnp.dot(hidden, lower, preferred_element_type=jnp.float32)  5.51 us
  transfers between devices with their start and end apart: 1, of which 0 were waited for; matrix products, arithmetic and copies ran while one was open for 7% of the time, Pallas kernels for 43%

profile of v3, /device:TPU:1, one launch (start us, length us, event | category | flops | bytes accessed | tf_op | source)
XLA Modules:
  0.0 210.5 jit_solution(7491313649127880495)
XLA Ops:
  6.5 0.7 all-gather.3.cloned.1.call-update
  7.3 1.1 convert_reduce_fusion.1
  8.4 1.1 fusion.57
  9.5 0.7 convert_element_type.92
  10.2 1.6 fusion.59.row_ref
  11.8 47.9 %shard_map.109 = (bf16[16,24,1408]{2,1,0:T(8,128)(2,1)}, bf16[32,44,384]{2,1,0:T(8,128)(2,1)}) custom-call(bf16[24,1408]{1,0:T(8,128)(2,1)} %fusion.59.row_ref, bf16[44,384]{1,0:T(8,128)(2,1)} %weight_ref.1), custom_call_target="tpu_custom_call" | custom-call | tf_op jit(solution)/shard_map/pallas_call | solution.py:159
  59.8 2.1 fusion.104
  62.1 0.4 copy-done.2
  62.7 2.6 %convolution_convert_fusion.1 = bf16[384,1408]{1,0:T(8,128)(2,1)} fusion(bf16[88,1408]{1,0:T(8,128)(2,1)} %param.15, f32[384,384]{0,1:T(8,128)S(1)} %get-tuple-element.18, f32[384]{0:T(512)S(1)} %fusion.12, f32[384]{0:T(512)S(1)} %get-tuple-element.17, bf16[384,3,1,88]{0,3,1,2:T(8,128)(2,1)} %copy-done.2), kind=kOutput, calls=%fused_computation.1 | convolution fusion | flops 122127360 | bytes 1989632 | tf_op jit(solution)/shard_map/dot_general | solution.py:248
  65.4 21.8 %shard_map.110 = f32[24,1408]{1,0:T(8,128)} custom-call(bf16[16,24,1408]{2,1,0:T(8,128)(2,1)} %bitcast.51), custom_call_target="tpu_custom_call" | custom-call | tf_op jit(solution)/shard_map/pallas_call | solution.py:207
  87.2 1.0 convert_reduce_fusion
  88.5 0.7 fusion.56.row_ref
  89.2 20.5 %shard_map.111 = bf16[16,24,1408]{2,1,0:T(8,128)(2,1)} custom-call(bf16[24,1408]{1,0:T(8,128)(2,1)} %fusion.56.row_ref), custom_call_target="tpu_custom_call" | custom-call | tf_op jit(solution)/shard_map/pallas_call | solution.py:42
  109.7 2.2 %reshape.138 = bf16[1408,384]{1,0:T(8,128)(2,1)} reshape(bf16[32,44,384]{2,1,0:T(8,128)(2,1)} %get-tuple-element.8) | data formatting | bytes 2162688 | tf_op jit(solution)/shard_map/reshape | solution.py:328
  112.3 2.2 %reshape.145 = bf16[1408,384]{1,0:T(8,128)(2,1)} reshape(bf16[32,44,384]{2,1,0:T(8,128)(2,1)} %all-gather.3.cloned.1.call-done) | data formatting | bytes 2162688
  114.5 5.5 %convolution_convert_fusion = bf16[384,1408]{1,0:T(8,128)(2,1)} fusion(bf16[1408,384]{1,0:T(8,128)(2,1)} %reshape.145, bf16[384,1408]{1,0:T(8,128)(2,1)} %bitcast.53, bf16[1408,384]{1,0:T(8,128)(2,1)} %reshape.138), kind=kOutput, calls=%fused_computation | convolution fusion | flops 840597504 | bytes 4325376 | tf_op jit(solution)/shard_map/dot_general | solution.py:336
  120.0 19.6 %shard_map.112 = f32[24,1408]{1,0:T(8,128)} custom-call(bf16[16,24,1408]{2,1,0:T(8,128)(2,1)} %bitcast.52), custom_call_target="tpu_custom_call" | custom-call | tf_op jit(solution)/shard_map/pallas_call | solution.py:207
  139.6 1.0 convert_reduce_fusion.2
  141.0 0.7 reshape.140.row_ref
  141.7 26.2 %shard_map.113 = bf16[16,6,5632]{2,1,0:T(8,128)(2,1)} custom-call(bf16[6,5632]{1,0:T(8,128)(2,1)} %reshape.140.row_ref), custom_call_target="tpu_custom_call" | custom-call | tf_op jit(solution)/shard_map/pallas_call | solution.py:42
  167.9 2.3 %reshape.141 = bf16[96,5632]{1,0:T(8,128)(2,1)} reshape(bf16[16,6,5632]{2,1,0:T(8,128)(2,1)} %shard_map.113) | data formatting | bytes 2162688 | tf_op jit(solution)/shard_map/reshape | solution.py:49
  170.2 2.1 %convolution_convert_fusion.2 = bf16[512,256]{1,0:T(8,128)(2,1)S(1)} fusion(bf16[96,5632]{1,0:T(8,128)(2,1)} %reshape.141, bf16[5632,256]{1,0:T(8,128)(2,1)S(1)} %copy-done, s32[96]{0:T(128)S(1)} %multiply_add_fusion), kind=kOutput, calls=%fused_computation.4 | convolution fusion | flops 302194688 | bytes 4227456 | tf_op jit(solution)/shard_map/dot_general | solution.py:299
  172.4 30.5 %all_to_all.5 = bf16[32,16,256]{2,1,0:T(8,128)(2,1)S(1)} all-to-all(bf16[32,16,256]{2,1,0:T(8,128)(2,1)S(1)} %bitcast.54), channel_id=1, replica_groups=mesh['tok'=32,'feat'=16] {'tok'}, dimensions={0} | all-to-all | bytes 524288 | tf_op jit(solution)/shard_map/all_to_all | solution.py:301
  202.9 0.7 copy.13
  (33 shorter events, 1.5 us)
Async XLA Ops:
  6.5 163.7 %copy-start = (bf16[5632,256]{1,0:T(8,128)(2,1)S(1)}, bf16[5632,256]{1,0:T(8,128)(2,1)}, u32[]{:S(2)}) copy-start(bf16[5632,256]{1,0:T(8,128)(2,1)} %param.18) | copy-start | bytes 8650756
  6.5 105.8 %all-gather.3.cloned.1.call-start = ((), (), s32[]{:S(2)}) async-start(), calls=%async_computation.1 | async-start | bytes 1216512 | tf_op jit(solution)/shard_map/all_gather | solution.py:326
  59.7 2.1 copy-start.3
  61.8 0.7 copy-start.2
  65.4 21.8 %copy-start.4 = (bf16[1408]{0:T(1024)(128)(2,1)S(1)}, bf16[1408]{0:T(1024)(128)(2,1)}, u32[]{:S(2)}) copy-start(bf16[1408]{0:T(1024)(128)(2,1)} %param.20) | copy-start | bytes 8452
  65.4 21.8 %copy-start.1 = (bf16[24,1408]{1,0:T(8,128)(2,1)S(1)}, bf16[24,1408]{1,0:T(8,128)(2,1)}, u32[]{:S(2)}) copy-start(bf16[24,1408]{1,0:T(8,128)(2,1)} %param.11) | copy-start | bytes 202756
  109.7 2.2 %copy-start.5 = (bf16[1408]{0:T(1024)(128)(2,1)S(1)}, bf16[1408]{0:T(1024)(128)(2,1)}, u32[]{:S(2)}) copy-start(bf16[1408]{0:T(1024)(128)(2,1)} %param.21) | copy-start | bytes 8452
  109.7 2.5 %copy-start.6 = (s32[32]{0:T(128)S(1)}, s32[32]{0:T(128)}, u32[]{:S(2)}) copy-start(s32[32]{0:T(128)} %param.13) | copy-start | bytes 388
Sparse Core Ops, SparseCore 0:
  9.5 76.8 all-gather.2

commit v4 on v3

--- a/solution.py
+++ b/solution.py
@@ -49,7 +49,7 @@
     )(row_block).reshape(n * rows, width)
 
 
-def _ring_gather(x_ref, out_ref, send_right, send_left, send_partner, recv_sem, feat_index):
+def _ring_gather(x_ref, out_ref, send_right, send_left, send_partner, recv_sem, feat_index, after_first=None):
     tok_count = out_ref.shape[0]
     chips = tok_count // 2
     right_steps = chips // 2
@@ -79,7 +79,7 @@
 
     sends_partner = []
     out_ref[me] = x_ref[...]
-    forward_partner(x_ref, me)
+    arrived = []
     for step in range(1, right_steps + 1):
         if step == 1:
             src_right = x_ref
@@ -87,20 +87,27 @@
         else:
             from_left = slot_of(-(step - 1))
             remote(x_ref, from_left, send_right.at[0], right).wait_recv()
-            forward_partner(out_ref.at[from_left], from_left)
             src_right = out_ref.at[from_left]
-            if step - 1 <= left_steps:
-                from_right = slot_of(step - 1)
-                remote(x_ref, from_right, send_left.at[0], left).wait_recv()
-                forward_partner(out_ref.at[from_right], from_right)
-                src_left = out_ref.at[from_right]
+            arrived.append(from_left)
         copy = remote(src_right, slot_of(-(step - 1)), send_right.at[step - 1], right)
         copy.start()
         sends.append(copy)
+        if step > 1 and step - 1 <= left_steps:
+            from_right = slot_of(step - 1)
+            remote(x_ref, from_right, send_left.at[0], left).wait_recv()
+            src_left = out_ref.at[from_right]
+            arrived.append(from_right)
         if step <= left_steps:
             copy = remote(src_left, slot_of(step - 1), send_left.at[step - 1], left)
             copy.start()
             sends.append(copy)
+        if step == 1:
+            if after_first is not None:
+                after_first()
+            forward_partner(x_ref, me)
+        for slot in arrived:
+            forward_partner(out_ref.at[slot], slot)
+        arrived = []
     last_left = slot_of(-right_steps)
     remote(x_ref, last_left, send_right.at[0], right).wait_recv()
     forward_partner(out_ref.at[last_left], last_left)
@@ -133,13 +140,16 @@
     for peer in ring_peers:
         pl.semaphore_signal(barrier, inc=1, device_id=(peer, me), device_id_type=MESH)
     pl.semaphore_wait(barrier, len(peers) + len(ring_peers))
-    for peer in peers:
-        pltpu.make_async_remote_copy(
-            src_ref=row_ref, dst_ref=out_ref.at[me], send_sem=send_sem.at[peer],
-            recv_sem=recv_sem.at[me], device_id=(tok_index, peer), device_id_type=MESH,
-        ).start()
+
+    def start_rows():
+        for peer in peers:
+            pltpu.make_async_remote_copy(
+                src_ref=row_ref, dst_ref=out_ref.at[me], send_sem=send_sem.at[peer],
+                recv_sem=recv_sem.at[me], device_id=(tok_index, peer), device_id_type=MESH,
+            ).start()
+
+    _ring_gather(weight_ref, weight_out, send_right, send_left, send_partner, weight_recv, me, start_rows)
     out_ref[me] = row_ref[...]
-    _ring_gather(weight_ref, weight_out, send_right, send_left, send_partner, weight_recv, me)
     for peer in peers:
         pltpu.make_async_remote_copy(
             src_ref=row_ref, dst_ref=out_ref.at[peer], send_sem=send_sem.at[peer],
@@ -177,6 +187,44 @@
     return gathered.reshape(n * rows, width), weights
 
 
+def _route_kernel(n, packed_ref, out_ref, send_sem, recv_sem):
+    me = lax.axis_index("tok")
+    feat_index = lax.axis_index("feat")
+    peers = [lax.rem(me + d, n) for d in range(1, n)]
+    barrier = pltpu.get_barrier_semaphore()
+    for peer in peers:
+        pl.semaphore_signal(barrier, inc=1, device_id=(peer, feat_index), device_id_type=MESH)
+    pl.semaphore_wait(barrier, len(peers))
+    for peer in peers:
+        pltpu.make_async_remote_copy(
+            src_ref=packed_ref.at[peer], dst_ref=out_ref.at[me], send_sem=send_sem.at[peer],
+            recv_sem=recv_sem.at[me], device_id=(peer, feat_index), device_id_type=MESH,
+        ).start()
+    out_ref[me] = packed_ref[me]
+    for peer in peers:
+        pltpu.make_async_remote_copy(
+            src_ref=packed_ref.at[peer], dst_ref=out_ref.at[peer], send_sem=send_sem.at[peer],
+            recv_sem=recv_sem.at[peer], device_id=(peer, feat_index), device_id_type=MESH,
+        ).wait_recv()
+    for peer in peers:
+        pltpu.make_async_remote_copy(
+            src_ref=packed_ref.at[peer], dst_ref=out_ref.at[me], send_sem=send_sem.at[peer],
+            recv_sem=recv_sem.at[me], device_id=(peer, feat_index), device_id_type=MESH,
+        ).wait_send()
+
+
+def route_exchange(packed, collective_id):
+    n = packed.shape[0]
+    return pl.pallas_call(
+        functools.partial(_route_kernel, n),
+        out_shape=jax.ShapeDtypeStruct(packed.shape, packed.dtype),
+        in_specs=[pl.BlockSpec(memory_space=pltpu.VMEM)],
+        out_specs=pl.BlockSpec(memory_space=pltpu.VMEM),
+        scratch_shapes=[pltpu.SemaphoreType.DMA((n,)), pltpu.SemaphoreType.DMA((n,))],
+        compiler_params=pltpu.CompilerParams(collective_id=collective_id, has_side_effects=True),
+    )(packed)
+
+
 def _scatter_kernel(n, part_ref, out_ref, held, send_sem, recv_sem):
     me = lax.axis_index("feat")
     tok_index = lax.axis_index("tok")
@@ -298,7 +346,7 @@
     ).astype(jnp.bfloat16)
     packed = jnp.dot(select, embedded, preferred_element_type=jnp.float32).astype(jnp.bfloat16)
     packed = packed.reshape(peer_count, slot_count, embedded.shape[1])
-    received = lax.all_to_all(packed, "tok", split_axis=0, concat_axis=0, tiled=True)
+    received = route_exchange(packed, 5)
     return received.reshape(peer_count * slot_count, embedded.shape[1])
 
 

time: 211 us -> 204 us (0.967)
  blocking collectives: 30.5 us -> 0 us
  Pallas kernels: 136 us -> 158 us
    all_to_all x1 -> x0, blocking collectives: 30.5 us -> none  [route_rows(): lax.all_to_all(packed, 'tok', split_axis=0, concat_axis=0, tiled=True)]
    pallas_call x0 -> x1, Pallas kernels: none -> 25.4 us  [route_exchange(): pl.pallas_call(functools.partial(_route_kernel, n), out_shape=jax.ShapeDt...]
    pallas_call x2, Pallas kernels: 46.7 us -> 44.5 us  [gather_feat(): pl.pallas_call(functools.partial(_gather_kernel, n), out_shape=jax.ShapeD...]
where the time goes in v4:
time: 204 us
  Pallas kernels  158 us (77%)
  between operations  13.6 us (7%)
  matrix products  13.4 us (7%)
  local copies, waits for them, and re-layouts  9.56 us (5%)
  other arithmetic  8.37 us (4%)
    pallas_call x1, Pallas kernels, first_exchange(): pl.pallas_call(functools.partial(_first_kernel, n), out_shape=(jax.ShapeD...  46.6 us
    pallas_call x2, Pallas kernels, gather_feat(): pl.pallas_call(functools.partial(_gather_kernel, n), out_shape=jax.ShapeD...  44.5 us
    pallas_call x2, Pallas kernels, scatter_feat(): pl.pallas_call(functools.partial(_scatter_kernel, n), out_shape=jax.Shape...  41.5 us
    pallas_call x1, Pallas kernels, route_exchange(): pl.pallas_call(functools.partial(_route_kernel, n), out_shape=jax.ShapeDt...  25.4 us
    dot_general x1, matrix products, body(): jnp.dot(hidden, lower, preferred_element_type=jnp.float32)  5.51 us
    unnamed x16, local copies, waits for them, and re-layouts  4.26 us
  transfers between devices with their start and end apart: 1, of which 0 were waited for; matrix products, arithmetic and copies ran while one was open for 7% of the time, Pallas kernels for 43%

profile of v4, /device:TPU:1, one launch (start us, length us, event | category | flops | bytes accessed | tf_op | source)
XLA Modules:
  0.0 203.5 jit_solution(12539412564360561498)
XLA Ops:
  6.5 0.7 all-gather.3.cloned.1.call-update
  7.3 1.1 convert_reduce_fusion.1
  8.4 1.1 fusion.57
  9.5 0.7 convert_element_type.92
  10.2 1.6 fusion.59.row_ref
  11.8 46.6 %shard_map.109 = (bf16[16,24,1408]{2,1,0:T(8,128)(2,1)}, bf16[32,44,384]{2,1,0:T(8,128)(2,1)}) custom-call(bf16[24,1408]{1,0:T(8,128)(2,1)} %fusion.59.row_ref, bf16[44,384]{1,0:T(8,128)(2,1)} %weight_ref.1), custom_call_target="tpu_custom_call" | custom-call | tf_op jit(solution)/shard_map/pallas_call | solution.py:169
  58.4 2.1 %fusion.104 = (bf16[384,3,1,88]{0,3,1,2:T(8,128)(2,1)S(1)}, f32[384,3,1,88]{0,3,1,2:T(8,128)S(1)}) fusion(bf16[384,1408,1]{1,0,2:T(8,128)(2,1)} %bitcast.57, bf16[1408,3,88]{0,2,1:T(8,128)(2,1)} %param.14), kind=kOutput, calls=%fused_computation.141 | convolution fusion | flops 285576192 | bytes 2433024 | tf_op jit(solution)/shard_map/dot_general | solution.py:377
  60.8 0.4 copy-done.2
  61.4 2.6 %convolution_convert_fusion.1 = bf16[384,1408]{1,0:T(8,128)(2,1)} fusion(bf16[88,1408]{1,0:T(8,128)(2,1)} %param.15, f32[384,384]{0,1:T(8,128)S(1)} %get-tuple-element.18, f32[384]{0:T(512)S(1)} %fusion.12, f32[384]{0:T(512)S(1)} %get-tuple-element.17, bf16[384,3,1,88]{0,3,1,2:T(8,128)(2,1)} %copy-done.2), kind=kOutput, calls=%fused_computation.1 | convolution fusion | flops 122127360 | bytes 1989632 | tf_op jit(solution)/shard_map/dot_general | solution.py:296
  64.1 20.3 %shard_map.110 = f32[24,1408]{1,0:T(8,128)} custom-call(bf16[16,24,1408]{2,1,0:T(8,128)(2,1)} %bitcast.51), custom_call_target="tpu_custom_call" | custom-call | tf_op jit(solution)/shard_map/pallas_call | solution.py:255
  84.4 1.0 convert_reduce_fusion
  85.6 0.7 fusion.56.row_ref
  86.3 21.1 %shard_map.111 = bf16[16,24,1408]{2,1,0:T(8,128)(2,1)} custom-call(bf16[24,1408]{1,0:T(8,128)(2,1)} %fusion.56.row_ref), custom_call_target="tpu_custom_call" | custom-call | tf_op jit(solution)/shard_map/pallas_call | solution.py:42
  107.5 2.2 %reshape.138 = bf16[1408,384]{1,0:T(8,128)(2,1)} reshape(bf16[32,44,384]{2,1,0:T(8,128)(2,1)} %get-tuple-element.8) | data formatting | bytes 2162688 | tf_op jit(solution)/shard_map/reshape | solution.py:376
  110.1 2.2 %reshape.145 = bf16[1408,384]{1,0:T(8,128)(2,1)} reshape(bf16[32,44,384]{2,1,0:T(8,128)(2,1)} %all-gather.3.cloned.1.call-done) | data formatting | bytes 2162688
  112.3 5.5 %convolution_convert_fusion = bf16[384,1408]{1,0:T(8,128)(2,1)} fusion(bf16[1408,384]{1,0:T(8,128)(2,1)} %reshape.145, bf16[384,1408]{1,0:T(8,128)(2,1)} %bitcast.53, bf16[1408,384]{1,0:T(8,128)(2,1)} %reshape.138), kind=kOutput, calls=%fused_computation | convolution fusion | flops 840597504 | bytes 4325376 | tf_op jit(solution)/shard_map/dot_general | solution.py:384
  117.8 21.2 %shard_map.112 = f32[24,1408]{1,0:T(8,128)} custom-call(bf16[16,24,1408]{2,1,0:T(8,128)(2,1)} %bitcast.52), custom_call_target="tpu_custom_call" | custom-call | tf_op jit(solution)/shard_map/pallas_call | solution.py:255
  139.1 1.0 convert_reduce_fusion.2
  140.4 0.7 reshape.140.row_ref
  141.1 23.3 %shard_map.113 = bf16[16,6,5632]{2,1,0:T(8,128)(2,1)} custom-call(bf16[6,5632]{1,0:T(8,128)(2,1)} %reshape.140.row_ref), custom_call_target="tpu_custom_call" | custom-call | tf_op jit(solution)/shard_map/pallas_call | solution.py:42
  164.5 2.3 %reshape.141 = bf16[96,5632]{1,0:T(8,128)(2,1)} reshape(bf16[16,6,5632]{2,1,0:T(8,128)(2,1)} %shard_map.113) | data formatting | bytes 2162688 | tf_op jit(solution)/shard_map/reshape | solution.py:49
  166.8 2.8 %convolution_convert_fusion.2 = bf16[512,256]{1,0:T(8,128)(2,1)} fusion(bf16[96,5632]{1,0:T(8,128)(2,1)} %reshape.141, bf16[5632,256]{1,0:T(8,128)(2,1)S(1)} %copy-done, s32[96]{0:T(128)S(1)} %multiply_add_fusion), kind=kOutput, calls=%fused_computation.4 | convolution fusion | flops 302194688 | bytes 4227456 | tf_op jit(solution)/shard_map/dot_general | solution.py:347
  169.6 25.4 %shard_map.114 = bf16[32,16,256]{2,1,0:T(8,128)(2,1)} custom-call(bf16[32,16,256]{2,1,0:T(8,128)(2,1)} %bitcast.54), custom_call_target="tpu_custom_call" | custom-call | tf_op jit(solution)/shard_map/pallas_call | solution.py:218
  195.0 1.7 copy.13
  (33 shorter events, 1.5 us)
Async XLA Ops:
  6.5 160.3 %copy-start = (bf16[5632,256]{1,0:T(8,128)(2,1)S(1)}, bf16[5632,256]{1,0:T(8,128)(2,1)}, u32[]{:S(2)}) copy-start(bf16[5632,256]{1,0:T(8,128)(2,1)} %param.18) | copy-start | bytes 8650756
  6.5 103.6 %all-gather.3.cloned.1.call-start = ((), (), s32[]{:S(2)}) async-start(), calls=%async_computation | async-start | bytes 1216512 | tf_op jit(solution)/shard_map/all_gather | solution.py:374
  58.4 2.1 %copy-start.3 = (s32[384]{0:T(512)S(1)}, s32[384]{0:T(512)}, u32[]{:S(2)}) copy-start(s32[384]{0:T(512)} %param.12) | copy-start | bytes 4612
  60.5 0.7 copy-start.2
  64.1 20.3 %copy-start.4 = (bf16[1408]{0:T(1024)(128)(2,1)S(1)}, bf16[1408]{0:T(1024)(128)(2,1)}, u32[]{:S(2)}) copy-start(bf16[1408]{0:T(1024)(128)(2,1)} %param.20) | copy-start | bytes 8452
  64.1 20.3 %copy-start.1 = (bf16[24,1408]{1,0:T(8,128)(2,1)S(1)}, bf16[24,1408]{1,0:T(8,128)(2,1)}, u32[]{:S(2)}) copy-start(bf16[24,1408]{1,0:T(8,128)(2,1)} %param.11) | copy-start | bytes 202756
  107.5 2.2 %copy-start.5 = (bf16[1408]{0:T(1024)(128)(2,1)S(1)}, bf16[1408]{0:T(1024)(128)(2,1)}, u32[]{:S(2)}) copy-start(bf16[1408]{0:T(1024)(128)(2,1)} %param.21) | copy-start | bytes 8452
  107.5 2.5 %copy-start.6 = (s32[32]{0:T(128)S(1)}, s32[32]{0:T(128)}, u32[]{:S(2)}) copy-start(s32[32]{0:T(128)} %param.13) | copy-start | bytes 388
Sparse Core Ops, SparseCore 0:
  9.5 76.8 all-gather.2

commit v5 on v4

--- a/solution.py
+++ b/solution.py
@@ -225,6 +225,71 @@
     )(packed)
 
 
+def _mix_kernel(n, part_ref, resid_ref, gain_ref, resid_out, out_ref, held, mine,
+                scatter_send, scatter_recv, gather_send, gather_recv):
+    me = lax.axis_index("feat")
+    tok_index = lax.axis_index("tok")
+    peers = [lax.rem(me + d, n) for d in range(1, n)]
+    _greet(peers, tok_index)
+
+    def scatter_copy(peer, slot):
+        return pltpu.make_async_remote_copy(
+            src_ref=part_ref.at[peer], dst_ref=held.at[slot], send_sem=scatter_send.at[peer],
+            recv_sem=scatter_recv.at[slot], device_id=(tok_index, peer), device_id_type=MESH,
+        )
+
+    def gather_copy(peer, slot):
+        return pltpu.make_async_remote_copy(
+            src_ref=mine, dst_ref=out_ref.at[slot], send_sem=gather_send.at[peer],
+            recv_sem=gather_recv.at[slot], device_id=(tok_index, peer), device_id_type=MESH,
+        )
+
+    for peer in peers:
+        scatter_copy(peer, me).start()
+    total = part_ref[me].astype(jnp.float32)
+    for peer in peers:
+        scatter_copy(peer, peer).wait_recv()
+        total = total + held[peer].astype(jnp.float32)
+    summed = (resid_ref[...].astype(jnp.float32) + total).astype(jnp.bfloat16)
+    resid_out[...] = summed
+    as_float = summed.astype(jnp.float32)
+    center = jnp.mean(as_float, axis=-1, keepdims=True)
+    spread = jnp.mean(jnp.square(as_float - center), axis=-1, keepdims=True)
+    normed = ((as_float - center) * lax.rsqrt(spread + epsilon) * gain_ref[...]).astype(jnp.bfloat16)
+    mine[...] = normed
+    out_ref[me] = normed
+    for peer in peers:
+        gather_copy(peer, me).start()
+    for peer in peers:
+        gather_copy(peer, peer).wait_recv()
+    for peer in peers:
+        scatter_copy(peer, me).wait_send()
+        gather_copy(peer, me).wait_send()
+
+
+def mix_feat(parts, resid, gain, n, collective_id):
+    _, rows, width = parts.shape
+    new_resid, gathered = pl.pallas_call(
+        functools.partial(_mix_kernel, n),
+        out_shape=(
+            jax.ShapeDtypeStruct((rows, width), jnp.bfloat16),
+            jax.ShapeDtypeStruct((n, rows, width), jnp.bfloat16),
+        ),
+        in_specs=[pl.BlockSpec(memory_space=pltpu.VMEM)] * 3,
+        out_specs=(pl.BlockSpec(memory_space=pltpu.VMEM),) * 2,
+        scratch_shapes=[
+            pltpu.VMEM((n, rows, width), parts.dtype),
+            pltpu.VMEM((rows, width), jnp.bfloat16),
+            pltpu.SemaphoreType.DMA((n,)),
+            pltpu.SemaphoreType.DMA((n,)),
+            pltpu.SemaphoreType.DMA((n,)),
+            pltpu.SemaphoreType.DMA((n,)),
+        ],
+        compiler_params=pltpu.CompilerParams(collective_id=collective_id, has_side_effects=True),
+    )(parts, resid, gain.astype(jnp.float32).reshape(1, width))
+    return new_resid, gathered.reshape(n * rows, width)
+
+
 def _scatter_kernel(n, part_ref, out_ref, held, send_sem, recv_sem):
     me = lax.axis_index("feat")
     tok_index = lax.axis_index("tok")
@@ -376,21 +441,19 @@
     upper = weights.reshape(tok_count * weight_up.shape[0], units)
     projected = jnp.dot(gathered, flat_in, preferred_element_type=jnp.float32)
     attended = attend(projected, segment_ids, head_count)
-    second = (tokens.astype(jnp.float32) + scatter_rows(attended, project_out, 1)).astype(jnp.bfloat16)
-    normed_hidden = layer_norm(second, gain_hidden)
+    attn_parts = jnp.dot(attended, project_out, preferred_element_type=jnp.float32).astype(jnp.bfloat16)
+    second, hidden_rows = mix_feat(
+        attn_parts.reshape(feat_count, local_count, model_width), tokens, gain_hidden, feat_count, 1
+    )
     hidden = jax.nn.gelu(
-        project_rows(normed_hidden, upper, 2), approximate=False
+        jnp.dot(hidden_rows, upper, preferred_element_type=jnp.float32), approximate=False
     ).astype(jnp.bfloat16)
     down_parts = jnp.dot(hidden, lower, preferred_element_type=jnp.float32).astype(jnp.bfloat16)
-    mlp_sum = scatter_feat(
-        down_parts.reshape(feat_count, down_parts.shape[0] // feat_count, down_parts.shape[1]),
-        feat_count,
-        3,
+    _, final_rows = mix_feat(
+        down_parts.reshape(feat_count, local_count, model_width), second, gain_final, feat_count, 3
     )
-    residual_out = (second.astype(jnp.float32) + mlp_sum).astype(jnp.bfloat16)
-    normed_final = layer_norm(residual_out, gain_final)
-    merged = normed_final.reshape(local_count // 4, 4 * model_width)
-    embedded = project_rows(merged, weight_merge, 4).astype(jnp.bfloat16)
+    merged = final_rows.reshape(final_rows.shape[0] // 4, 4 * model_width)
+    embedded = jnp.dot(merged, weight_merge, preferred_element_type=jnp.float32).astype(jnp.bfloat16)
     return route_rows(embedded, segment_ids, owners)
 
 

time: 204 us -> 189 us (0.926)
  Pallas kernels: 158 us -> 144 us
  other arithmetic: 8.37 us -> 5.03 us
    pallas_call x4 -> x2, Pallas kernels: 86 us -> 71.4 us  [mix_feat(): pl.pallas_call(functools.partial(_mix_kernel, n), out_shape=(jax.ShapeDty...]
    another operation x0 -> x1, local copies, waits for them, and re-layouts: none -> 2.59 us  [body(): merged = final_rows.reshape(final_rows.shape[0] // 4, 4 * model_width)]
    reduce_sum x3 -> x1, other arithmetic: 3.21 us -> 1.14 us  [layer_norm(): center = jnp.mean(as_float, axis=-1, keepdims=True)]
    unnamed x16 -> x12, local copies, waits for them, and re-layouts: 4.26 us -> 4.24 us
  transfers between devices with their start and end apart: 1 -> 1, of which waited for: 0 -> 0; matrix products, arithmetic and copies ran while one was open for 7% -> 8% of each run, Pallas kernels for 43% -> 44%
where the time goes in v5:
time: 189 us; the launch traced here: 188 us
  Pallas kernels  144 us (76%)
  between operations  13.5 us (7%)
  matrix products  13.4 us (7%)
  local copies, waits for them, and re-layouts  11 us (6%)
  other arithmetic  5.03 us (3%)
    pallas_call x2, Pallas kernels, mix_feat(): pl.pallas_call(functools.partial(_mix_kernel, n), out_shape=(jax.ShapeDty...  71.4 us
    pallas_call x1, Pallas kernels, first_exchange(): pl.pallas_call(functools.partial(_first_kernel, n), out_shape=(jax.ShapeD...  46.1 us
    pallas_call x1, Pallas kernels, route_exchange(): pl.pallas_call(functools.partial(_route_kernel, n), out_shape=jax.ShapeDt...  26.8 us
    dot_general x1, matrix products, body(): jnp.dot(hidden, lower, preferred_element_type=jnp.float32)  5.51 us
    unnamed x12, local copies, waits for them, and re-layouts  4.24 us
  transfers between devices with their start and end apart: 1, of which 0 were waited for; matrix products, arithmetic and copies ran while one was open for 8% of the time, Pallas kernels for 44%

profile of v5, /device:TPU:1, one launch (start us, length us, event | category | flops | bytes accessed | tf_op | source)
XLA Modules:
  0.0 187.9 jit_solution(13456121102883957489)
XLA Ops:
  6.5 0.7 all-gather.3.cloned.1.call-update
  7.3 1.1 convert_reduce_fusion
  8.4 1.1 fusion.50
  9.5 0.7 convert_element_type.68
  10.2 1.3 reshape.125.gain_ref
  11.5 1.6 fusion.52.row_ref
  13.1 46.1 %shard_map.109 = (bf16[16,24,1408]{2,1,0:T(8,128)(2,1)}, bf16[32,44,384]{2,1,0:T(8,128)(2,1)}) custom-call(bf16[24,1408]{1,0:T(8,128)(2,1)} %fusion.52.row_ref, bf16[44,384]{1,0:T(8,128)(2,1)} %weight_ref.1), custom_call_target="tpu_custom_call" | custom-call | tf_op jit(solution)/shard_map/pallas_call | solution.py:169
  59.2 2.2 %reshape.118 = bf16[1408,384]{1,0:T(8,128)(2,1)} reshape(bf16[32,44,384]{2,1,0:T(8,128)(2,1)} %get-tuple-element.12) | data formatting | bytes 2162688 | tf_op jit(solution)/shard_map/reshape | solution.py:441
  61.4 0.6 reshape.127.gain_ref
  62.1 2.1 %fusion.90 = (bf16[384,3,1,88]{0,3,1,2:T(8,128)(2,1)S(1)}, f32[384,3,1,88]{0,3,1,2:T(8,128)S(1)}) fusion(bf16[384,1408,1]{1,0,2:T(8,128)(2,1)} %bitcast.57, bf16[1408,3,88]{0,2,1:T(8,128)(2,1)} %param.14), kind=kOutput, calls=%fused_computation.119 | convolution fusion | flops 285576192 | bytes 2433024 | tf_op jit(solution)/shard_map/dot_general | solution.py:442
  64.2 0.3 fusion.91
  64.5 0.4 copy-done.1
  64.9 0.1 fusion.12
  65.0 2.7 %convolution_convert_fusion.1 = bf16[384,1408]{1,0:T(8,128)(2,1)} fusion(bf16[88,1408]{1,0:T(8,128)(2,1)} %param.15, f32[384,384]{0,1:T(8,128)S(1)} %get-tuple-element.20, f32[384]{0:T(512)S(1)} %fusion.12, f32[384]{0:T(512)S(1)} %get-tuple-element.19, bf16[384,3,1,88]{0,3,1,2:T(8,128)(2,1)} %copy-done.1), kind=kOutput, calls=%fused_computation.1 | convolution fusion | flops 122127360 | bytes 1989632 | tf_op jit(solution)/shard_map/dot_general | solution.py:444
  67.7 37.2 %shard_map.110 = (bf16[24,1408]{1,0:T(8,128)(2,1)}, bf16[16,24,1408]{2,1,0:T(8,128)(2,1)}) custom-call(bf16[16,24,1408]{2,1,0:T(8,128)(2,1)} %bitcast.52, bf16[24,1408]{1,0:T(8,128)(2,1)} %resid_ref.1, f32[1,1408]{1,0:T(1,128)} %reshape.125.gain_ref), custom_call_target="tpu_custom_call" | custom-call | tf_op jit(solution)/shard_map/pallas_call | solution.py:272
  104.9 0.1 subtract_reduce_fusion
  105.0 0.2 convert_reduce_fusion.1
  105.3 2.2 %reshape.129 = bf16[1408,384]{1,0:T(8,128)(2,1)} reshape(bf16[32,44,384]{2,1,0:T(8,128)(2,1)} %all-gather.3.cloned.1.call-done) | data formatting | bytes 2162688
  107.5 5.5 %convolution_convert_fusion = bf16[384,1408]{1,0:T(8,128)(2,1)} fusion(bf16[1408,384]{1,0:T(8,128)(2,1)} %reshape.129, bf16[384,1408]{1,0:T(8,128)(2,1)} %bitcast.56, bf16[1408,384]{1,0:T(8,128)(2,1)} %reshape.118), kind=kOutput, calls=%fused_computation | convolution fusion | flops 840597504 | bytes 4325376 | tf_op jit(solution)/shard_map/dot_general | solution.py:451
  113.0 34.2 %shard_map.111 = (bf16[24,1408]{1,0:T(8,128)(2,1)}, bf16[16,24,1408]{2,1,0:T(8,128)(2,1)}) custom-call(bf16[16,24,1408]{2,1,0:T(8,128)(2,1)} %bitcast.51, bf16[24,1408]{1,0:T(8,128)(2,1)} %get-tuple-element.13.resid_ref, f32[1,1408]{1,0:T(1,128)} %reshape.127.gain_ref), custom_call_target="tpu_custom_call" | custom-call | tf_op jit(solution)/shard_map/pallas_call | solution.py:272
  147.2 2.6 %reshape_reshape.3 = bf16[96,5632]{1,0:T(8,128)(2,1)} reshape(bf16[16,24,1408]{2,1,0:T(8,128)(2,1)} %get-tuple-element.14) | data formatting | bytes 2162688 | tf_op jit(solution)/shard_map/reshape;reshape | solution.py:455
  149.8 2.8 %convolution_convert_fusion.2 = bf16[512,256]{1,0:T(8,128)(2,1)} fusion(bf16[96,5632]{1,0:T(8,128)(2,1)} %reshape_reshape.3, bf16[5632,256]{1,0:T(8,128)(2,1)S(1)} %copy-done, s32[96]{0:T(128)S(1)} %multiply_add_fusion), kind=kOutput, calls=%fused_computation.4 | convolution fusion | flops 302194688 | bytes 4227456 | tf_op jit(solution)/shard_map/dot_general | solution.py:412
  152.6 26.8 %shard_map.112 = bf16[32,16,256]{2,1,0:T(8,128)(2,1)} custom-call(bf16[32,16,256]{2,1,0:T(8,128)(2,1)} %bitcast.53), custom_call_target="tpu_custom_call" | custom-call | tf_op jit(solution)/shard_map/pallas_call | solution.py:218
  179.4 1.7 copy.13
  (16 shorter events, 0.3 us)
Async XLA Ops:
  6.5 143.3 %copy-start = (bf16[5632,256]{1,0:T(8,128)(2,1)S(1)}, bf16[5632,256]{1,0:T(8,128)(2,1)}, u32[]{:S(2)}) copy-start(bf16[5632,256]{1,0:T(8,128)(2,1)} %param.18) | copy-start | bytes 8650756
  6.5 98.7 %all-gather.3.cloned.1.call-start = ((), (), s32[]{:S(2)}) async-start(), calls=%async_computation | async-start | bytes 1216512 | tf_op jit(solution)/shard_map/all_gather | solution.py:439
  59.2 2.2 %copy-start.3 = (bf16[1408]{0:T(1024)(128)(2,1)S(1)}, bf16[1408]{0:T(1024)(128)(2,1)}, u32[]{:S(2)}) copy-start(bf16[1408]{0:T(1024)(128)(2,1)} %param.21) | copy-start | bytes 8452
  59.2 2.8 %copy-start.2 = (s32[384]{0:T(512)S(1)}, s32[384]{0:T(512)}, u32[]{:S(2)}) copy-start(s32[384]{0:T(512)} %param.12) | copy-start | bytes 4612
  64.2 0.7 copy-start.1
  67.7 37.5 %copy-start.4 = (s32[32]{0:T(128)S(1)}, s32[32]{0:T(128)}, u32[]{:S(2)}) copy-start(s32[32]{0:T(128)} %param.13) | copy-start | bytes 388
Sparse Core Ops, SparseCore 0:
  9.5 76.8 all-gather.2

commit v6 on v5

--- a/solution.py
+++ b/solution.py
@@ -436,9 +436,10 @@
     flat_in = project_in.reshape(model_width, 3 * project_in.shape[2])
     local_count = tokens.shape[0]
     normed = layer_norm(tokens, gain_attend)
-    lower = lax.all_gather(weight_down, "tok", axis=1, tiled=True)
-    gathered, weights = first_exchange(normed, weight_up, feat_count, tok_count, 0)
-    upper = weights.reshape(tok_count * weight_up.shape[0], units)
+    stacked = jnp.concatenate([weight_up, weight_down.T], axis=1)
+    gathered, weights = first_exchange(normed, stacked, feat_count, tok_count, 0)
+    upper = weights[:, :, :units].reshape(tok_count * weight_up.shape[0], units)
+    lower_t = weights[:, :, units:].reshape(tok_count * weight_up.shape[0], units)
     projected = jnp.dot(gathered, flat_in, preferred_element_type=jnp.float32)
     attended = attend(projected, segment_ids, head_count)
     attn_parts = jnp.dot(attended, project_out, preferred_element_type=jnp.float32).astype(jnp.bfloat16)
@@ -448,7 +449,9 @@
     hidden = jax.nn.gelu(
         jnp.dot(hidden_rows, upper, preferred_element_type=jnp.float32), approximate=False
     ).astype(jnp.bfloat16)
-    down_parts = jnp.dot(hidden, lower, preferred_element_type=jnp.float32).astype(jnp.bfloat16)
+    down_parts = lax.dot_general(
+        hidden, lower_t, (((1,), (1,)), ((), ())), preferred_element_type=jnp.float32
+    ).astype(jnp.bfloat16)
     _, final_rows = mix_feat(
         down_parts.reshape(feat_count, local_count, model_width), second, gain_final, feat_count, 3
     )

time: 189 us -> 182 us (0.963)
  between operations: 13.5 us -> 0.11 us
  Pallas kernels: 144 us -> 148 us
  local copies, waits for them, and re-layouts: 11 us -> 13.5 us
    pallas_call x1, Pallas kernels: 46.1 us -> 50.7 us  [first_exchange(): pl.pallas_call(functools.partial(_first_kernel, n), out_shape=(jax.ShapeD...]
    slice x0 -> x1, local copies, waits for them, and re-layouts: none -> 3.25 us  [body(): upper = weights[:, :, :units].reshape(tok_count * weight_up.shape[0], units)]
    unnamed x12 -> x13, local copies, waits for them, and re-layouts: 4.24 us -> 2.05 us
    pallas_call x1, Pallas kernels: 26.8 us -> 24.6 us  [route_exchange(): pl.pallas_call(functools.partial(_route_kernel, n), out_shape=jax.ShapeDt...]
    reshape x1 -> x2, local copies, waits for them, and re-layouts: 2.17 us -> 4.3 us  [the longest x1 2.15 us: body(): weights[:, :, units:].reshape(tok_count * weight_up.shape[0], units)]
  transfers between devices with their start and end apart: 1 -> 0, of which waited for: 0 -> 0; matrix products, arithmetic and copies ran while one was open for 8% -> 0% of each run, Pallas kernels for 44% -> 0%
where the time goes in v6:
time: 182 us; the launch traced here: 181 us
  Pallas kernels  148 us (81%)
  local copies, waits for them, and re-layouts  13.5 us (7%)
  matrix products  13.4 us (7%)
  other arithmetic  6.5 us (4%)
    pallas_call x2, Pallas kernels, mix_feat(): pl.pallas_call(functools.partial(_mix_kernel, n), out_shape=(jax.ShapeDty...  72.4 us
    pallas_call x1, Pallas kernels, first_exchange(): pl.pallas_call(functools.partial(_first_kernel, n), out_shape=(jax.ShapeD...  50.7 us
    pallas_call x1, Pallas kernels, route_exchange(): pl.pallas_call(functools.partial(_route_kernel, n), out_shape=jax.ShapeDt...  24.6 us
    dot_general x1, matrix products, body(): lax.dot_general(hidden, lower_t, (((1,), (1,)), ((), ())), preferred_elem...  5.53 us

profile of v6, /device:TPU:1, one launch (start us, length us, event | category | flops | bytes accessed | tf_op | source)
XLA Modules:
  0.0 181.1 jit_solution(17597620845536163714)
XLA Ops:
  0.0 0.8 convert_element_type.68
  0.8 1.0 convert_reduce_fusion
  1.9 1.1 fusion.50
  3.0 1.6 fusion.52.row_ref
  4.6 1.4 pad_maximum_fusion.weight_ref
  6.0 50.7 %shard_map.109 = (bf16[16,24,1408]{2,1,0:T(8,128)(2,1)}, bf16[32,44,768]{2,1,0:T(8,128)(2,1)}) custom-call(bf16[24,1408]{1,0:T(8,128)(2,1)} %fusion.52.row_ref, bf16[44,768]{1,0:T(8,128)(2,1)} %pad_maximum_fusion.weight_ref), custom_call_target="tpu_custom_call" | custom-call | tf_op jit(solution)/shard_map/pallas_call | solution.py:169
  56.7 3.3 %fusion.90 = (bf16[32,44,384]{2,1,0:T(8,128)(2,1)}, bf16[32,44,384]{2,1,0:T(8,128)(2,1)}) fusion(bf16[32,44,768]{2,1,0:T(8,128)(2,1)} %get-tuple-element.12), kind=kLoop, calls=%fused_computation.120 | loop fusion | bytes 4325376 | tf_op jit(solution)/shard_map/slice | solution.py:441
  59.9 2.2 %reshape.122 = bf16[1408,384]{1,0:T(8,128)(2,1)} reshape(bf16[32,44,384]{2,1,0:T(8,128)(2,1)} %get-tuple-element.18) | data formatting | bytes 2162688 | tf_op jit(solution)/shard_map/reshape | solution.py:442
  62.1 2.1 %fusion.91 = (bf16[384,3,1,88]{0,3,1,2:T(8,128)(2,1)S(1)}, f32[384,3,1,88]{0,3,1,2:T(8,128)S(1)}) fusion(bf16[384,1408,1]{1,0,2:T(8,128)(2,1)} %bitcast.54, bf16[1408,3,88]{0,2,1:T(8,128)(2,1)} %param.14), kind=kOutput, calls=%fused_computation.121 | convolution fusion | flops 285576192 | bytes 2433024 | tf_op jit(solution)/shard_map/dot_general | solution.py:443
  64.2 0.3 fusion.92
  64.5 0.4 copy-done.1
  64.8 0.1 fusion.12
  65.0 2.7 %convolution_convert_fusion.1 = bf16[384,1408]{1,0:T(8,128)(2,1)} fusion(bf16[88,1408]{1,0:T(8,128)(2,1)} %param.15, f32[384,384]{0,1:T(8,128)S(1)} %get-tuple-element.22, f32[384]{0:T(512)S(1)} %fusion.12, f32[384]{0:T(512)S(1)} %get-tuple-element.21, bf16[384,3,1,88]{0,3,1,2:T(8,128)(2,1)} %copy-done.1), kind=kOutput, calls=%fused_computation.1 | convolution fusion | flops 122127360 | bytes 1989632 | tf_op jit(solution)/shard_map/dot_general | solution.py:445
  67.6 0.6 reshape.129.gain_ref
  68.2 36.5 %shard_map.110 = (bf16[24,1408]{1,0:T(8,128)(2,1)}, bf16[16,24,1408]{2,1,0:T(8,128)(2,1)}) custom-call(bf16[16,24,1408]{2,1,0:T(8,128)(2,1)} %bitcast.50, bf16[24,1408]{1,0:T(8,128)(2,1)} %resid_ref.1, f32[1,1408]{1,0:T(1,128)} %reshape.129.gain_ref), custom_call_target="tpu_custom_call" | custom-call | tf_op jit(solution)/shard_map/pallas_call | solution.py:272
  104.7 2.1 %reshape.121 = bf16[1408,384]{1,0:T(8,128)(2,1)} reshape(bf16[32,44,384]{2,1,0:T(8,128)(2,1)} %get-tuple-element.17) | data formatting | bytes 2162688 | tf_op jit(solution)/shard_map/reshape | solution.py:441
  106.8 5.5 %convolution_convert_fusion = bf16[384,1408]{1,0:T(8,128)(2,1)} fusion(bf16[1408,384]{1,0:T(8,128)(2,1)} %reshape.122, bf16[384,1408]{1,0:T(8,128)(2,1)} %bitcast.55, bf16[1408,384]{1,0:T(8,128)(2,1)} %reshape.121), kind=kOutput, calls=%fused_computation | convolution fusion | flops 840597504 | bytes 4325376 | tf_op jit(solution)/shard_map/dot_general | solution.py:452
  112.4 0.6 reshape.131.gain_ref
  113.0 35.9 %shard_map.111 = (bf16[24,1408]{1,0:T(8,128)(2,1)}, bf16[16,24,1408]{2,1,0:T(8,128)(2,1)}) custom-call(bf16[16,24,1408]{2,1,0:T(8,128)(2,1)} %bitcast.49, bf16[24,1408]{1,0:T(8,128)(2,1)} %get-tuple-element.13.resid_ref, f32[1,1408]{1,0:T(1,128)} %reshape.131.gain_ref), custom_call_target="tpu_custom_call" | custom-call | tf_op jit(solution)/shard_map/pallas_call | solution.py:272
  148.9 2.6 %reshape_reshape.3 = bf16[96,5632]{1,0:T(8,128)(2,1)} reshape(bf16[16,24,1408]{2,1,0:T(8,128)(2,1)} %get-tuple-element.14) | data formatting | bytes 2162688 | tf_op jit(solution)/shard_map/reshape;reshape | solution.py:458
  151.7 0.2 convert_reduce_fusion.1
  152.0 2.8 %convolution_convert_fusion.2 = bf16[512,256]{1,0:T(8,128)(2,1)} fusion(bf16[96,5632]{1,0:T(8,128)(2,1)} %reshape_reshape.3, bf16[5632,256]{1,0:T(8,128)(2,1)S(1)} %copy-done, s32[96]{0:T(128)S(1)} %multiply_add_fusion), kind=kOutput, calls=%fused_computation.4 | convolution fusion | flops 302194688 | bytes 4227456 | tf_op jit(solution)/shard_map/dot_general | solution.py:412
  154.8 24.6 %shard_map.112 = bf16[32,16,256]{2,1,0:T(8,128)(2,1)} custom-call(bf16[32,16,256]{2,1,0:T(8,128)(2,1)} %bitcast.51), custom_call_target="tpu_custom_call" | custom-call | tf_op jit(solution)/shard_map/pallas_call | solution.py:218
  179.5 1.7 copy.13
  (17 shorter events, 0.3 us)
Async XLA Ops:
  0.0 152.0 %copy-start = (bf16[5632,256]{1,0:T(8,128)(2,1)S(1)}, bf16[5632,256]{1,0:T(8,128)(2,1)}, u32[]{:S(2)}) copy-start(bf16[5632,256]{1,0:T(8,128)(2,1)} %param.18) | copy-start | bytes 8650756
  62.1 2.1 %copy-start.2 = (s32[384]{0:T(512)S(1)}, s32[384]{0:T(512)}, u32[]{:S(2)}) copy-start(s32[384]{0:T(512)} %param.12) | copy-start | bytes 4612
  64.1 0.7 copy-start.1
  65.0 2.7 %copy-start.3 = (bf16[1408]{0:T(1024)(128)(2,1)S(1)}, bf16[1408]{0:T(1024)(128)(2,1)}, u32[]{:S(2)}) copy-start(bf16[1408]{0:T(1024)(128)(2,1)} %param.20) | copy-start | bytes 8452
  106.8 5.5 %copy-start.4 = (bf16[1408]{0:T(1024)(128)(2,1)S(1)}, bf16[1408]{0:T(1024)(128)(2,1)}, u32[]{:S(2)}) copy-start(bf16[1408]{0:T(1024)(128)(2,1)} %param.21) | copy-start | bytes 8452
  148.9 3.0 %copy-start.5 = (s32[32]{0:T(128)S(1)}, s32[32]{0:T(128)}, u32[]{:S(2)}) copy-start(s32[32]{0:T(128)} %param.13) | copy-start | bytes 388

commit v7 on v6

--- a/solution.py
+++ b/solution.py
@@ -438,8 +438,9 @@
     normed = layer_norm(tokens, gain_attend)
     stacked = jnp.concatenate([weight_up, weight_down.T], axis=1)
     gathered, weights = first_exchange(normed, stacked, feat_count, tok_count, 0)
-    upper = weights[:, :, :units].reshape(tok_count * weight_up.shape[0], units)
-    lower_t = weights[:, :, units:].reshape(tok_count * weight_up.shape[0], units)
+    both = weights.reshape(tok_count * weight_up.shape[0], 2 * units)
+    upper = both[:, :units]
+    lower_t = both[:, units:]
     projected = jnp.dot(gathered, flat_in, preferred_element_type=jnp.float32)
     attended = attend(projected, segment_ids, head_count)
     attn_parts = jnp.dot(attended, project_out, preferred_element_type=jnp.float32).astype(jnp.bfloat16)

time: 182 us -> 178 us (0.978)
  local copies, waits for them, and re-layouts: 13.5 us -> 9.94 us
    slice x1 -> x0, local copies, waits for them, and re-layouts: 3.25 us -> none  [body(): upper = weights[:, :, :units].reshape(tok_count * weight_up.shape[0], units)]
    reshape x2 -> x1, local copies, waits for them, and re-layouts: 4.3 us -> 4 us  [body(): both = weights.reshape(tok_count * weight_up.shape[0], 2 * units)]
where the time goes in v7:
time: 178 us
  Pallas kernels  148 us (83%)
  matrix products  13.4 us (8%)
  local copies, waits for them, and re-layouts  9.94 us (6%)
  other arithmetic  6.5 us (4%)
    pallas_call x2, Pallas kernels, mix_feat(): pl.pallas_call(functools.partial(_mix_kernel, n), out_shape=(jax.ShapeDty...  72.4 us
    pallas_call x1, Pallas kernels, first_exchange(): pl.pallas_call(functools.partial(_first_kernel, n), out_shape=(jax.ShapeD...  50.7 us
    pallas_call x1, Pallas kernels, route_exchange(): pl.pallas_call(functools.partial(_route_kernel, n), out_shape=jax.ShapeDt...  24.6 us
    dot_general x1, matrix products, body(): lax.dot_general(hidden, lower_t, (((1,), (1,)), ((), ())), preferred_elem...  5.52 us
    reshape x1, local copies, waits for them, and re-layouts, body(): both = weights.reshape(tok_count * weight_up.shape[0], 2 * units)  4 us

profile of v7, /device:TPU:1, one launch (start us, length us, event | category | flops | bytes accessed | tf_op | source)
XLA Modules:
  0.0 177.6 jit_solution(8023634854884408262)
XLA Ops:
  0.0 0.8 convert_element_type.68
  0.8 1.0 convert_reduce_fusion
  1.9 1.1 fusion.56
  3.0 1.6 fusion.58.row_ref
  4.6 1.4 pad_maximum_fusion.weight_ref
  6.0 50.7 %shard_map.109 = (bf16[16,24,1408]{2,1,0:T(8,128)(2,1)}, bf16[32,44,768]{2,1,0:T(8,128)(2,1)}) custom-call(bf16[24,1408]{1,0:T(8,128)(2,1)} %fusion.58.row_ref, bf16[44,768]{1,0:T(8,128)(2,1)} %pad_maximum_fusion.weight_ref), custom_call_target="tpu_custom_call" | custom-call | tf_op jit(solution)/shard_map/pallas_call | solution.py:169
  56.7 4.0 %reshape.118 = bf16[1408,768]{1,0:T(8,128)(2,1)} reshape(bf16[32,44,768]{2,1,0:T(8,128)(2,1)} %get-tuple-element.12) | data formatting | bytes 4325376 | tf_op jit(solution)/shard_map/reshape | solution.py:441
  60.7 2.1 %fusion.96 = (bf16[384,3,1,88]{0,3,1,2:T(8,128)(2,1)S(1)}, f32[384,3,1,88]{0,3,1,2:T(8,128)S(1)}) fusion(bf16[384,1408,1]{1,0,2:T(8,128)(2,1)} %bitcast.52, bf16[1408,3,88]{0,2,1:T(8,128)(2,1)} %param.14), kind=kOutput, calls=%fused_computation.123 | convolution fusion | flops 285576192 | bytes 2433024 | tf_op jit(solution)/shard_map/dot_general | solution.py:444
  62.8 0.3 fusion.97
  63.1 0.4 copy-done.1
  63.4 0.1 fusion.19
  63.5 2.7 %convolution_convert_fusion.1 = bf16[384,1408]{1,0:T(8,128)(2,1)} fusion(bf16[88,1408]{1,0:T(8,128)(2,1)} %param.15, f32[384,384]{0,1:T(8,128)S(1)} %get-tuple-element.20, f32[384]{0:T(512)S(1)} %fusion.19, f32[384]{0:T(512)S(1)} %get-tuple-element.19, bf16[384,3,1,88]{0,3,1,2:T(8,128)(2,1)} %copy-done.1), kind=kOutput, calls=%fused_computation.1 | convolution fusion | flops 122127360 | bytes 1989632 | tf_op jit(solution)/shard_map/dot_general | solution.py:446
  66.2 0.6 reshape.125.gain_ref
  66.8 36.5 %shard_map.110 = (bf16[24,1408]{1,0:T(8,128)(2,1)}, bf16[16,24,1408]{2,1,0:T(8,128)(2,1)}) custom-call(bf16[16,24,1408]{2,1,0:T(8,128)(2,1)} %bitcast.47, bf16[24,1408]{1,0:T(8,128)(2,1)} %resid_ref.1, f32[1,1408]{1,0:T(1,128)} %reshape.125.gain_ref), custom_call_target="tpu_custom_call" | custom-call | tf_op jit(solution)/shard_map/pallas_call | solution.py:272
  103.3 5.5 %convolution_convert_fusion = bf16[384,1408]{1,0:T(8,128)(2,1)} fusion(bf16[1408,768]{1,0:T(8,128)(2,1)} %reshape.118, bf16[384,1408]{1,0:T(8,128)(2,1)} %bitcast.53), kind=kOutput, calls=%fused_computation | convolution fusion | flops 840597504 | bytes 4325376 | tf_op jit(solution)/shard_map/dot_general | solution.py:453
  108.8 0.6 reshape.127.gain_ref
  109.4 35.9 %shard_map.111 = (bf16[24,1408]{1,0:T(8,128)(2,1)}, bf16[16,24,1408]{2,1,0:T(8,128)(2,1)}) custom-call(bf16[16,24,1408]{2,1,0:T(8,128)(2,1)} %bitcast.48, bf16[24,1408]{1,0:T(8,128)(2,1)} %get-tuple-element.13.resid_ref, f32[1,1408]{1,0:T(1,128)} %reshape.127.gain_ref), custom_call_target="tpu_custom_call" | custom-call | tf_op jit(solution)/shard_map/pallas_call | solution.py:272
  145.3 2.6 %reshape_reshape.3 = bf16[96,5632]{1,0:T(8,128)(2,1)} reshape(bf16[16,24,1408]{2,1,0:T(8,128)(2,1)} %get-tuple-element.14) | data formatting | bytes 2162688 | tf_op jit(solution)/shard_map/reshape;reshape | solution.py:459
  147.9 0.1 reshape.109
  148.1 0.1 subtract_reduce_fusion
  148.2 0.2 convert_reduce_fusion.1
  148.5 2.8 %convolution_convert_fusion.2 = bf16[512,256]{1,0:T(8,128)(2,1)} fusion(bf16[96,5632]{1,0:T(8,128)(2,1)} %reshape_reshape.3, bf16[5632,256]{1,0:T(8,128)(2,1)S(1)} %copy-done, s32[96]{0:T(128)S(1)} %multiply_add_fusion), kind=kOutput, calls=%fused_computation.4 | convolution fusion | flops 302194688 | bytes 4227456 | tf_op jit(solution)/shard_map/dot_general | solution.py:412
  151.3 24.6 %shard_map.112 = bf16[32,16,256]{2,1,0:T(8,128)(2,1)} custom-call(bf16[32,16,256]{2,1,0:T(8,128)(2,1)} %bitcast.49), custom_call_target="tpu_custom_call" | custom-call | tf_op jit(solution)/shard_map/pallas_call | solution.py:218
  175.9 1.7 copy.13
  (15 shorter events, 0.1 us)
Async XLA Ops:
  0.0 148.5 %copy-start = (bf16[5632,256]{1,0:T(8,128)(2,1)S(1)}, bf16[5632,256]{1,0:T(8,128)(2,1)}, u32[]{:S(2)}) copy-start(bf16[5632,256]{1,0:T(8,128)(2,1)} %param.18) | copy-start | bytes 8650756
  60.7 2.1 %copy-start.2 = (s32[384]{0:T(512)S(1)}, s32[384]{0:T(512)}, u32[]{:S(2)}) copy-start(s32[384]{0:T(512)} %param.12) | copy-start | bytes 4612
  62.7 0.7 copy-start.1
  63.5 2.7 %copy-start.3 = (bf16[1408]{0:T(1024)(128)(2,1)S(1)}, bf16[1408]{0:T(1024)(128)(2,1)}, u32[]{:S(2)}) copy-start(bf16[1408]{0:T(1024)(128)(2,1)} %param.20) | copy-start | bytes 8452
  103.3 5.5 %copy-start.4 = (bf16[1408]{0:T(1024)(128)(2,1)S(1)}, bf16[1408]{0:T(1024)(128)(2,1)}, u32[]{:S(2)}) copy-start(bf16[1408]{0:T(1024)(128)(2,1)} %param.21) | copy-start | bytes 8452
  145.3 3.0 %copy-start.5 = (s32[32]{0:T(128)S(1)}, s32[32]{0:T(128)}, u32[]{:S(2)}) copy-start(s32[32]{0:T(128)} %param.13) | copy-start | bytes 388

commit v8 on v6

--- a/solution.py
+++ b/solution.py
@@ -49,7 +49,8 @@
     )(row_block).reshape(n * rows, width)
 
 
-def _ring_gather(x_ref, out_ref, send_right, send_left, send_partner, recv_sem, feat_index, after_first=None):
+def _ring_gather(x_ref, out_ref, send_right, send_left, send_partner, recv_sem, feat_index, after_first=None,
+                 hook=None, hook_step=1):
     tok_count = out_ref.shape[0]
     chips = tok_count // 2
     right_steps = chips // 2
@@ -108,6 +109,8 @@
         for slot in arrived:
             forward_partner(out_ref.at[slot], slot)
         arrived = []
+        if hook is not None and step == min(hook_step, right_steps):
+            hook()
     last_left = slot_of(-right_steps)
     remote(x_ref, last_left, send_right.at[0], right).wait_recv()
     forward_partner(out_ref.at[last_left], last_left)
@@ -288,6 +291,97 @@
         compiler_params=pltpu.CompilerParams(collective_id=collective_id, has_side_effects=True),
     )(parts, resid, gain.astype(jnp.float32).reshape(1, width))
     return new_resid, gathered.reshape(n * rows, width)
+
+
+def _mix_ring_kernel(n, part_ref, resid_ref, gain_ref, weight_ref, resid_out, out_ref, weight_out,
+                     held, mine, scatter_send, scatter_recv, gather_send, gather_recv,
+                     send_right, send_left, send_partner, weight_recv):
+    me = lax.axis_index("feat")
+    tok_index = lax.axis_index("tok")
+    chips = weight_out.shape[0] // 2
+    chip = tok_index // 2
+    core = tok_index % 2
+    peers = [lax.rem(me + d, n) for d in range(1, n)]
+    barrier = pltpu.get_barrier_semaphore()
+    for peer in peers:
+        pl.semaphore_signal(barrier, inc=1, device_id=(tok_index, peer), device_id_type=MESH)
+    ring_peers = [
+        lax.rem(chip + 1, chips) * 2 + core,
+        lax.rem(chip + chips - 1, chips) * 2 + core,
+        chip * 2 + (1 - core),
+    ]
+    for peer in ring_peers:
+        pl.semaphore_signal(barrier, inc=1, device_id=(peer, me), device_id_type=MESH)
+    pl.semaphore_wait(barrier, len(peers) + len(ring_peers))
+
+    def scatter_copy(peer, slot):
+        return pltpu.make_async_remote_copy(
+            src_ref=part_ref.at[peer], dst_ref=held.at[slot], send_sem=scatter_send.at[peer],
+            recv_sem=scatter_recv.at[slot], device_id=(tok_index, peer), device_id_type=MESH,
+        )
+
+    def gather_copy(peer, slot):
+        return pltpu.make_async_remote_copy(
+            src_ref=mine, dst_ref=out_ref.at[slot], send_sem=gather_send.at[peer],
+            recv_sem=gather_recv.at[slot], device_id=(tok_index, peer), device_id_type=MESH,
+        )
+
+    for peer in peers:
+        scatter_copy(peer, me).start()
+
+    def norm_and_send():
+        total = part_ref[me].astype(jnp.float32)
+        for peer in peers:
+            scatter_copy(peer, peer).wait_recv()
+            total = total + held[peer].astype(jnp.float32)
+        summed = (resid_ref[...].astype(jnp.float32) + total).astype(jnp.bfloat16)
+        resid_out[...] = summed
+        as_float = summed.astype(jnp.float32)
+        center = jnp.mean(as_float, axis=-1, keepdims=True)
+        spread = jnp.mean(jnp.square(as_float - center), axis=-1, keepdims=True)
+        normed = ((as_float - center) * lax.rsqrt(spread + epsilon) * gain_ref[...]).astype(jnp.bfloat16)
+        mine[...] = normed
+        out_ref[me] = normed
+        for peer in peers:
+            gather_copy(peer, me).start()
+
+    _ring_gather(weight_ref, weight_out, send_right, send_left, send_partner, weight_recv, me,
+                 hook=norm_and_send, hook_step=3)
+    for peer in peers:
+        gather_copy(peer, peer).wait_recv()
+    for peer in peers:
+        scatter_copy(peer, me).wait_send()
+        gather_copy(peer, me).wait_send()
+
+
+def mix_ring_feat(parts, resid, gain, weight_block, n, tok_count, collective_id):
+    _, rows, width = parts.shape
+    weight_rows, weight_width = weight_block.shape
+    chips = tok_count // 2
+    new_resid, gathered, weights = pl.pallas_call(
+        functools.partial(_mix_ring_kernel, n),
+        out_shape=(
+            jax.ShapeDtypeStruct((rows, width), jnp.bfloat16),
+            jax.ShapeDtypeStruct((n, rows, width), jnp.bfloat16),
+            jax.ShapeDtypeStruct((tok_count, weight_rows, weight_width), weight_block.dtype),
+        ),
+        in_specs=[pl.BlockSpec(memory_space=pltpu.VMEM)] * 4,
+        out_specs=(pl.BlockSpec(memory_space=pltpu.VMEM),) * 3,
+        scratch_shapes=[
+            pltpu.VMEM((n, rows, width), parts.dtype),
+            pltpu.VMEM((rows, width), jnp.bfloat16),
+            pltpu.SemaphoreType.DMA((n,)),
+            pltpu.SemaphoreType.DMA((n,)),
+            pltpu.SemaphoreType.DMA((n,)),
+            pltpu.SemaphoreType.DMA((n,)),
+            pltpu.SemaphoreType.DMA((chips,)),
+            pltpu.SemaphoreType.DMA((chips,)),
+            pltpu.SemaphoreType.DMA((chips,)),
+            pltpu.SemaphoreType.DMA((tok_count,)),
+        ],
+        compiler_params=pltpu.CompilerParams(collective_id=collective_id, has_side_effects=True),
+    )(parts, resid, gain.astype(jnp.float32).reshape(1, width), weight_block)
+    return new_resid, gathered.reshape(n * rows, width), weights
 
 
 def _scatter_kernel(n, part_ref, out_ref, held, send_sem, recv_sem):
@@ -437,15 +531,17 @@
     local_count = tokens.shape[0]
     normed = layer_norm(tokens, gain_attend)
     stacked = jnp.concatenate([weight_up, weight_down.T], axis=1)
-    gathered, weights = first_exchange(normed, stacked, feat_count, tok_count, 0)
-    upper = weights[:, :, :units].reshape(tok_count * weight_up.shape[0], units)
-    lower_t = weights[:, :, units:].reshape(tok_count * weight_up.shape[0], units)
+    gathered = gather_feat(normed, feat_count, 0)
     projected = jnp.dot(gathered, flat_in, preferred_element_type=jnp.float32)
     attended = attend(projected, segment_ids, head_count)
     attn_parts = jnp.dot(attended, project_out, preferred_element_type=jnp.float32).astype(jnp.bfloat16)
-    second, hidden_rows = mix_feat(
-        attn_parts.reshape(feat_count, local_count, model_width), tokens, gain_hidden, feat_count, 1
+    second, hidden_rows, weights = mix_ring_feat(
+        attn_parts.reshape(feat_count, local_count, model_width), tokens, gain_hidden, stacked,
+        feat_count, tok_count, 1,
     )
+    both = weights.reshape(tok_count * weight_up.shape[0], 2 * units)
+    upper = both[:, :units]
+    lower_t = both[:, units:]
     hidden = jax.nn.gelu(
         jnp.dot(hidden_rows, upper, preferred_element_type=jnp.float32), approximate=False
     ).astype(jnp.bfloat16)

time: 182 us -> 168 us (0.923)
  Pallas kernels: 148 us -> 137 us
  local copies, waits for them, and re-layouts: 13.5 us -> 10.6 us
    pallas_call x2 -> x1, Pallas kernels: 72.4 us -> 39.5 us  [mix_feat(): pl.pallas_call(functools.partial(_mix_kernel, n), out_shape=(jax.ShapeDty...]
    pallas_call x1 -> x2, Pallas kernels: 50.7 us -> 75.8 us  [the longest x1 53.7 us: mix_ring_feat(): pl.pallas_call(functools.partial(_mix_ring_kernel, n), out_shape=(jax.Sha...]
    slice x1 -> x0, local copies, waits for them, and re-layouts: 3.25 us -> none  [body(): upper = weights[:, :, :units].reshape(tok_count * weight_up.shape[0], units)]
    pallas_call x1, Pallas kernels: 24.6 us -> 21.6 us  [route_exchange(): pl.pallas_call(functools.partial(_route_kernel, n), out_shape=jax.ShapeDt...]
where the time goes in v8:
time: 168 us; the launch traced here: 167 us
  Pallas kernels  137 us (82%)
  matrix products  13.4 us (8%)
  local copies, waits for them, and re-layouts  10.6 us (6%)
  other arithmetic  6.28 us (4%)
    pallas_call x1, Pallas kernels, mix_ring_feat(): pl.pallas_call(functools.partial(_mix_ring_kernel, n), out_shape=(jax.Sha...  53.7 us
    pallas_call x1, Pallas kernels, mix_feat(): pl.pallas_call(functools.partial(_mix_kernel, n), out_shape=(jax.ShapeDty...  39.5 us
    pallas_call x1, Pallas kernels, gather_feat(): pl.pallas_call(functools.partial(_gather_kernel, n), out_shape=jax.ShapeD...  22.2 us
    pallas_call x1, Pallas kernels, route_exchange(): pl.pallas_call(functools.partial(_route_kernel, n), out_shape=jax.ShapeDt...  21.6 us
    dot_general x1, matrix products, body(): lax.dot_general(hidden, lower_t, (((1,), (1,)), ((), ())), preferred_elem...  5.52 us
    reshape x1, local copies, waits for them, and re-layouts, body(): both = weights.reshape(tok_count * weight_up.shape[0], 2 * units)  4 us

profile of v8, /device:TPU:1, one launch (start us, length us, event | category | flops | bytes accessed | tf_op | source)
XLA Modules:
  0.0 167.3 jit_solution(7187031722600013165)
XLA Ops:
  0.0 1.2 convert_reduce_fusion
  1.2 1.1 fusion.56
  2.3 0.7 convert_element_type.68
  3.0 1.6 fusion.58.row_ref
  4.5 22.2 %shard_map.109 = bf16[16,24,1408]{2,1,0:T(8,128)(2,1)} custom-call(bf16[24,1408]{1,0:T(8,128)(2,1)} %fusion.58.row_ref), custom_call_target="tpu_custom_call" | custom-call | tf_op jit(solution)/shard_map/pallas_call | solution.py:42
  26.7 2.1 %fusion.96 = (bf16[384,3,1,88]{0,3,1,2:T(8,128)(2,1)S(1)}, f32[384,3,1,88]{0,3,1,2:T(8,128)S(1)}) fusion(bf16[384,1408,1]{1,0,2:T(8,128)(2,1)} %bitcast.49, bf16[1408,3,88]{0,2,1:T(8,128)(2,1)} %param.14), kind=kOutput, calls=%fused_computation.123 | convolution fusion | flops 285576192 | bytes 2433024 | tf_op jit(solution)/shard_map/dot_general | solution.py:535
  28.8 0.3 fusion.97
  29.1 0.4 copy-done.3
  29.5 0.7 fusion.19
  30.2 2.7 %convolution_convert_fusion.1 = bf16[384,1408]{1,0:T(8,128)(2,1)} fusion(bf16[88,1408]{1,0:T(8,128)(2,1)} %param.15, f32[384,384]{0,1:T(8,128)S(1)} %get-tuple-element.18, f32[384]{0:T(512)} %fusion.19, f32[384]{0:T(512)S(1)} %get-tuple-element.17, bf16[384,3,1,88]{0,3,1,2:T(8,128)(2,1)} %copy-done.3), kind=kOutput, calls=%fused_computation.1 | convolution fusion | flops 122127360 | bytes 1990144 | tf_op jit(solution)/shard_map/dot_general | solution.py:537
  32.9 0.6 pad_maximum_fusion.weight_ref
  33.5 1.3 reshape.125.gain_ref
  34.8 53.7 %shard_map.110 = (bf16[24,1408]{1,0:T(8,128)(2,1)}, bf16[16,24,1408]{2,1,0:T(8,128)(2,1)}, bf16[32,44,768]{2,1,0:T(8,128)(2,1)}) custom-call(bf16[16,24,1408]{2,1,0:T(8,128)(2,1)} %bitcast.47, bf16[24,1408]{1,0:T(8,128)(2,1)} %resid_ref.1, f32[1,1408]{1,0:T(1,128)} %reshape.125.gain_ref, bf16[44,768]{1,0:T(8,128)(2,1)} %pad_maximum_fusion.weight_ref), custom_call_target="tpu_custom_call" | custom-call | tf_op jit(solution)/shard_map/pallas_call | solution.py:361
  88.5 4.0 %reshape.118 = bf16[1408,768]{1,0:T(8,128)(2,1)} reshape(bf16[32,44,768]{2,1,0:T(8,128)(2,1)} %get-tuple-element.10) | data formatting | bytes 4325376 | tf_op jit(solution)/shard_map/reshape | solution.py:542
  92.5 5.5 %convolution_convert_fusion = bf16[384,1408]{1,0:T(8,128)(2,1)} fusion(bf16[1408,768]{1,0:T(8,128)(2,1)} %reshape.118, bf16[384,1408]{1,0:T(8,128)(2,1)} %bitcast.53), kind=kOutput, calls=%fused_computation | convolution fusion | flops 840597504 | bytes 4325376 | tf_op jit(solution)/shard_map/dot_general | solution.py:548
  98.0 0.6 reshape.127.gain_ref
  98.6 39.5 %shard_map.111 = (bf16[24,1408]{1,0:T(8,128)(2,1)}, bf16[16,24,1408]{2,1,0:T(8,128)(2,1)}) custom-call(bf16[16,24,1408]{2,1,0:T(8,128)(2,1)} %bitcast.48, bf16[24,1408]{1,0:T(8,128)(2,1)} %get-tuple-element.11.resid_ref, f32[1,1408]{1,0:T(1,128)} %reshape.127.gain_ref), custom_call_target="tpu_custom_call" | custom-call | tf_op jit(solution)/shard_map/pallas_call | solution.py:275
  138.1 2.6 %reshape_reshape.3 = bf16[96,5632]{1,0:T(8,128)(2,1)} reshape(bf16[16,24,1408]{2,1,0:T(8,128)(2,1)} %get-tuple-element.12) | data formatting | bytes 2162688 | tf_op jit(solution)/shard_map/reshape;reshape | solution.py:554
  140.7 0.1 reshape.109
  140.8 0.1 subtract_reduce_fusion
  140.9 0.2 convert_reduce_fusion.1
  141.2 2.8 %convolution_convert_fusion.2 = bf16[512,256]{1,0:T(8,128)(2,1)} fusion(bf16[96,5632]{1,0:T(8,128)(2,1)} %reshape_reshape.3, bf16[5632,256]{1,0:T(8,128)(2,1)S(1)} %copy-done, s32[96]{0:T(128)S(1)} %multiply_add_fusion), kind=kOutput, calls=%fused_computation.4 | convolution fusion | flops 302194688 | bytes 4227456 | tf_op jit(solution)/shard_map/dot_general | solution.py:506
  144.0 21.6 %shard_map.112 = bf16[32,16,256]{2,1,0:T(8,128)(2,1)} custom-call(bf16[32,16,256]{2,1,0:T(8,128)(2,1)} %bitcast.50), custom_call_target="tpu_custom_call" | custom-call | tf_op jit(solution)/shard_map/pallas_call | solution.py:221
  165.6 1.7 copy.13
  (17 shorter events, 0.1 us)
Async XLA Ops:
  0.0 141.2 %copy-start = (bf16[5632,256]{1,0:T(8,128)(2,1)S(1)}, bf16[5632,256]{1,0:T(8,128)(2,1)}, u32[]{:S(2)}) copy-start(bf16[5632,256]{1,0:T(8,128)(2,1)} %param.18) | copy-start | bytes 8650756
  26.7 2.1 %copy-start.4 = (s32[384]{0:T(512)S(1)}, s32[384]{0:T(512)}, u32[]{:S(2)}) copy-start(s32[384]{0:T(512)} %param.12) | copy-start | bytes 4612
  28.8 0.7 copy-start.3
  30.2 2.7 %copy-start.1 = (bf16[384,44]{0,1:T(8,128)(2,1)S(1)}, bf16[384,44]{0,1:T(8,128)(2,1)}, u32[]{:S(2)}) copy-start(bf16[384,44]{0,1:T(8,128)(2,1)} %param.17) | copy-start | bytes 101380
  30.2 2.7 %copy-start.2 = (bf16[44,384]{1,0:T(8,128)(2,1)S(1)}, bf16[44,384]{1,0:T(8,128)(2,1)}, u32[]{:S(2)}) copy-start(bf16[44,384]{1,0:T(8,128)(2,1)} %param.16) | copy-start | bytes 101380
  92.5 5.5 %copy-start.5 = (bf16[1408]{0:T(1024)(128)(2,1)S(1)}, bf16[1408]{0:T(1024)(128)(2,1)}, u32[]{:S(2)}) copy-start(bf16[1408]{0:T(1024)(128)(2,1)} %param.21) | copy-start | bytes 8452
  138.1 3.0 %copy-start.6 = (s32[32]{0:T(128)S(1)}, s32[32]{0:T(128)}, u32[]{:S(2)}) copy-start(s32[32]{0:T(128)} %param.13) | copy-start | bytes 388

commit v9 on v8

--- a/solution.py
+++ b/solution.py
@@ -228,7 +228,7 @@
     )(packed)
 
 
-def _mix_kernel(n, part_ref, resid_ref, gain_ref, resid_out, out_ref, held, mine,
+def _mix_kernel(n, gain_row, part_ref, resid_ref, gain_ref, resid_out, out_ref, held, mine,
                 scatter_send, scatter_recv, gather_send, gather_recv):
     me = lax.axis_index("feat")
     tok_index = lax.axis_index("tok")
@@ -258,7 +258,7 @@
     as_float = summed.astype(jnp.float32)
     center = jnp.mean(as_float, axis=-1, keepdims=True)
     spread = jnp.mean(jnp.square(as_float - center), axis=-1, keepdims=True)
-    normed = ((as_float - center) * lax.rsqrt(spread + epsilon) * gain_ref[...]).astype(jnp.bfloat16)
+    normed = ((as_float - center) * lax.rsqrt(spread + epsilon) * gain_ref[gain_row:gain_row + 1, :]).astype(jnp.bfloat16)
     mine[...] = normed
     out_ref[me] = normed
     for peer in peers:
@@ -270,10 +270,10 @@
         gather_copy(peer, me).wait_send()
 
 
-def mix_feat(parts, resid, gain, n, collective_id):
+def mix_feat(parts, resid, gains, gain_row, n, collective_id):
     _, rows, width = parts.shape
     new_resid, gathered = pl.pallas_call(
-        functools.partial(_mix_kernel, n),
+        functools.partial(_mix_kernel, n, gain_row),
         out_shape=(
             jax.ShapeDtypeStruct((rows, width), jnp.bfloat16),
             jax.ShapeDtypeStruct((n, rows, width), jnp.bfloat16),
@@ -289,11 +289,11 @@
             pltpu.SemaphoreType.DMA((n,)),
         ],
         compiler_params=pltpu.CompilerParams(collective_id=collective_id, has_side_effects=True),
-    )(parts, resid, gain.astype(jnp.float32).reshape(1, width))
+    )(parts, resid, gains)
     return new_resid, gathered.reshape(n * rows, width)
 
 
-def _mix_ring_kernel(n, part_ref, resid_ref, gain_ref, weight_ref, resid_out, out_ref, weight_out,
+def _mix_ring_kernel(n, gain_row, part_ref, resid_ref, gain_ref, weight_ref, resid_out, out_ref, weight_out,
                      held, mine, scatter_send, scatter_recv, gather_send, gather_recv,
                      send_right, send_left, send_partner, weight_recv):
     me = lax.axis_index("feat")
@@ -339,7 +339,7 @@
         as_float = summed.astype(jnp.float32)
         center = jnp.mean(as_float, axis=-1, keepdims=True)
         spread = jnp.mean(jnp.square(as_float - center), axis=-1, keepdims=True)
-        normed = ((as_float - center) * lax.rsqrt(spread + epsilon) * gain_ref[...]).astype(jnp.bfloat16)
+        normed = ((as_float - center) * lax.rsqrt(spread + epsilon) * gain_ref[gain_row:gain_row + 1, :]).astype(jnp.bfloat16)
         mine[...] = normed
         out_ref[me] = normed
         for peer in peers:
@@ -354,12 +354,12 @@
         gather_copy(peer, me).wait_send()
 
 
-def mix_ring_feat(parts, resid, gain, weight_block, n, tok_count, collective_id):
+def mix_ring_feat(parts, resid, gains, gain_row, weight_block, n, tok_count, collective_id):
     _, rows, width = parts.shape
     weight_rows, weight_width = weight_block.shape
     chips = tok_count // 2
     new_resid, gathered, weights = pl.pallas_call(
-        functools.partial(_mix_ring_kernel, n),
+        functools.partial(_mix_ring_kernel, n, gain_row),
         out_shape=(
             jax.ShapeDtypeStruct((rows, width), jnp.bfloat16),
             jax.ShapeDtypeStruct((n, rows, width), jnp.bfloat16),
@@ -380,8 +380,50 @@
             pltpu.SemaphoreType.DMA((tok_count,)),
         ],
         compiler_params=pltpu.CompilerParams(collective_id=collective_id, has_side_effects=True),
-    )(parts, resid, gain.astype(jnp.float32).reshape(1, width), weight_block)
+    )(parts, resid, gains, weight_block)
     return new_resid, gathered.reshape(n * rows, width), weights
+
+
+def _norm_gather_kernel(n, gain_row, tok_ref, gain_ref, out_ref, mine, send_sem, recv_sem):
+    me = lax.axis_index("feat")
+    tok_index = lax.axis_index("tok")
+    peers = [lax.rem(me + d, n) for d in range(1, n)]
+    _greet(peers, tok_index)
+    as_float = tok_ref[...].astype(jnp.float32)
+    center = jnp.mean(as_float, axis=-1, keepdims=True)
+    spread = jnp.mean(jnp.square(as_float - center), axis=-1, keepdims=True)
+    normed = ((as_float - center) * lax.rsqrt(spread + epsilon) * gain_ref[gain_row:gain_row + 1, :]).astype(jnp.bfloat16)
+    mine[...] = normed
+    out_ref[me] = normed
+
+    def copy(peer, slot):
+        return pltpu.make_async_remote_copy(
+            src_ref=mine, dst_ref=out_ref.at[slot], send_sem=send_sem.at[peer],
+            recv_sem=recv_sem.at[slot], device_id=(tok_index, peer), device_id_type=MESH,
+        )
+
+    for peer in peers:
+        copy(peer, me).start()
+    for peer in peers:
+        copy(peer, peer).wait_recv()
+    for peer in peers:
+        copy(peer, me).wait_send()
+
+
+def norm_gather_feat(rows, gains, gain_row, n, collective_id):
+    count, width = rows.shape
+    return pl.pallas_call(
+        functools.partial(_norm_gather_kernel, n, gain_row),
+        out_shape=jax.ShapeDtypeStruct((n, count, width), jnp.bfloat16),
+        in_specs=[pl.BlockSpec(memory_space=pltpu.VMEM)] * 2,
+        out_specs=pl.BlockSpec(memory_space=pltpu.VMEM),
+        scratch_shapes=[
+            pltpu.VMEM((count, width), jnp.bfloat16),
+            pltpu.SemaphoreType.DMA((n,)),
+            pltpu.SemaphoreType.DMA((n,)),
+        ],
+        compiler_params=pltpu.CompilerParams(collective_id=collective_id, has_side_effects=True),
+    )(rows, gains).reshape(n * count, width)
 
 
 def _scatter_kernel(n, part_ref, out_ref, held, send_sem, recv_sem):
@@ -529,14 +571,14 @@
     tok_count = lax.axis_size("tok")
     flat_in = project_in.reshape(model_width, 3 * project_in.shape[2])
     local_count = tokens.shape[0]
-    normed = layer_norm(tokens, gain_attend)
+    gains = jnp.stack([gain_attend, gain_hidden, gain_final]).astype(jnp.float32)
     stacked = jnp.concatenate([weight_up, weight_down.T], axis=1)
-    gathered = gather_feat(normed, feat_count, 0)
+    gathered = norm_gather_feat(tokens, gains, 0, feat_count, 0)
     projected = jnp.dot(gathered, flat_in, preferred_element_type=jnp.float32)
     attended = attend(projected, segment_ids, head_count)
     attn_parts = jnp.dot(attended, project_out, preferred_element_type=jnp.float32).astype(jnp.bfloat16)
     second, hidden_rows, weights = mix_ring_feat(
-        attn_parts.reshape(feat_count, local_count, model_width), tokens, gain_hidden, stacked,
+        attn_parts.reshape(feat_count, local_count, model_width), tokens, gains, 1, stacked,
         feat_count, tok_count, 1,
     )
     both = weights.reshape(tok_count * weight_up.shape[0], 2 * units)
@@ -549,7 +591,7 @@
         hidden, lower_t, (((1,), (1,)), ((), ())), preferred_element_type=jnp.float32
     ).astype(jnp.bfloat16)
     _, final_rows = mix_feat(
-        down_parts.reshape(feat_count, local_count, model_width), second, gain_final, feat_count, 3
+        down_parts.reshape(feat_count, local_count, model_width), second, gains, 2, feat_count, 3
     )
     merged = final_rows.reshape(final_rows.shape[0] // 4, 4 * model_width)
     embedded = jnp.dot(merged, weight_merge, preferred_element_type=jnp.float32).astype(jnp.bfloat16)

time: 168 us -> 165 us (0.982)
  other arithmetic: 6.28 us -> 2.38 us
    another operation x0 -> x3, local copies, waits for them, and re-layouts: none -> 2.26 us  [body(): jnp.stack([gain_attend, gain_hidden, gain_final]).astype(jnp.float32)]
    reduce_sum x2 -> x0, other arithmetic: 2.23 us -> none  [the longest x1 1.15 us: layer_norm(): center = jnp.mean(as_float, axis=-1, keepdims=True)]
    reshape x2 -> x0, local copies, waits for them, and re-layouts: 1.88 us -> none  [the longest x1 1.28 us: mix_ring_feat(): gain.astype(jnp.float32).reshape(1, width)]
where the time goes in v9:
time: 165 us; the launch traced here: 164 us
  Pallas kernels  137 us (83%)
  matrix products  13.4 us (8%)
  local copies, waits for them, and re-layouts  11 us (7%)
  other arithmetic  2.38 us (1%)
    pallas_call x1, Pallas kernels, mix_ring_feat(): pl.pallas_call(functools.partial(_mix_ring_kernel, n, gain_row), out_shap...  53.6 us
    pallas_call x1, Pallas kernels, mix_feat(): pl.pallas_call(functools.partial(_mix_kernel, n, gain_row), out_shape=(ja...  39.5 us
    pallas_call x1, Pallas kernels, norm_gather_feat(): pl.pallas_call(functools.partial(_norm_gather_kernel, n, gain_row), out_s...  22.4 us
    pallas_call x1, Pallas kernels, route_exchange(): pl.pallas_call(functools.partial(_route_kernel, n), out_shape=jax.ShapeDt...  21.6 us
    dot_general x1, matrix products, body(): lax.dot_general(hidden, lower_t, (((1,), (1,)), ((), ())), preferred_elem...  5.51 us
    reshape x1, local copies, waits for them, and re-layouts, body(): both = weights.reshape(tok_count * weight_up.shape[0], 2 * units)  4 us

profile of v9, /device:TPU:1, one launch (start us, length us, event | category | flops | bytes accessed | tf_op | source)
XLA Modules:
  0.0 163.9 jit_solution(3513140908982574470)
XLA Ops:
  0.0 0.8 stack.12
  0.8 0.7 stack.13
  1.6 0.7 stack.14
  2.3 0.6 maximum_convert_fusion.gain_ref
  2.9 22.4 %shard_map.109 = bf16[16,24,1408]{2,1,0:T(8,128)(2,1)} custom-call(bf16[24,1408]{1,0:T(8,128)(2,1)} %resid_ref.1, f32[3,1408]{1,0:T(4,128)} %maximum_convert_fusion.gain_ref), custom_call_target="tpu_custom_call" | custom-call | tf_op jit(solution)/shard_map/pallas_call | solution.py:415
  25.3 0.0 copy-start.4
  25.3 2.1 %fusion.91 = (bf16[384,3,1,88]{0,3,1,2:T(8,128)(2,1)S(1)}, f32[384,3,1,88]{0,3,1,2:T(8,128)S(1)}) fusion(bf16[384,1408,1]{1,0,2:T(8,128)(2,1)} %bitcast.49, bf16[1408,3,88]{0,2,1:T(8,128)(2,1)} %param.14), kind=kOutput, calls=%fused_computation.115 | convolution fusion | flops 285576192 | bytes 2433024 | tf_op jit(solution)/shard_map/dot_general | solution.py:577
  27.4 0.3 fusion.92
  27.7 0.4 copy-done.3
  28.1 0.7 fusion.19
  28.8 2.7 %convolution_convert_fusion.1 = bf16[384,1408]{1,0:T(8,128)(2,1)} fusion(bf16[88,1408]{1,0:T(8,128)(2,1)} %param.15, f32[384,384]{0,1:T(8,128)S(1)} %get-tuple-element.18, f32[384]{0:T(512)} %fusion.19, f32[384]{0:T(512)S(1)} %get-tuple-element.17, bf16[384,3,1,88]{0,3,1,2:T(8,128)(2,1)} %copy-done.3), kind=kOutput, calls=%fused_computation.1 | convolution fusion | flops 122127360 | bytes 1990144 | tf_op jit(solution)/shard_map/dot_general | solution.py:579
  31.5 0.6 pad_maximum_fusion.weight_ref
  32.1 53.6 %shard_map.110 = (bf16[24,1408]{1,0:T(8,128)(2,1)}, bf16[16,24,1408]{2,1,0:T(8,128)(2,1)}, bf16[32,44,768]{2,1,0:T(8,128)(2,1)}) custom-call(bf16[16,24,1408]{2,1,0:T(8,128)(2,1)} %bitcast.47, bf16[24,1408]{1,0:T(8,128)(2,1)} %resid_ref.1, f32[3,1408]{1,0:T(4,128)} %maximum_convert_fusion.gain_ref, bf16[44,768]{1,0:T(8,128)(2,1)} %pad_maximum_fusion.weight_ref), custom_call_target="tpu_custom_call" | custom-call | tf_op jit(solution)/shard_map/pallas_call | solution.py:361
  85.7 4.0 %reshape.93 = bf16[1408,768]{1,0:T(8,128)(2,1)} reshape(bf16[32,44,768]{2,1,0:T(8,128)(2,1)} %get-tuple-element.10) | data formatting | bytes 4325376 | tf_op jit(solution)/shard_map/reshape | solution.py:584
  89.7 5.5 %convolution_convert_fusion = bf16[384,1408]{1,0:T(8,128)(2,1)} fusion(bf16[1408,768]{1,0:T(8,128)(2,1)} %reshape.93, bf16[384,1408]{1,0:T(8,128)(2,1)} %bitcast.53), kind=kOutput, calls=%fused_computation | convolution fusion | flops 840597504 | bytes 4325376 | tf_op jit(solution)/shard_map/dot_general | solution.py:590
  95.2 39.5 %shard_map.111 = (bf16[24,1408]{1,0:T(8,128)(2,1)}, bf16[16,24,1408]{2,1,0:T(8,128)(2,1)}) custom-call(bf16[16,24,1408]{2,1,0:T(8,128)(2,1)} %bitcast.48, bf16[24,1408]{1,0:T(8,128)(2,1)} %get-tuple-element.11.resid_ref, f32[3,1408]{1,0:T(4,128)} %maximum_convert_fusion.gain_ref), custom_call_target="tpu_custom_call" | custom-call | tf_op jit(solution)/shard_map/pallas_call | solution.py:275
  134.7 2.6 %reshape_reshape.3 = bf16[96,5632]{1,0:T(8,128)(2,1)} reshape(bf16[16,24,1408]{2,1,0:T(8,128)(2,1)} %get-tuple-element.12) | data formatting | bytes 2162688 | tf_op jit(solution)/shard_map/reshape;reshape | solution.py:596
  137.3 0.1 reshape.86
  137.4 0.1 subtract_reduce_fusion
  137.6 0.2 convert_reduce_fusion
  137.7 0.1 select_reduce_fusion
  137.9 2.8 %convolution_convert_fusion.2 = bf16[512,256]{1,0:T(8,128)(2,1)} fusion(bf16[96,5632]{1,0:T(8,128)(2,1)} %reshape_reshape.3, bf16[5632,256]{1,0:T(8,128)(2,1)S(1)} %copy-done, s32[96]{0:T(128)S(1)} %multiply_add_fusion), kind=kOutput, calls=%fused_computation.4 | convolution fusion | flops 302194688 | bytes 4227456 | tf_op jit(solution)/shard_map/dot_general | solution.py:548
  140.7 21.6 %shard_map.112 = bf16[32,16,256]{2,1,0:T(8,128)(2,1)} custom-call(bf16[32,16,256]{2,1,0:T(8,128)(2,1)} %bitcast.50), custom_call_target="tpu_custom_call" | custom-call | tf_op jit(solution)/shard_map/pallas_call | solution.py:221
  162.3 1.7 %copy.13 = bf16[512,256]{1,0:T(8,128)(2,1)} copy(bf16[512,256]{1,0:T(8,128)(2,1)} %bitcast.51) | data formatting | bytes 524288
  (11 shorter events, 0.0 us)
Async XLA Ops:
  0.0 137.8 %copy-start = (bf16[5632,256]{1,0:T(8,128)(2,1)S(1)}, bf16[5632,256]{1,0:T(8,128)(2,1)}, u32[]{:S(2)}) copy-start(bf16[5632,256]{1,0:T(8,128)(2,1)} %param.18) | copy-start | bytes 8650756
  25.3 2.1 %copy-start.4 = (s32[384]{0:T(512)S(1)}, s32[384]{0:T(512)}, u32[]{:S(2)}) copy-start(s32[384]{0:T(512)} %param.12) | copy-start | bytes 4612
  27.4 0.7 copy-start.3
  28.8 2.7 %copy-start.1 = (bf16[384,44]{0,1:T(8,128)(2,1)S(1)}, bf16[384,44]{0,1:T(8,128)(2,1)}, u32[]{:S(2)}) copy-start(bf16[384,44]{0,1:T(8,128)(2,1)} %param.17) | copy-start | bytes 101380
  28.8 2.7 %copy-start.2 = (bf16[44,384]{1,0:T(8,128)(2,1)S(1)}, bf16[44,384]{1,0:T(8,128)(2,1)}, u32[]{:S(2)}) copy-start(bf16[44,384]{1,0:T(8,128)(2,1)} %param.16) | copy-start | bytes 101380
  134.7 3.0 %copy-start.5 = (s32[32]{0:T(128)S(1)}, s32[32]{0:T(128)}, u32[]{:S(2)}) copy-start(s32[32]{0:T(128)} %param.13) | copy-start | bytes 388

commit v10 on v9

--- a/solution.py
+++ b/solution.py
@@ -293,8 +293,8 @@
     return new_resid, gathered.reshape(n * rows, width)
 
 
-def _mix_ring_kernel(n, gain_row, part_ref, resid_ref, gain_ref, weight_ref, resid_out, out_ref, weight_out,
-                     held, mine, scatter_send, scatter_recv, gather_send, gather_recv,
+def _mix_ring_kernel(n, gain_row, part_ref, resid_ref, gain_ref, weight_ref, resid_out, out_ref, weight_flat,
+                     weight_out, held, mine, scatter_send, scatter_recv, gather_send, gather_recv,
                      send_right, send_left, send_partner, weight_recv):
     me = lax.axis_index("feat")
     tok_index = lax.axis_index("tok")
@@ -347,6 +347,9 @@
 
     _ring_gather(weight_ref, weight_out, send_right, send_left, send_partner, weight_recv, me,
                  hook=norm_and_send, hook_step=3)
+    block_rows = weight_out.shape[1]
+    for slot in range(weight_out.shape[0]):
+        weight_flat[slot * block_rows:(slot + 1) * block_rows, :] = weight_out[slot]
     for peer in peers:
         gather_copy(peer, peer).wait_recv()
     for peer in peers:
@@ -363,11 +366,12 @@
         out_shape=(
             jax.ShapeDtypeStruct((rows, width), jnp.bfloat16),
             jax.ShapeDtypeStruct((n, rows, width), jnp.bfloat16),
-            jax.ShapeDtypeStruct((tok_count, weight_rows, weight_width), weight_block.dtype),
+            jax.ShapeDtypeStruct((tok_count * weight_rows, weight_width), weight_block.dtype),
         ),
         in_specs=[pl.BlockSpec(memory_space=pltpu.VMEM)] * 4,
         out_specs=(pl.BlockSpec(memory_space=pltpu.VMEM),) * 3,
         scratch_shapes=[
+            pltpu.VMEM((tok_count, weight_rows, weight_width), weight_block.dtype),
             pltpu.VMEM((n, rows, width), parts.dtype),
             pltpu.VMEM((rows, width), jnp.bfloat16),
             pltpu.SemaphoreType.DMA((n,)),
@@ -581,7 +585,7 @@
         attn_parts.reshape(feat_count, local_count, model_width), tokens, gains, 1, stacked,
         feat_count, tok_count, 1,
     )
-    both = weights.reshape(tok_count * weight_up.shape[0], 2 * units)
+    both = weights
     upper = both[:, :units]
     lower_t = both[:, units:]
     hidden = jax.nn.gelu(

time: 165 us -> 160 us (0.970)
  local copies, waits for them, and re-layouts: 11 us -> 7 us
    reshape x1 -> x0, local copies, waits for them, and re-layouts: 4 us -> none  [body(): both = weights.reshape(tok_count * weight_up.shape[0], 2 * units)]
where the time goes in v10:
time: 160 us
  Pallas kernels  137 us (86%)
  matrix products  13.4 us (8%)
  local copies, waits for them, and re-layouts  7 us (4%)
  other arithmetic  2.36 us (1%)
    pallas_call x1, Pallas kernels, mix_ring_feat(): pl.pallas_call(functools.partial(_mix_ring_kernel, n, gain_row), out_shap...  53.8 us
    pallas_call x1, Pallas kernels, mix_feat(): pl.pallas_call(functools.partial(_mix_kernel, n, gain_row), out_shape=(ja...  38.9 us
    pallas_call x1, Pallas kernels, norm_gather_feat(): pl.pallas_call(functools.partial(_norm_gather_kernel, n, gain_row), out_s...  22.4 us
    pallas_call x1, Pallas kernels, route_exchange(): pl.pallas_call(functools.partial(_route_kernel, n), out_shape=jax.ShapeDt...  22 us
    dot_general x1, matrix products, body(): lax.dot_general(hidden, lower_t, (((1,), (1,)), ((), ())), preferred_elem...  5.52 us

profile of v10, /device:TPU:1, one launch (start us, length us, event | category | flops | bytes accessed | tf_op | source)
XLA Modules:
  0.0 159.9 jit_solution(2287964966661987824)
XLA Ops:
  0.0 0.8 stack.12
  0.8 0.7 stack.13
  1.6 0.7 stack.14
  2.3 0.6 maximum_convert_fusion.gain_ref
  2.9 22.4 %shard_map.109 = bf16[16,24,1408]{2,1,0:T(8,128)(2,1)} custom-call(bf16[24,1408]{1,0:T(8,128)(2,1)} %resid_ref.1, f32[3,1408]{1,0:T(4,128)} %maximum_convert_fusion.gain_ref), custom_call_target="tpu_custom_call" | custom-call | tf_op jit(solution)/shard_map/pallas_call | solution.py:419
  25.3 0.0 copy-start.4
  25.3 2.1 %fusion.91 = (bf16[384,3,1,88]{0,3,1,2:T(8,128)(2,1)S(1)}, f32[384,3,1,88]{0,3,1,2:T(8,128)S(1)}) fusion(bf16[384,1408,1]{1,0,2:T(8,128)(2,1)} %bitcast.49, bf16[1408,3,88]{0,2,1:T(8,128)(2,1)} %param.14), kind=kOutput, calls=%fused_computation.115 | convolution fusion | flops 285576192 | bytes 2433024 | tf_op jit(solution)/shard_map/dot_general | solution.py:581
  27.4 0.0 copy-start.3
  27.4 0.3 fusion.92
  27.7 0.4 copy-done.3
  28.1 0.7 fusion.19
  28.8 2.7 %convolution_convert_fusion.1 = bf16[384,1408]{1,0:T(8,128)(2,1)} fusion(bf16[88,1408]{1,0:T(8,128)(2,1)} %param.15, f32[384,384]{0,1:T(8,128)S(1)} %get-tuple-element.18, f32[384]{0:T(512)} %fusion.19, f32[384]{0:T(512)S(1)} %get-tuple-element.17, bf16[384,3,1,88]{0,3,1,2:T(8,128)(2,1)} %copy-done.3), kind=kOutput, calls=%fused_computation.1 | convolution fusion | flops 122127360 | bytes 1990144 | tf_op jit(solution)/shard_map/dot_general | solution.py:583
  31.5 0.6 pad_maximum_fusion.weight_ref
  32.1 53.8 %shard_map.110 = (bf16[24,1408]{1,0:T(8,128)(2,1)}, bf16[16,24,1408]{2,1,0:T(8,128)(2,1)}, bf16[1408,768]{1,0:T(8,128)(2,1)}) custom-call(bf16[16,24,1408]{2,1,0:T(8,128)(2,1)} %bitcast.47, bf16[24,1408]{1,0:T(8,128)(2,1)} %resid_ref.1, f32[3,1408]{1,0:T(4,128)} %maximum_convert_fusion.gain_ref, bf16[44,768]{1,0:T(8,128)(2,1)} %pad_maximum_fusion.weight_ref), custom_call_target="tpu_custom_call" | custom-call | tf_op jit(solution)/shard_map/pallas_call | solution.py:364
  85.9 5.5 %convolution_convert_fusion = bf16[384,1408]{1,0:T(8,128)(2,1)} fusion(bf16[1408,768]{1,0:T(8,128)(2,1)} %get-tuple-element.10, bf16[384,1408]{1,0:T(8,128)(2,1)} %bitcast.53), kind=kOutput, calls=%fused_computation | convolution fusion | flops 840597504 | bytes 4325376 | tf_op jit(solution)/shard_map/dot_general | solution.py:594
  91.4 38.9 %shard_map.111 = (bf16[24,1408]{1,0:T(8,128)(2,1)}, bf16[16,24,1408]{2,1,0:T(8,128)(2,1)}) custom-call(bf16[16,24,1408]{2,1,0:T(8,128)(2,1)} %bitcast.48, bf16[24,1408]{1,0:T(8,128)(2,1)} %get-tuple-element.11.resid_ref, f32[3,1408]{1,0:T(4,128)} %maximum_convert_fusion.gain_ref), custom_call_target="tpu_custom_call" | custom-call | tf_op jit(solution)/shard_map/pallas_call | solution.py:275
  130.3 2.6 %reshape_reshape.3 = bf16[96,5632]{1,0:T(8,128)(2,1)} reshape(bf16[16,24,1408]{2,1,0:T(8,128)(2,1)} %get-tuple-element.12) | data formatting | bytes 2162688 | tf_op jit(solution)/shard_map/reshape;reshape | solution.py:600
  132.9 0.1 reshape.83
  133.0 0.1 subtract_reduce_fusion
  133.1 0.2 convert_reduce_fusion
  133.3 0.1 select_reduce_fusion
  133.4 2.8 %convolution_convert_fusion.2 = bf16[512,256]{1,0:T(8,128)(2,1)} fusion(bf16[96,5632]{1,0:T(8,128)(2,1)} %reshape_reshape.3, bf16[5632,256]{1,0:T(8,128)(2,1)S(1)} %copy-done, s32[96]{0:T(128)S(1)} %multiply_add_fusion), kind=kOutput, calls=%fused_computation.4 | convolution fusion | flops 302194688 | bytes 4227456 | tf_op jit(solution)/shard_map/dot_general | solution.py:552
  136.2 22.0 %shard_map.112 = bf16[32,16,256]{2,1,0:T(8,128)(2,1)} custom-call(bf16[32,16,256]{2,1,0:T(8,128)(2,1)} %bitcast.50), custom_call_target="tpu_custom_call" | custom-call | tf_op jit(solution)/shard_map/pallas_call | solution.py:221
  158.3 1.7 %copy.13 = bf16[512,256]{1,0:T(8,128)(2,1)} copy(bf16[512,256]{1,0:T(8,128)(2,1)} %bitcast.51) | data formatting | bytes 524288
  (10 shorter events, 0.0 us)
Async XLA Ops:
  0.0 133.4 %copy-start = (bf16[5632,256]{1,0:T(8,128)(2,1)S(1)}, bf16[5632,256]{1,0:T(8,128)(2,1)}, u32[]{:S(2)}) copy-start(bf16[5632,256]{1,0:T(8,128)(2,1)} %param.18) | copy-start | bytes 8650756
  25.3 2.1 %copy-start.4 = (s32[384]{0:T(512)S(1)}, s32[384]{0:T(512)}, u32[]{:S(2)}) copy-start(s32[384]{0:T(512)} %param.12) | copy-start | bytes 4612
  27.4 0.7 copy-start.3
  28.8 2.7 %copy-start.1 = (bf16[384,44]{0,1:T(8,128)(2,1)S(1)}, bf16[384,44]{0,1:T(8,128)(2,1)}, u32[]{:S(2)}) copy-start(bf16[384,44]{0,1:T(8,128)(2,1)} %param.17) | copy-start | bytes 101380
  28.8 2.7 %copy-start.2 = (bf16[44,384]{1,0:T(8,128)(2,1)S(1)}, bf16[44,384]{1,0:T(8,128)(2,1)}, u32[]{:S(2)}) copy-start(bf16[44,384]{1,0:T(8,128)(2,1)} %param.16) | copy-start | bytes 101380
  130.3 3.0 %copy-start.5 = (s32[32]{0:T(128)S(1)}, s32[32]{0:T(128)}, u32[]{:S(2)}) copy-start(s32[32]{0:T(128)} %param.13) | copy-start | bytes 388

commit v11 on v10

--- a/solution.py
+++ b/solution.py
@@ -228,7 +228,7 @@
     )(packed)
 
 
-def _mix_kernel(n, gain_row, part_ref, resid_ref, gain_ref, resid_out, out_ref, held, mine,
+def _mix_kernel(n, gain_row, part_ref, resid_ref, gain_ref, resid_out, out_ref, merged_out, held, mine,
                 scatter_send, scatter_recv, gather_send, gather_recv):
     me = lax.axis_index("feat")
     tok_index = lax.axis_index("tok")
@@ -265,6 +265,17 @@
         gather_copy(peer, me).start()
     for peer in peers:
         gather_copy(peer, peer).wait_recv()
+    group = 4
+    width = out_ref.shape[2]
+    row_count = n * out_ref.shape[1]
+    rows = out_ref[...].astype(jnp.float32).reshape(row_count, width).astype(jnp.bfloat16)
+    merged_index = lax.broadcasted_iota(jnp.int32, (row_count // group, row_count), 0)
+    row_index = lax.broadcasted_iota(jnp.int32, (row_count // group, row_count), 1)
+    for part in range(group):
+        pick = (row_index == merged_index * group + part).astype(jnp.bfloat16)
+        merged_out[:, part * width:(part + 1) * width] = jnp.dot(
+            pick, rows, preferred_element_type=jnp.float32
+        ).astype(jnp.bfloat16)
     for peer in peers:
         scatter_copy(peer, me).wait_send()
         gather_copy(peer, me).wait_send()
@@ -272,14 +283,15 @@
 
 def mix_feat(parts, resid, gains, gain_row, n, collective_id):
     _, rows, width = parts.shape
-    new_resid, gathered = pl.pallas_call(
+    new_resid, _, merged = pl.pallas_call(
         functools.partial(_mix_kernel, n, gain_row),
         out_shape=(
             jax.ShapeDtypeStruct((rows, width), jnp.bfloat16),
             jax.ShapeDtypeStruct((n, rows, width), jnp.bfloat16),
+            jax.ShapeDtypeStruct((n * rows // 4, 4 * width), jnp.bfloat16),
         ),
         in_specs=[pl.BlockSpec(memory_space=pltpu.VMEM)] * 3,
-        out_specs=(pl.BlockSpec(memory_space=pltpu.VMEM),) * 2,
+        out_specs=(pl.BlockSpec(memory_space=pltpu.VMEM),) * 3,
         scratch_shapes=[
             pltpu.VMEM((n, rows, width), parts.dtype),
             pltpu.VMEM((rows, width), jnp.bfloat16),
@@ -290,7 +302,7 @@
         ],
         compiler_params=pltpu.CompilerParams(collective_id=collective_id, has_side_effects=True),
     )(parts, resid, gains)
-    return new_resid, gathered.reshape(n * rows, width)
+    return new_resid, merged
 
 
 def _mix_ring_kernel(n, gain_row, part_ref, resid_ref, gain_ref, weight_ref, resid_out, out_ref, weight_flat,
@@ -594,10 +606,9 @@
     down_parts = lax.dot_general(
         hidden, lower_t, (((1,), (1,)), ((), ())), preferred_element_type=jnp.float32
     ).astype(jnp.bfloat16)
-    _, final_rows = mix_feat(
+    _, merged = mix_feat(
         down_parts.reshape(feat_count, local_count, model_width), second, gains, 2, feat_count, 3
     )
-    merged = final_rows.reshape(final_rows.shape[0] // 4, 4 * model_width)
     embedded = jnp.dot(merged, weight_merge, preferred_element_type=jnp.float32).astype(jnp.bfloat16)
     return route_rows(embedded, segment_ids, owners)
 

time: 160 us -> 159 us (level)
  local copies, waits for them, and re-layouts: 7 us -> 4.42 us
  Pallas kernels: 137 us -> 139 us
    another operation x1 -> x0, local copies, waits for them, and re-layouts: 2.58 us -> none  [body(): merged = final_rows.reshape(final_rows.shape[0] // 4, 4 * model_width)]
    pallas_call x1, Pallas kernels: 38.9 us -> 40.8 us  [mix_feat(): pl.pallas_call(functools.partial(_mix_kernel, n, gain_row), out_shape=(ja...]
where the time goes in v11:
time: 159 us
  Pallas kernels  139 us (87%)
  matrix products  13.4 us (8%)
  local copies, waits for them, and re-layouts  4.42 us (3%)
  other arithmetic  2.36 us (1%)
    pallas_call x1, Pallas kernels, mix_ring_feat(): pl.pallas_call(functools.partial(_mix_ring_kernel, n, gain_row), out_shap...  53.7 us
    pallas_call x1, Pallas kernels, mix_feat(): pl.pallas_call(functools.partial(_mix_kernel, n, gain_row), out_shape=(ja...  40.8 us
    pallas_call x1, Pallas kernels, norm_gather_feat(): pl.pallas_call(functools.partial(_norm_gather_kernel, n, gain_row), out_s...  22.4 us
    pallas_call x1, Pallas kernels, route_exchange(): pl.pallas_call(functools.partial(_route_kernel, n), out_shape=jax.ShapeDt...  21.6 us
    dot_general x1, matrix products, body(): lax.dot_general(hidden, lower_t, (((1,), (1,)), ((), ())), preferred_elem...  5.52 us

profile of v11, /device:TPU:1, one launch (start us, length us, event | category | flops | bytes accessed | tf_op | source)
XLA Modules:
  0.0 158.8 jit_solution(468490150220507005)
XLA Ops:
  0.0 0.8 stack.12
  0.8 0.7 stack.13
  1.6 0.7 stack.14
  2.3 0.6 maximum_convert_fusion.gain_ref
  2.9 22.4 %shard_map.109 = bf16[16,24,1408]{2,1,0:T(8,128)(2,1)} custom-call(bf16[24,1408]{1,0:T(8,128)(2,1)} %resid_ref.1, f32[3,1408]{1,0:T(4,128)} %maximum_convert_fusion.gain_ref), custom_call_target="tpu_custom_call" | custom-call | tf_op jit(solution)/shard_map/pallas_call | solution.py:431
  25.3 0.0 copy-start.4
  25.3 2.1 %fusion.91 = (bf16[384,3,1,88]{0,3,1,2:T(8,128)(2,1)S(1)}, f32[384,3,1,88]{0,3,1,2:T(8,128)S(1)}) fusion(bf16[384,1408,1]{1,0,2:T(8,128)(2,1)} %bitcast.49, bf16[1408,3,88]{0,2,1:T(8,128)(2,1)} %param.14), kind=kOutput, calls=%fused_computation.115 | convolution fusion | flops 285576192 | bytes 2433024 | tf_op jit(solution)/shard_map/dot_general | solution.py:593
  27.4 0.0 copy-start.3
  27.4 0.0 copy-done.4
  27.4 0.3 fusion.92
  27.7 0.4 copy-done.3
  28.1 0.7 fusion.19
  28.8 2.7 %convolution_convert_fusion.1 = bf16[384,1408]{1,0:T(8,128)(2,1)} fusion(bf16[88,1408]{1,0:T(8,128)(2,1)} %param.15, f32[384,384]{0,1:T(8,128)S(1)} %get-tuple-element.18, f32[384]{0:T(512)} %fusion.19, f32[384]{0:T(512)S(1)} %get-tuple-element.17, bf16[384,3,1,88]{0,3,1,2:T(8,128)(2,1)} %copy-done.3), kind=kOutput, calls=%fused_computation.1 | convolution fusion | flops 122127360 | bytes 1990144 | tf_op jit(solution)/shard_map/dot_general | solution.py:595
  31.5 0.6 pad_maximum_fusion.weight_ref
  32.1 53.7 %shard_map.110 = (bf16[24,1408]{1,0:T(8,128)(2,1)}, bf16[16,24,1408]{2,1,0:T(8,128)(2,1)}, bf16[1408,768]{1,0:T(8,128)(2,1)}) custom-call(bf16[16,24,1408]{2,1,0:T(8,128)(2,1)} %bitcast.47, bf16[24,1408]{1,0:T(8,128)(2,1)} %resid_ref.1, f32[3,1408]{1,0:T(4,128)} %maximum_convert_fusion.gain_ref, bf16[44,768]{1,0:T(8,128)(2,1)} %pad_maximum_fusion.weight_ref), custom_call_target="tpu_custom_call" | custom-call | tf_op jit(solution)/shard_map/pallas_call | solution.py:376
  85.9 5.5 %convolution_convert_fusion = bf16[384,1408]{1,0:T(8,128)(2,1)} fusion(bf16[1408,768]{1,0:T(8,128)(2,1)} %get-tuple-element.10, bf16[384,1408]{1,0:T(8,128)(2,1)} %bitcast.53), kind=kOutput, calls=%fused_computation | convolution fusion | flops 840597504 | bytes 4325376 | tf_op jit(solution)/shard_map/dot_general | solution.py:606
  91.4 40.8 %shard_map.111 = (bf16[24,1408]{1,0:T(8,128)(2,1)}, bf16[16,24,1408]{2,1,0:T(8,128)(2,1)}, bf16[96,5632]{1,0:T(8,128)(2,1)}) custom-call(bf16[16,24,1408]{2,1,0:T(8,128)(2,1)} %bitcast.48, bf16[24,1408]{1,0:T(8,128)(2,1)} %get-tuple-element.11.resid_ref, f32[3,1408]{1,0:T(4,128)} %maximum_convert_fusion.gain_ref), custom_call_target="tpu_custom_call" | custom-call | tf_op jit(solution)/shard_map/pallas_call | solution.py:286
  132.2 0.1 reshape.83
  132.3 0.1 subtract_reduce_fusion
  132.4 0.2 convert_reduce_fusion
  132.6 0.1 select_reduce_fusion
  132.7 2.8 %convolution_convert_fusion.2 = bf16[512,256]{1,0:T(8,128)(2,1)} fusion(bf16[96,5632]{1,0:T(8,128)(2,1)} %get-tuple-element.12, bf16[5632,256]{1,0:T(8,128)(2,1)S(1)} %copy-done, s32[96]{0:T(128)S(1)} %multiply_add_fusion), kind=kOutput, calls=%fused_computation.4 | convolution fusion | flops 302194688 | bytes 4227456 | tf_op jit(solution)/shard_map/dot_general | solution.py:564
  135.6 21.6 %shard_map.112 = bf16[32,16,256]{2,1,0:T(8,128)(2,1)} custom-call(bf16[32,16,256]{2,1,0:T(8,128)(2,1)} %bitcast.50), custom_call_target="tpu_custom_call" | custom-call | tf_op jit(solution)/shard_map/pallas_call | solution.py:221
  157.1 1.7 %copy.13 = bf16[512,256]{1,0:T(8,128)(2,1)} copy(bf16[512,256]{1,0:T(8,128)(2,1)} %bitcast.51) | data formatting | bytes 524288
  (9 shorter events, 0.0 us)
Async XLA Ops:
  0.0 132.7 %copy-start = (bf16[5632,256]{1,0:T(8,128)(2,1)S(1)}, bf16[5632,256]{1,0:T(8,128)(2,1)}, u32[]{:S(2)}) copy-start(bf16[5632,256]{1,0:T(8,128)(2,1)} %param.18) | copy-start | bytes 8650756
  25.3 2.1 %copy-start.4 = (s32[384]{0:T(512)S(1)}, s32[384]{0:T(512)}, u32[]{:S(2)}) copy-start(s32[384]{0:T(512)} %param.12) | copy-start | bytes 4612
  27.4 0.7 copy-start.3
  28.8 2.7 %copy-start.1 = (bf16[384,44]{0,1:T(8,128)(2,1)S(1)}, bf16[384,44]{0,1:T(8,128)(2,1)}, u32[]{:S(2)}) copy-start(bf16[384,44]{0,1:T(8,128)(2,1)} %param.17) | copy-start | bytes 101380
  28.8 2.7 %copy-start.2 = (bf16[44,384]{1,0:T(8,128)(2,1)S(1)}, bf16[44,384]{1,0:T(8,128)(2,1)}, u32[]{:S(2)}) copy-start(bf16[44,384]{1,0:T(8,128)(2,1)} %param.16) | copy-start | bytes 101380
  91.4 41.2 %copy-start.5 = (s32[32]{0:T(128)S(1)}, s32[32]{0:T(128)}, u32[]{:S(2)}) copy-start(s32[32]{0:T(128)} %param.13) | copy-start | bytes 388

commit v12 on v11

--- a/solution.py
+++ b/solution.py
@@ -258,7 +258,7 @@
     as_float = summed.astype(jnp.float32)
     center = jnp.mean(as_float, axis=-1, keepdims=True)
     spread = jnp.mean(jnp.square(as_float - center), axis=-1, keepdims=True)
-    normed = ((as_float - center) * lax.rsqrt(spread + epsilon) * gain_ref[gain_row:gain_row + 1, :]).astype(jnp.bfloat16)
+    normed = ((as_float - center) * lax.rsqrt(spread + epsilon) * gain_ref[...].astype(jnp.float32)[None, :]).astype(jnp.bfloat16)
     mine[...] = normed
     out_ref[me] = normed
     for peer in peers:
@@ -351,7 +351,7 @@
         as_float = summed.astype(jnp.float32)
         center = jnp.mean(as_float, axis=-1, keepdims=True)
         spread = jnp.mean(jnp.square(as_float - center), axis=-1, keepdims=True)
-        normed = ((as_float - center) * lax.rsqrt(spread + epsilon) * gain_ref[gain_row:gain_row + 1, :]).astype(jnp.bfloat16)
+        normed = ((as_float - center) * lax.rsqrt(spread + epsilon) * gain_ref[...].astype(jnp.float32)[None, :]).astype(jnp.bfloat16)
         mine[...] = normed
         out_ref[me] = normed
         for peer in peers:
@@ -408,7 +408,7 @@
     as_float = tok_ref[...].astype(jnp.float32)
     center = jnp.mean(as_float, axis=-1, keepdims=True)
     spread = jnp.mean(jnp.square(as_float - center), axis=-1, keepdims=True)
-    normed = ((as_float - center) * lax.rsqrt(spread + epsilon) * gain_ref[gain_row:gain_row + 1, :]).astype(jnp.bfloat16)
+    normed = ((as_float - center) * lax.rsqrt(spread + epsilon) * gain_ref[...].astype(jnp.float32)[None, :]).astype(jnp.bfloat16)
     mine[...] = normed
     out_ref[me] = normed
 
@@ -587,14 +587,13 @@
     tok_count = lax.axis_size("tok")
     flat_in = project_in.reshape(model_width, 3 * project_in.shape[2])
     local_count = tokens.shape[0]
-    gains = jnp.stack([gain_attend, gain_hidden, gain_final]).astype(jnp.float32)
     stacked = jnp.concatenate([weight_up, weight_down.T], axis=1)
-    gathered = norm_gather_feat(tokens, gains, 0, feat_count, 0)
+    gathered = norm_gather_feat(tokens, gain_attend, 0, feat_count, 0)
     projected = jnp.dot(gathered, flat_in, preferred_element_type=jnp.float32)
     attended = attend(projected, segment_ids, head_count)
     attn_parts = jnp.dot(attended, project_out, preferred_element_type=jnp.float32).astype(jnp.bfloat16)
     second, hidden_rows, weights = mix_ring_feat(
-        attn_parts.reshape(feat_count, local_count, model_width), tokens, gains, 1, stacked,
+        attn_parts.reshape(feat_count, local_count, model_width), tokens, gain_hidden, 1, stacked,
         feat_count, tok_count, 1,
     )
     both = weights
@@ -607,7 +606,7 @@
         hidden, lower_t, (((1,), (1,)), ((), ())), preferred_element_type=jnp.float32
     ).astype(jnp.bfloat16)
     _, merged = mix_feat(
-        down_parts.reshape(feat_count, local_count, model_width), second, gains, 2, feat_count, 3
+        down_parts.reshape(feat_count, local_count, model_width), second, gain_final, 2, feat_count, 3
     )
     embedded = jnp.dot(merged, weight_merge, preferred_element_type=jnp.float32).astype(jnp.bfloat16)
     return route_rows(embedded, segment_ids, owners)

time: 159 us -> 157 us (0.987)
  local copies, waits for them, and re-layouts: 4.42 us -> 2.15 us
    another operation x3 -> x0, local copies, waits for them, and re-layouts: 2.26 us -> none  [body(): jnp.stack([gain_attend, gain_hidden, gain_final]).astype(jnp.float32)]
where the time goes in v12:
time: 157 us
  Pallas kernels  139 us (89%)
  matrix products  13.4 us (9%)
  local copies, waits for them, and re-layouts  2.15 us (1%)
  other arithmetic  1.74 us (1%)
    pallas_call x1, Pallas kernels, mix_ring_feat(): pl.pallas_call(functools.partial(_mix_ring_kernel, n, gain_row), out_shap...  53.7 us
    pallas_call x1, Pallas kernels, mix_feat(): pl.pallas_call(functools.partial(_mix_kernel, n, gain_row), out_shape=(ja...  40.3 us
    pallas_call x1, Pallas kernels, norm_gather_feat(): pl.pallas_call(functools.partial(_norm_gather_kernel, n, gain_row), out_s...  22.6 us
    pallas_call x1, Pallas kernels, route_exchange(): pl.pallas_call(functools.partial(_route_kernel, n), out_shape=jax.ShapeDt...  22.5 us
    dot_general x1, matrix products, body(): lax.dot_general(hidden, lower_t, (((1,), (1,)), ((), ())), preferred_elem...  5.52 us

profile of v12, /device:TPU:1, one launch (start us, length us, event | category | flops | bytes accessed | tf_op | source)
XLA Modules:
  0.0 156.5 jit_solution(5783306501672881522)
XLA Ops:
  0.0 0.0 copy-start
  0.0 22.6 %shard_map.109 = bf16[16,24,1408]{2,1,0:T(8,128)(2,1)} custom-call(bf16[24,1408]{1,0:T(8,128)(2,1)} %resid_ref.1, bf16[1408]{0:T(1024)(128)(2,1)} %gain_ref.3), custom_call_target="tpu_custom_call" | custom-call | tf_op jit(solution)/shard_map/pallas_call | solution.py:431
  22.6 0.0 copy-start.4
  22.6 2.1 %fusion.91 = (bf16[384,3,1,88]{0,3,1,2:T(8,128)(2,1)S(1)}, f32[384,3,1,88]{0,3,1,2:T(8,128)S(1)}) fusion(bf16[384,1408,1]{1,0,2:T(8,128)(2,1)} %bitcast.49, bf16[1408,3,88]{0,2,1:T(8,128)(2,1)} %param.14), kind=kOutput, calls=%fused_computation.114 | convolution fusion | flops 285576192 | bytes 2433024 | tf_op jit(solution)/shard_map/dot_general | solution.py:592
  24.7 0.0 copy-start.3
  24.7 0.0 copy-done.4
  24.7 0.3 fusion.92
  25.0 0.4 copy-done.3
  25.3 0.7 fusion.19
  26.1 2.7 %convolution_convert_fusion.1 = bf16[384,1408]{1,0:T(8,128)(2,1)} fusion(bf16[88,1408]{1,0:T(8,128)(2,1)} %param.15, f32[384,384]{0,1:T(8,128)S(1)} %get-tuple-element.18, f32[384]{0:T(512)} %fusion.19, f32[384]{0:T(512)S(1)} %get-tuple-element.17, bf16[384,3,1,88]{0,3,1,2:T(8,128)(2,1)} %copy-done.3), kind=kOutput, calls=%fused_computation.1 | convolution fusion | flops 122127360 | bytes 1990144 | tf_op jit(solution)/shard_map/dot_general | solution.py:594
  28.7 0.0 copy-done.1
  28.7 0.0 copy-done.2
  28.8 0.6 pad_maximum_fusion.weight_ref
  29.4 53.7 %shard_map.110 = (bf16[24,1408]{1,0:T(8,128)(2,1)}, bf16[16,24,1408]{2,1,0:T(8,128)(2,1)}, bf16[1408,768]{1,0:T(8,128)(2,1)}) custom-call(bf16[16,24,1408]{2,1,0:T(8,128)(2,1)} %bitcast.47, bf16[24,1408]{1,0:T(8,128)(2,1)} %resid_ref.1, bf16[1408]{0:T(1024)(128)(2,1)} %gain_ref.4, bf16[44,768]{1,0:T(8,128)(2,1)} %pad_maximum_fusion.weight_ref), custom_call_target="tpu_custom_call" | custom-call | tf_op jit(solution)/shard_map/pallas_call | solution.py:376
  83.1 5.5 %convolution_convert_fusion = bf16[384,1408]{1,0:T(8,128)(2,1)} fusion(bf16[1408,768]{1,0:T(8,128)(2,1)} %get-tuple-element.10, bf16[384,1408]{1,0:T(8,128)(2,1)} %bitcast.53), kind=kOutput, calls=%fused_computation | convolution fusion | flops 840597504 | bytes 4325376 | tf_op jit(solution)/shard_map/dot_general | solution.py:605
  88.7 40.3 %shard_map.111 = (bf16[24,1408]{1,0:T(8,128)(2,1)}, bf16[16,24,1408]{2,1,0:T(8,128)(2,1)}, bf16[96,5632]{1,0:T(8,128)(2,1)}) custom-call(bf16[16,24,1408]{2,1,0:T(8,128)(2,1)} %bitcast.48, bf16[24,1408]{1,0:T(8,128)(2,1)} %get-tuple-element.11.resid_ref, bf16[1408]{0:T(1024)(128)(2,1)} %gain_ref.5), custom_call_target="tpu_custom_call" | custom-call | tf_op jit(solution)/shard_map/pallas_call | solution.py:286
  129.0 0.1 reshape.83
  129.1 0.1 subtract_reduce_fusion
  129.2 0.2 convert_reduce_fusion
  129.4 0.0 copy-done.5
  129.4 0.1 select_reduce_fusion
  129.5 2.8 %convolution_convert_fusion.2 = bf16[512,256]{1,0:T(8,128)(2,1)} fusion(bf16[96,5632]{1,0:T(8,128)(2,1)} %get-tuple-element.12, bf16[5632,256]{1,0:T(8,128)(2,1)S(1)} %copy-done, s32[96]{0:T(128)S(1)} %multiply_add_fusion), kind=kOutput, calls=%fused_computation.4 | convolution fusion | flops 302194688 | bytes 4227456 | tf_op jit(solution)/shard_map/dot_general | solution.py:564
  132.3 22.5 %shard_map.112 = bf16[32,16,256]{2,1,0:T(8,128)(2,1)} custom-call(bf16[32,16,256]{2,1,0:T(8,128)(2,1)} %bitcast.50), custom_call_target="tpu_custom_call" | custom-call | tf_op jit(solution)/shard_map/pallas_call | solution.py:221
  154.9 1.7 %copy.13 = bf16[512,256]{1,0:T(8,128)(2,1)} copy(bf16[512,256]{1,0:T(8,128)(2,1)} %bitcast.51) | data formatting | bytes 524288
  (5 shorter events, 0.0 us)
Async XLA Ops:
  0.0 129.5 %copy-start = (bf16[5632,256]{1,0:T(8,128)(2,1)S(1)}, bf16[5632,256]{1,0:T(8,128)(2,1)}, u32[]{:S(2)}) copy-start(bf16[5632,256]{1,0:T(8,128)(2,1)} %param.18) | copy-start | bytes 8650756
  22.6 2.1 %copy-start.4 = (s32[384]{0:T(512)S(1)}, s32[384]{0:T(512)}, u32[]{:S(2)}) copy-start(s32[384]{0:T(512)} %param.12) | copy-start | bytes 4612
  24.7 0.7 copy-start.3
  26.1 2.7 %copy-start.1 = (bf16[384,44]{0,1:T(8,128)(2,1)S(1)}, bf16[384,44]{0,1:T(8,128)(2,1)}, u32[]{:S(2)}) copy-start(bf16[384,44]{0,1:T(8,128)(2,1)} %param.17) | copy-start | bytes 101380
  26.1 2.7 %copy-start.2 = (bf16[44,384]{1,0:T(8,128)(2,1)S(1)}, bf16[44,384]{1,0:T(8,128)(2,1)}, u32[]{:S(2)}) copy-start(bf16[44,384]{1,0:T(8,128)(2,1)} %param.16) | copy-start | bytes 101380
  88.7 40.7 %copy-start.5 = (s32[32]{0:T(128)S(1)}, s32[32]{0:T(128)}, u32[]{:S(2)}) copy-start(s32[32]{0:T(128)} %param.13) | copy-start | bytes 388

commit v13 on v12

--- a/solution.py
+++ b/solution.py
@@ -228,43 +228,54 @@
     )(packed)
 
 
-def _mix_kernel(n, gain_row, part_ref, resid_ref, gain_ref, resid_out, out_ref, merged_out, held, mine,
-                scatter_send, scatter_recv, gather_send, gather_recv):
+def _mix_kernel(n, gain_row, part_ref, resid_ref, gain_ref, resid_out, out_ref, merged_out, held, mine_a,
+                mine_b, scatter_send, scatter_recv, gather_send, gather_recv):
     me = lax.axis_index("feat")
     tok_index = lax.axis_index("tok")
     peers = [lax.rem(me + d, n) for d in range(1, n)]
     _greet(peers, tok_index)
-
-    def scatter_copy(peer, slot):
+    split = 16
+    halves = [(0, split), (split, part_ref.shape[1] - split)]
+    mines = [mine_a, mine_b]
+
+    def scatter_copy(half, peer, slot):
+        first, size = halves[half]
         return pltpu.make_async_remote_copy(
-            src_ref=part_ref.at[peer], dst_ref=held.at[slot], send_sem=scatter_send.at[peer],
-            recv_sem=scatter_recv.at[slot], device_id=(tok_index, peer), device_id_type=MESH,
+            src_ref=part_ref.at[peer, pl.ds(first, size)], dst_ref=held.at[slot, pl.ds(first, size)],
+            send_sem=scatter_send.at[half, peer], recv_sem=scatter_recv.at[half, slot],
+            device_id=(tok_index, peer), device_id_type=MESH,
         )
 
-    def gather_copy(peer, slot):
+    def gather_copy(half, peer, slot):
+        first, size = halves[half]
         return pltpu.make_async_remote_copy(
-            src_ref=mine, dst_ref=out_ref.at[slot], send_sem=gather_send.at[peer],
-            recv_sem=gather_recv.at[slot], device_id=(tok_index, peer), device_id_type=MESH,
+            src_ref=mines[half], dst_ref=out_ref.at[slot, pl.ds(first, size)],
+            send_sem=gather_send.at[half, peer], recv_sem=gather_recv.at[half, slot],
+            device_id=(tok_index, peer), device_id_type=MESH,
         )
 
-    for peer in peers:
-        scatter_copy(peer, me).start()
-    total = part_ref[me].astype(jnp.float32)
-    for peer in peers:
-        scatter_copy(peer, peer).wait_recv()
-        total = total + held[peer].astype(jnp.float32)
-    summed = (resid_ref[...].astype(jnp.float32) + total).astype(jnp.bfloat16)
-    resid_out[...] = summed
-    as_float = summed.astype(jnp.float32)
-    center = jnp.mean(as_float, axis=-1, keepdims=True)
-    spread = jnp.mean(jnp.square(as_float - center), axis=-1, keepdims=True)
-    normed = ((as_float - center) * lax.rsqrt(spread + epsilon) * gain_ref[...].astype(jnp.float32)[None, :]).astype(jnp.bfloat16)
-    mine[...] = normed
-    out_ref[me] = normed
-    for peer in peers:
-        gather_copy(peer, me).start()
-    for peer in peers:
-        gather_copy(peer, peer).wait_recv()
+    for half in range(2):
+        for peer in peers:
+            scatter_copy(half, peer, me).start()
+    for half in range(2):
+        first, size = halves[half]
+        total = part_ref[me, first:first + size, :].astype(jnp.float32)
+        for peer in peers:
+            scatter_copy(half, peer, peer).wait_recv()
+            total = total + held[peer, first:first + size, :].astype(jnp.float32)
+        summed = (resid_ref[first:first + size, :].astype(jnp.float32) + total).astype(jnp.bfloat16)
+        resid_out[first:first + size, :] = summed
+        as_float = summed.astype(jnp.float32)
+        center = jnp.mean(as_float, axis=-1, keepdims=True)
+        spread = jnp.mean(jnp.square(as_float - center), axis=-1, keepdims=True)
+        normed = ((as_float - center) * lax.rsqrt(spread + epsilon) * gain_ref[...].astype(jnp.float32)[None, :]).astype(jnp.bfloat16)
+        mines[half][...] = normed
+        out_ref[me, first:first + size, :] = normed
+        for peer in peers:
+            gather_copy(half, peer, me).start()
+    for half in range(2):
+        for peer in peers:
+            gather_copy(half, peer, peer).wait_recv()
     group = 4
     width = out_ref.shape[2]
     row_count = n * out_ref.shape[1]
@@ -276,9 +287,10 @@
         merged_out[:, part * width:(part + 1) * width] = jnp.dot(
             pick, rows, preferred_element_type=jnp.float32
         ).astype(jnp.bfloat16)
-    for peer in peers:
-        scatter_copy(peer, me).wait_send()
-        gather_copy(peer, me).wait_send()
+    for half in range(2):
+        for peer in peers:
+            scatter_copy(half, peer, me).wait_send()
+            gather_copy(half, peer, me).wait_send()
 
 
 def mix_feat(parts, resid, gains, gain_row, n, collective_id):
@@ -294,11 +306,12 @@
         out_specs=(pl.BlockSpec(memory_space=pltpu.VMEM),) * 3,
         scratch_shapes=[
             pltpu.VMEM((n, rows, width), parts.dtype),
-            pltpu.VMEM((rows, width), jnp.bfloat16),
-            pltpu.SemaphoreType.DMA((n,)),
-            pltpu.SemaphoreType.DMA((n,)),
-            pltpu.SemaphoreType.DMA((n,)),
-            pltpu.SemaphoreType.DMA((n,)),
+            pltpu.VMEM((16, width), jnp.bfloat16),
+            pltpu.VMEM((rows - 16, width), jnp.bfloat16),
+            pltpu.SemaphoreType.DMA((2, n)),
+            pltpu.SemaphoreType.DMA((2, n)),
+            pltpu.SemaphoreType.DMA((2, n)),
+            pltpu.SemaphoreType.DMA((2, n)),
         ],
         compiler_params=pltpu.CompilerParams(collective_id=collective_id, has_side_effects=True),
     )(parts, resid, gains)

time: 157 us -> 153 us (0.975)
  Pallas kernels: 139 us -> 135 us
    pallas_call x1, Pallas kernels: 40.3 us -> 36 us  [mix_feat(): pl.pallas_call(functools.partial(_mix_kernel, n, gain_row), out_shape=(ja...]
where the time goes in v13:
time: 153 us; the launch traced here: 152 us
  Pallas kernels  135 us (88%)
  matrix products  13.4 us (9%)
  local copies, waits for them, and re-layouts  2.15 us (1%)
  other arithmetic  1.74 us (1%)
    pallas_call x1, Pallas kernels, mix_ring_feat(): pl.pallas_call(functools.partial(_mix_ring_kernel, n, gain_row), out_shap...  53.7 us
    pallas_call x1, Pallas kernels, mix_feat(): pl.pallas_call(functools.partial(_mix_kernel, n, gain_row), out_shape=(ja...  36 us
    pallas_call x1, Pallas kernels, norm_gather_feat(): pl.pallas_call(functools.partial(_norm_gather_kernel, n, gain_row), out_s...  22.6 us
    pallas_call x1, Pallas kernels, route_exchange(): pl.pallas_call(functools.partial(_route_kernel, n), out_shape=jax.ShapeDt...  22.6 us
    dot_general x1, matrix products, body(): lax.dot_general(hidden, lower_t, (((1,), (1,)), ((), ())), preferred_elem...  5.52 us

profile of v13, /device:TPU:1, one launch (start us, length us, event | category | flops | bytes accessed | tf_op | source)
XLA Modules:
  0.0 152.3 jit_solution(14521372860816505831)
XLA Ops:
  0.0 0.0 copy-start
  0.0 22.6 %shard_map.109 = bf16[16,24,1408]{2,1,0:T(8,128)(2,1)} custom-call(bf16[24,1408]{1,0:T(8,128)(2,1)} %resid_ref.1, bf16[1408]{0:T(1024)(128)(2,1)} %gain_ref.3), custom_call_target="tpu_custom_call" | custom-call | tf_op jit(solution)/shard_map/pallas_call | solution.py:444
  22.6 0.0 copy-start.4
  22.6 2.1 %fusion.91 = (bf16[384,3,1,88]{0,3,1,2:T(8,128)(2,1)S(1)}, f32[384,3,1,88]{0,3,1,2:T(8,128)S(1)}) fusion(bf16[384,1408,1]{1,0,2:T(8,128)(2,1)} %bitcast.49, bf16[1408,3,88]{0,2,1:T(8,128)(2,1)} %param.14), kind=kOutput, calls=%fused_computation.114 | convolution fusion | flops 285576192 | bytes 2433024 | tf_op jit(solution)/shard_map/dot_general | solution.py:605
  24.7 0.0 copy-start.3
  24.7 0.0 copy-done.4
  24.7 0.3 fusion.92
  25.0 0.4 copy-done.3
  25.3 0.7 fusion.19
  26.1 2.7 %convolution_convert_fusion.1 = bf16[384,1408]{1,0:T(8,128)(2,1)} fusion(bf16[88,1408]{1,0:T(8,128)(2,1)} %param.15, f32[384,384]{0,1:T(8,128)S(1)} %get-tuple-element.18, f32[384]{0:T(512)} %fusion.19, f32[384]{0:T(512)S(1)} %get-tuple-element.17, bf16[384,3,1,88]{0,3,1,2:T(8,128)(2,1)} %copy-done.3), kind=kOutput, calls=%fused_computation.1 | convolution fusion | flops 122127360 | bytes 1990144 | tf_op jit(solution)/shard_map/dot_general | solution.py:607
  28.7 0.0 copy-done.1
  28.7 0.0 copy-done.2
  28.8 0.6 pad_maximum_fusion.weight_ref
  29.4 53.7 %shard_map.110 = (bf16[24,1408]{1,0:T(8,128)(2,1)}, bf16[16,24,1408]{2,1,0:T(8,128)(2,1)}, bf16[1408,768]{1,0:T(8,128)(2,1)}) custom-call(bf16[16,24,1408]{2,1,0:T(8,128)(2,1)} %bitcast.47, bf16[24,1408]{1,0:T(8,128)(2,1)} %resid_ref.1, bf16[1408]{0:T(1024)(128)(2,1)} %gain_ref.4, bf16[44,768]{1,0:T(8,128)(2,1)} %pad_maximum_fusion.weight_ref), custom_call_target="tpu_custom_call" | custom-call | tf_op jit(solution)/shard_map/pallas_call | solution.py:389
  83.1 5.5 %convolution_convert_fusion = bf16[384,1408]{1,0:T(8,128)(2,1)} fusion(bf16[1408,768]{1,0:T(8,128)(2,1)} %get-tuple-element.10, bf16[384,1408]{1,0:T(8,128)(2,1)} %bitcast.53), kind=kOutput, calls=%fused_computation | convolution fusion | flops 840597504 | bytes 4325376 | tf_op jit(solution)/shard_map/dot_general | solution.py:618
  88.7 36.0 %shard_map.111 = (bf16[24,1408]{1,0:T(8,128)(2,1)}, bf16[16,24,1408]{2,1,0:T(8,128)(2,1)}, bf16[96,5632]{1,0:T(8,128)(2,1)}) custom-call(bf16[16,24,1408]{2,1,0:T(8,128)(2,1)} %bitcast.48, bf16[24,1408]{1,0:T(8,128)(2,1)} %get-tuple-element.11.resid_ref, bf16[1408]{0:T(1024)(128)(2,1)} %gain_ref.5), custom_call_target="tpu_custom_call" | custom-call | tf_op jit(solution)/shard_map/pallas_call | solution.py:298
  124.7 0.1 reshape.83
  124.8 0.1 subtract_reduce_fusion
  124.9 0.2 convert_reduce_fusion
  125.1 0.0 copy-done.5
  125.1 0.1 select_reduce_fusion
  125.2 2.8 %convolution_convert_fusion.2 = bf16[512,256]{1,0:T(8,128)(2,1)} fusion(bf16[96,5632]{1,0:T(8,128)(2,1)} %get-tuple-element.12, bf16[5632,256]{1,0:T(8,128)(2,1)S(1)} %copy-done, s32[96]{0:T(128)S(1)} %multiply_add_fusion), kind=kOutput, calls=%fused_computation.4 | convolution fusion | flops 302194688 | bytes 4227456 | tf_op jit(solution)/shard_map/dot_general | solution.py:577
  128.1 22.6 %shard_map.112 = bf16[32,16,256]{2,1,0:T(8,128)(2,1)} custom-call(bf16[32,16,256]{2,1,0:T(8,128)(2,1)} %bitcast.50), custom_call_target="tpu_custom_call" | custom-call | tf_op jit(solution)/shard_map/pallas_call | solution.py:221
  150.6 1.7 %copy.13 = bf16[512,256]{1,0:T(8,128)(2,1)} copy(bf16[512,256]{1,0:T(8,128)(2,1)} %bitcast.51) | data formatting | bytes 524288
  (5 shorter events, 0.0 us)
Async XLA Ops:
  0.0 125.2 %copy-start = (bf16[5632,256]{1,0:T(8,128)(2,1)S(1)}, bf16[5632,256]{1,0:T(8,128)(2,1)}, u32[]{:S(2)}) copy-start(bf16[5632,256]{1,0:T(8,128)(2,1)} %param.18) | copy-start | bytes 8650756
  22.6 2.1 %copy-start.4 = (s32[384]{0:T(512)S(1)}, s32[384]{0:T(512)}, u32[]{:S(2)}) copy-start(s32[384]{0:T(512)} %param.12) | copy-start | bytes 4612
  24.7 0.7 copy-start.3
  26.1 2.7 %copy-start.1 = (bf16[384,44]{0,1:T(8,128)(2,1)S(1)}, bf16[384,44]{0,1:T(8,128)(2,1)}, u32[]{:S(2)}) copy-start(bf16[384,44]{0,1:T(8,128)(2,1)} %param.17) | copy-start | bytes 101380
  26.1 2.7 %copy-start.2 = (bf16[44,384]{1,0:T(8,128)(2,1)S(1)}, bf16[44,384]{1,0:T(8,128)(2,1)}, u32[]{:S(2)}) copy-start(bf16[44,384]{1,0:T(8,128)(2,1)} %param.16) | copy-start | bytes 101380
  88.7 36.5 %copy-start.5 = (s32[32]{0:T(128)S(1)}, s32[32]{0:T(128)}, u32[]{:S(2)}) copy-start(s32[32]{0:T(128)} %param.13) | copy-start | bytes 388

commit v14 on v13

--- a/solution.py
+++ b/solution.py
@@ -319,7 +319,7 @@
 
 
 def _mix_ring_kernel(n, gain_row, part_ref, resid_ref, gain_ref, weight_ref, resid_out, out_ref, weight_flat,
-                     weight_out, held, mine, scatter_send, scatter_recv, gather_send, gather_recv,
+                     weight_out, held, mine_a, mine_b, scatter_send, scatter_recv, gather_send, gather_recv,
                      send_right, send_left, send_partner, weight_recv):
     me = lax.axis_index("feat")
     tok_index = lax.axis_index("tok")
@@ -339,47 +339,60 @@
         pl.semaphore_signal(barrier, inc=1, device_id=(peer, me), device_id_type=MESH)
     pl.semaphore_wait(barrier, len(peers) + len(ring_peers))
 
-    def scatter_copy(peer, slot):
+    split = 16
+    halves = [(0, split), (split, part_ref.shape[1] - split)]
+    mines = [mine_a, mine_b]
+
+    def scatter_copy(half, peer, slot):
+        first, size = halves[half]
         return pltpu.make_async_remote_copy(
-            src_ref=part_ref.at[peer], dst_ref=held.at[slot], send_sem=scatter_send.at[peer],
-            recv_sem=scatter_recv.at[slot], device_id=(tok_index, peer), device_id_type=MESH,
+            src_ref=part_ref.at[peer, pl.ds(first, size)], dst_ref=held.at[slot, pl.ds(first, size)],
+            send_sem=scatter_send.at[half, peer], recv_sem=scatter_recv.at[half, slot],
+            device_id=(tok_index, peer), device_id_type=MESH,
         )
 
-    def gather_copy(peer, slot):
+    def gather_copy(half, peer, slot):
+        first, size = halves[half]
         return pltpu.make_async_remote_copy(
-            src_ref=mine, dst_ref=out_ref.at[slot], send_sem=gather_send.at[peer],
-            recv_sem=gather_recv.at[slot], device_id=(tok_index, peer), device_id_type=MESH,
+            src_ref=mines[half], dst_ref=out_ref.at[slot, pl.ds(first, size)],
+            send_sem=gather_send.at[half, peer], recv_sem=gather_recv.at[half, slot],
+            device_id=(tok_index, peer), device_id_type=MESH,
         )
 
-    for peer in peers:
-        scatter_copy(peer, me).start()
+    for half in range(2):
+        for peer in peers:
+            scatter_copy(half, peer, me).start()
 
     def norm_and_send():
-        total = part_ref[me].astype(jnp.float32)
-        for peer in peers:
-            scatter_copy(peer, peer).wait_recv()
-            total = total + held[peer].astype(jnp.float32)
-        summed = (resid_ref[...].astype(jnp.float32) + total).astype(jnp.bfloat16)
-        resid_out[...] = summed
-        as_float = summed.astype(jnp.float32)
-        center = jnp.mean(as_float, axis=-1, keepdims=True)
-        spread = jnp.mean(jnp.square(as_float - center), axis=-1, keepdims=True)
-        normed = ((as_float - center) * lax.rsqrt(spread + epsilon) * gain_ref[...].astype(jnp.float32)[None, :]).astype(jnp.bfloat16)
-        mine[...] = normed
-        out_ref[me] = normed
-        for peer in peers:
-            gather_copy(peer, me).start()
+        for half in range(2):
+            first, size = halves[half]
+            total = part_ref[me, first:first + size, :].astype(jnp.float32)
+            for peer in peers:
+                scatter_copy(half, peer, peer).wait_recv()
+                total = total + held[peer, first:first + size, :].astype(jnp.float32)
+            summed = (resid_ref[first:first + size, :].astype(jnp.float32) + total).astype(jnp.bfloat16)
+            resid_out[first:first + size, :] = summed
+            as_float = summed.astype(jnp.float32)
+            center = jnp.mean(as_float, axis=-1, keepdims=True)
+            spread = jnp.mean(jnp.square(as_float - center), axis=-1, keepdims=True)
+            normed = ((as_float - center) * lax.rsqrt(spread + epsilon) * gain_ref[...].astype(jnp.float32)[None, :]).astype(jnp.bfloat16)
+            mines[half][...] = normed
+            out_ref[me, first:first + size, :] = normed
+            for peer in peers:
+                gather_copy(half, peer, me).start()
 
     _ring_gather(weight_ref, weight_out, send_right, send_left, send_partner, weight_recv, me,
                  hook=norm_and_send, hook_step=3)
     block_rows = weight_out.shape[1]
     for slot in range(weight_out.shape[0]):
         weight_flat[slot * block_rows:(slot + 1) * block_rows, :] = weight_out[slot]
-    for peer in peers:
-        gather_copy(peer, peer).wait_recv()
-    for peer in peers:
-        scatter_copy(peer, me).wait_send()
-        gather_copy(peer, me).wait_send()
+    for half in range(2):
+        for peer in peers:
+            gather_copy(half, peer, peer).wait_recv()
+    for half in range(2):
+        for peer in peers:
+            scatter_copy(half, peer, me).wait_send()
+            gather_copy(half, peer, me).wait_send()
 
 
 def mix_ring_feat(parts, resid, gains, gain_row, weight_block, n, tok_count, collective_id):
@@ -398,11 +411,12 @@
         scratch_shapes=[
             pltpu.VMEM((tok_count, weight_rows, weight_width), weight_block.dtype),
             pltpu.VMEM((n, rows, width), parts.dtype),
-            pltpu.VMEM((rows, width), jnp.bfloat16),
-            pltpu.SemaphoreType.DMA((n,)),
-            pltpu.SemaphoreType.DMA((n,)),
-            pltpu.SemaphoreType.DMA((n,)),
-            pltpu.SemaphoreType.DMA((n,)),
+            pltpu.VMEM((16, width), jnp.bfloat16),
+            pltpu.VMEM((rows - 16, width), jnp.bfloat16),
+            pltpu.SemaphoreType.DMA((2, n)),
+            pltpu.SemaphoreType.DMA((2, n)),
+            pltpu.SemaphoreType.DMA((2, n)),
+            pltpu.SemaphoreType.DMA((2, n)),
             pltpu.SemaphoreType.DMA((chips,)),
             pltpu.SemaphoreType.DMA((chips,)),
             pltpu.SemaphoreType.DMA((chips,)),

time: 153 us -> 155 us (1.013)
  Pallas kernels: 135 us -> 137 us
    pallas_call x1, Pallas kernels: 53.7 us -> 55.9 us  [mix_ring_feat(): pl.pallas_call(functools.partial(_mix_ring_kernel, n, gain_row), out_shap...]
where the time goes in v14:
time: 155 us
  Pallas kernels  137 us (88%)
  matrix products  13.4 us (9%)
  local copies, waits for them, and re-layouts  2.15 us (1%)
  other arithmetic  1.74 us (1%)
    pallas_call x1, Pallas kernels, mix_ring_feat(): pl.pallas_call(functools.partial(_mix_ring_kernel, n, gain_row), out_shap...  55.9 us
    pallas_call x1, Pallas kernels, mix_feat(): pl.pallas_call(functools.partial(_mix_kernel, n, gain_row), out_shape=(ja...  35.5 us
    pallas_call x1, Pallas kernels, route_exchange(): pl.pallas_call(functools.partial(_route_kernel, n), out_shape=jax.ShapeDt...  23.4 us
    pallas_call x1, Pallas kernels, norm_gather_feat(): pl.pallas_call(functools.partial(_norm_gather_kernel, n, gain_row), out_s...  22.6 us
    dot_general x1, matrix products, body(): lax.dot_general(hidden, lower_t, (((1,), (1,)), ((), ())), preferred_elem...  5.52 us

profile of v14, /device:TPU:1, one launch (start us, length us, event | category | flops | bytes accessed | tf_op | source)
XLA Modules:
  0.0 154.8 jit_solution(7258165684993107344)
XLA Ops:
  0.0 0.0 copy-start
  0.0 22.6 %shard_map.109 = bf16[16,24,1408]{2,1,0:T(8,128)(2,1)} custom-call(bf16[24,1408]{1,0:T(8,128)(2,1)} %resid_ref.1, bf16[1408]{0:T(1024)(128)(2,1)} %gain_ref.3), custom_call_target="tpu_custom_call" | custom-call | tf_op jit(solution)/shard_map/pallas_call | solution.py:458
  22.6 0.0 copy-start.4
  22.6 2.1 %fusion.91 = (bf16[384,3,1,88]{0,3,1,2:T(8,128)(2,1)S(1)}, f32[384,3,1,88]{0,3,1,2:T(8,128)S(1)}) fusion(bf16[384,1408,1]{1,0,2:T(8,128)(2,1)} %bitcast.49, bf16[1408,3,88]{0,2,1:T(8,128)(2,1)} %param.14), kind=kOutput, calls=%fused_computation.114 | convolution fusion | flops 285576192 | bytes 2433024 | tf_op jit(solution)/shard_map/dot_general | solution.py:619
  24.7 0.0 copy-start.3
  24.7 0.0 copy-done.4
  24.7 0.3 fusion.92
  25.0 0.4 copy-done.3
  25.3 0.7 fusion.19
  26.1 2.7 %convolution_convert_fusion.1 = bf16[384,1408]{1,0:T(8,128)(2,1)} fusion(bf16[88,1408]{1,0:T(8,128)(2,1)} %param.15, f32[384,384]{0,1:T(8,128)S(1)} %get-tuple-element.18, f32[384]{0:T(512)} %fusion.19, f32[384]{0:T(512)S(1)} %get-tuple-element.17, bf16[384,3,1,88]{0,3,1,2:T(8,128)(2,1)} %copy-done.3), kind=kOutput, calls=%fused_computation.1 | convolution fusion | flops 122127360 | bytes 1990144 | tf_op jit(solution)/shard_map/dot_general | solution.py:621
  28.7 0.0 copy-done.1
  28.8 0.6 pad_maximum_fusion.weight_ref
  29.4 55.9 %shard_map.110 = (bf16[24,1408]{1,0:T(8,128)(2,1)}, bf16[16,24,1408]{2,1,0:T(8,128)(2,1)}, bf16[1408,768]{1,0:T(8,128)(2,1)}) custom-call(bf16[16,24,1408]{2,1,0:T(8,128)(2,1)} %bitcast.47, bf16[24,1408]{1,0:T(8,128)(2,1)} %resid_ref.1, bf16[1408]{0:T(1024)(128)(2,1)} %gain_ref.4, bf16[44,768]{1,0:T(8,128)(2,1)} %pad_maximum_fusion.weight_ref), custom_call_target="tpu_custom_call" | custom-call | tf_op jit(solution)/shard_map/pallas_call | solution.py:402
  85.3 5.5 %convolution_convert_fusion = bf16[384,1408]{1,0:T(8,128)(2,1)} fusion(bf16[1408,768]{1,0:T(8,128)(2,1)} %get-tuple-element.10, bf16[384,1408]{1,0:T(8,128)(2,1)} %bitcast.53), kind=kOutput, calls=%fused_computation | convolution fusion | flops 840597504 | bytes 4325376 | tf_op jit(solution)/shard_map/dot_general | solution.py:632
  90.9 35.5 %shard_map.111 = (bf16[24,1408]{1,0:T(8,128)(2,1)}, bf16[16,24,1408]{2,1,0:T(8,128)(2,1)}, bf16[96,5632]{1,0:T(8,128)(2,1)}) custom-call(bf16[16,24,1408]{2,1,0:T(8,128)(2,1)} %bitcast.48, bf16[24,1408]{1,0:T(8,128)(2,1)} %get-tuple-element.11.resid_ref, bf16[1408]{0:T(1024)(128)(2,1)} %gain_ref.5), custom_call_target="tpu_custom_call" | custom-call | tf_op jit(solution)/shard_map/pallas_call | solution.py:298
  126.4 0.1 reshape.83
  126.5 0.1 subtract_reduce_fusion
  126.6 0.2 convert_reduce_fusion
  126.8 0.0 copy-done.5
  126.8 0.1 select_reduce_fusion
  126.9 0.0 copy-done
  126.9 2.8 %convolution_convert_fusion.2 = bf16[512,256]{1,0:T(8,128)(2,1)} fusion(bf16[96,5632]{1,0:T(8,128)(2,1)} %get-tuple-element.12, bf16[5632,256]{1,0:T(8,128)(2,1)S(1)} %copy-done, s32[96]{0:T(128)S(1)} %multiply_add_fusion), kind=kOutput, calls=%fused_computation.4 | convolution fusion | flops 302194688 | bytes 4227456 | tf_op jit(solution)/shard_map/dot_general | solution.py:591
  129.7 23.4 %shard_map.112 = bf16[32,16,256]{2,1,0:T(8,128)(2,1)} custom-call(bf16[32,16,256]{2,1,0:T(8,128)(2,1)} %bitcast.50), custom_call_target="tpu_custom_call" | custom-call | tf_op jit(solution)/shard_map/pallas_call | solution.py:221
  153.2 1.7 %copy.13 = bf16[512,256]{1,0:T(8,128)(2,1)} copy(bf16[512,256]{1,0:T(8,128)(2,1)} %bitcast.51) | data formatting | bytes 524288
  (5 shorter events, 0.0 us)
Async XLA Ops:
  0.0 126.9 %copy-start = (bf16[5632,256]{1,0:T(8,128)(2,1)S(1)}, bf16[5632,256]{1,0:T(8,128)(2,1)}, u32[]{:S(2)}) copy-start(bf16[5632,256]{1,0:T(8,128)(2,1)} %param.18) | copy-start | bytes 8650756
  22.6 2.1 %copy-start.4 = (s32[384]{0:T(512)S(1)}, s32[384]{0:T(512)}, u32[]{:S(2)}) copy-start(s32[384]{0:T(512)} %param.12) | copy-start | bytes 4612
  24.7 0.7 copy-start.3
  26.1 2.7 %copy-start.1 = (bf16[384,44]{0,1:T(8,128)(2,1)S(1)}, bf16[384,44]{0,1:T(8,128)(2,1)}, u32[]{:S(2)}) copy-start(bf16[384,44]{0,1:T(8,128)(2,1)} %param.17) | copy-start | bytes 101380
  26.1 2.7 %copy-start.2 = (bf16[44,384]{1,0:T(8,128)(2,1)S(1)}, bf16[44,384]{1,0:T(8,128)(2,1)}, u32[]{:S(2)}) copy-start(bf16[44,384]{1,0:T(8,128)(2,1)} %param.16) | copy-start | bytes 101380
  90.9 35.9 %copy-start.5 = (s32[32]{0:T(128)S(1)}, s32[32]{0:T(128)}, u32[]{:S(2)}) copy-start(s32[32]{0:T(128)} %param.13) | copy-start | bytes 388

commit v15 on v13

--- a/solution.py
+++ b/solution.py
@@ -371,7 +371,7 @@
             gather_copy(peer, me).start()
 
     _ring_gather(weight_ref, weight_out, send_right, send_left, send_partner, weight_recv, me,
-                 hook=norm_and_send, hook_step=3)
+                 hook=norm_and_send, hook_step=5)
     block_rows = weight_out.shape[1]
     for slot in range(weight_out.shape[0]):
         weight_flat[slot * block_rows:(slot + 1) * block_rows, :] = weight_out[slot]

time: 153 us -> 150 us (0.980)
  Pallas kernels: 135 us -> 133 us
    pallas_call x1, Pallas kernels: 53.7 us -> 50.3 us  [mix_ring_feat(): pl.pallas_call(functools.partial(_mix_ring_kernel, n, gain_row), out_shap...]
    pallas_call x1, Pallas kernels: 22.6 us -> 25.3 us  [route_exchange(): pl.pallas_call(functools.partial(_route_kernel, n), out_shape=jax.ShapeDt...]
    pallas_call x1, Pallas kernels: 36 us -> 34.4 us  [mix_feat(): pl.pallas_call(functools.partial(_mix_kernel, n, gain_row), out_shape=(ja...]
where the time goes in v15:
time: 150 us
  Pallas kernels  133 us (89%)
  matrix products  13.4 us (9%)
  local copies, waits for them, and re-layouts  2.15 us (1%)
  other arithmetic  1.74 us (1%)
    pallas_call x1, Pallas kernels, mix_ring_feat(): pl.pallas_call(functools.partial(_mix_ring_kernel, n, gain_row), out_shap...  50.3 us
    pallas_call x1, Pallas kernels, mix_feat(): pl.pallas_call(functools.partial(_mix_kernel, n, gain_row), out_shape=(ja...  34.4 us
    pallas_call x1, Pallas kernels, route_exchange(): pl.pallas_call(functools.partial(_route_kernel, n), out_shape=jax.ShapeDt...  25.3 us
    pallas_call x1, Pallas kernels, norm_gather_feat(): pl.pallas_call(functools.partial(_norm_gather_kernel, n, gain_row), out_s...  22.6 us
    dot_general x1, matrix products, body(): lax.dot_general(hidden, lower_t, (((1,), (1,)), ((), ())), preferred_elem...  5.52 us

profile of v15, /device:TPU:1, one launch (start us, length us, event | category | flops | bytes accessed | tf_op | source)
XLA Modules:
  0.0 150.1 jit_solution(17156952115324475398)
XLA Ops:
  0.0 0.0 copy-start
  0.0 22.6 %shard_map.109 = bf16[16,24,1408]{2,1,0:T(8,128)(2,1)} custom-call(bf16[24,1408]{1,0:T(8,128)(2,1)} %resid_ref.1, bf16[1408]{0:T(1024)(128)(2,1)} %gain_ref.3), custom_call_target="tpu_custom_call" | custom-call | tf_op jit(solution)/shard_map/pallas_call | solution.py:444
  22.6 0.0 copy-start.4
  22.6 2.1 %fusion.91 = (bf16[384,3,1,88]{0,3,1,2:T(8,128)(2,1)S(1)}, f32[384,3,1,88]{0,3,1,2:T(8,128)S(1)}) fusion(bf16[384,1408,1]{1,0,2:T(8,128)(2,1)} %bitcast.49, bf16[1408,3,88]{0,2,1:T(8,128)(2,1)} %param.14), kind=kOutput, calls=%fused_computation.114 | convolution fusion | flops 285576192 | bytes 2433024 | tf_op jit(solution)/shard_map/dot_general | solution.py:605
  24.7 0.0 copy-start.3
  24.7 0.0 copy-done.4
  24.7 0.3 fusion.92
  25.0 0.4 copy-done.3
  25.3 0.7 fusion.19
  26.1 2.7 %convolution_convert_fusion.1 = bf16[384,1408]{1,0:T(8,128)(2,1)} fusion(bf16[88,1408]{1,0:T(8,128)(2,1)} %param.15, f32[384,384]{0,1:T(8,128)S(1)} %get-tuple-element.18, f32[384]{0:T(512)} %fusion.19, f32[384]{0:T(512)S(1)} %get-tuple-element.17, bf16[384,3,1,88]{0,3,1,2:T(8,128)(2,1)} %copy-done.3), kind=kOutput, calls=%fused_computation.1 | convolution fusion | flops 122127360 | bytes 1990144 | tf_op jit(solution)/shard_map/dot_general | solution.py:607
  28.7 0.0 copy-done.1
  28.8 0.6 pad_maximum_fusion.weight_ref
  29.4 50.3 %shard_map.110 = (bf16[24,1408]{1,0:T(8,128)(2,1)}, bf16[16,24,1408]{2,1,0:T(8,128)(2,1)}, bf16[1408,768]{1,0:T(8,128)(2,1)}) custom-call(bf16[16,24,1408]{2,1,0:T(8,128)(2,1)} %bitcast.47, bf16[24,1408]{1,0:T(8,128)(2,1)} %resid_ref.1, bf16[1408]{0:T(1024)(128)(2,1)} %gain_ref.4, bf16[44,768]{1,0:T(8,128)(2,1)} %pad_maximum_fusion.weight_ref), custom_call_target="tpu_custom_call" | custom-call | tf_op jit(solution)/shard_map/pallas_call | solution.py:389
  79.7 5.5 %convolution_convert_fusion = bf16[384,1408]{1,0:T(8,128)(2,1)} fusion(bf16[1408,768]{1,0:T(8,128)(2,1)} %get-tuple-element.10, bf16[384,1408]{1,0:T(8,128)(2,1)} %bitcast.53), kind=kOutput, calls=%fused_computation | convolution fusion | flops 840597504 | bytes 4325376 | tf_op jit(solution)/shard_map/dot_general | solution.py:618
  85.3 34.4 %shard_map.111 = (bf16[24,1408]{1,0:T(8,128)(2,1)}, bf16[16,24,1408]{2,1,0:T(8,128)(2,1)}, bf16[96,5632]{1,0:T(8,128)(2,1)}) custom-call(bf16[16,24,1408]{2,1,0:T(8,128)(2,1)} %bitcast.48, bf16[24,1408]{1,0:T(8,128)(2,1)} %get-tuple-element.11.resid_ref, bf16[1408]{0:T(1024)(128)(2,1)} %gain_ref.5), custom_call_target="tpu_custom_call" | custom-call | tf_op jit(solution)/shard_map/pallas_call | solution.py:298
  119.7 0.1 reshape.83
  119.8 0.1 subtract_reduce_fusion
  119.9 0.2 convert_reduce_fusion
  120.1 0.0 copy-done.5
  120.1 0.1 select_reduce_fusion
  120.2 0.0 copy-done
  120.2 2.8 %convolution_convert_fusion.2 = bf16[512,256]{1,0:T(8,128)(2,1)} fusion(bf16[96,5632]{1,0:T(8,128)(2,1)} %get-tuple-element.12, bf16[5632,256]{1,0:T(8,128)(2,1)S(1)} %copy-done, s32[96]{0:T(128)S(1)} %multiply_add_fusion), kind=kOutput, calls=%fused_computation.4 | convolution fusion | flops 302194688 | bytes 4227456 | tf_op jit(solution)/shard_map/dot_general | solution.py:577
  123.1 25.3 %shard_map.112 = bf16[32,16,256]{2,1,0:T(8,128)(2,1)} custom-call(bf16[32,16,256]{2,1,0:T(8,128)(2,1)} %bitcast.50), custom_call_target="tpu_custom_call" | custom-call | tf_op jit(solution)/shard_map/pallas_call | solution.py:221
  148.4 1.7 %copy.13 = bf16[512,256]{1,0:T(8,128)(2,1)} copy(bf16[512,256]{1,0:T(8,128)(2,1)} %bitcast.51) | data formatting | bytes 524288
  (5 shorter events, 0.0 us)
Async XLA Ops:
  0.0 120.2 %copy-start = (bf16[5632,256]{1,0:T(8,128)(2,1)S(1)}, bf16[5632,256]{1,0:T(8,128)(2,1)}, u32[]{:S(2)}) copy-start(bf16[5632,256]{1,0:T(8,128)(2,1)} %param.18) | copy-start | bytes 8650756
  22.6 2.1 %copy-start.4 = (s32[384]{0:T(512)S(1)}, s32[384]{0:T(512)}, u32[]{:S(2)}) copy-start(s32[384]{0:T(512)} %param.12) | copy-start | bytes 4612
  24.7 0.7 copy-start.3
  26.1 2.7 %copy-start.1 = (bf16[384,44]{0,1:T(8,128)(2,1)S(1)}, bf16[384,44]{0,1:T(8,128)(2,1)}, u32[]{:S(2)}) copy-start(bf16[384,44]{0,1:T(8,128)(2,1)} %param.17) | copy-start | bytes 101380
  26.1 2.7 %copy-start.2 = (bf16[44,384]{1,0:T(8,128)(2,1)S(1)}, bf16[44,384]{1,0:T(8,128)(2,1)}, u32[]{:S(2)}) copy-start(bf16[44,384]{1,0:T(8,128)(2,1)} %param.16) | copy-start | bytes 101380
  85.3 34.9 %copy-start.5 = (s32[32]{0:T(128)S(1)}, s32[32]{0:T(128)}, u32[]{:S(2)}) copy-start(s32[32]{0:T(128)} %param.13) | copy-start | bytes 388

commit v16 on v15

--- a/solution.py
+++ b/solution.py
@@ -371,7 +371,7 @@
             gather_copy(peer, me).start()
 
     _ring_gather(weight_ref, weight_out, send_right, send_left, send_partner, weight_recv, me,
-                 hook=norm_and_send, hook_step=5)
+                 hook=norm_and_send, hook_step=7)
     block_rows = weight_out.shape[1]
     for slot in range(weight_out.shape[0]):
         weight_flat[slot * block_rows:(slot + 1) * block_rows, :] = weight_out[slot]

time: 150 us -> 151 us (level)
    pallas_call x1, Pallas kernels: 34.4 us -> 30.5 us  [mix_feat(): pl.pallas_call(functools.partial(_mix_kernel, n, gain_row), out_shape=(ja...]
    pallas_call x1, Pallas kernels: 25.3 us -> 29.2 us  [route_exchange(): pl.pallas_call(functools.partial(_route_kernel, n), out_shape=jax.ShapeDt...]
where the time goes in v16:
time: 151 us
  Pallas kernels  133 us (88%)
  matrix products  13.4 us (9%)
  local copies, waits for them, and re-layouts  2.15 us (1%)
  other arithmetic  1.74 us (1%)
    pallas_call x1, Pallas kernels, mix_ring_feat(): pl.pallas_call(functools.partial(_mix_ring_kernel, n, gain_row), out_shap...  51 us
    pallas_call x1, Pallas kernels, mix_feat(): pl.pallas_call(functools.partial(_mix_kernel, n, gain_row), out_shape=(ja...  30.5 us
    pallas_call x1, Pallas kernels, route_exchange(): pl.pallas_call(functools.partial(_route_kernel, n), out_shape=jax.ShapeDt...  29.2 us
    pallas_call x1, Pallas kernels, norm_gather_feat(): pl.pallas_call(functools.partial(_norm_gather_kernel, n, gain_row), out_s...  22.6 us
    dot_general x1, matrix products, body(): lax.dot_general(hidden, lower_t, (((1,), (1,)), ((), ())), preferred_elem...  5.52 us

profile of v16, /device:TPU:1, one launch (start us, length us, event | category | flops | bytes accessed | tf_op | source)
XLA Modules:
  0.0 150.6 jit_solution(10874236844204887865)
XLA Ops:
  0.0 0.0 copy-start
  0.0 22.6 %shard_map.109 = bf16[16,24,1408]{2,1,0:T(8,128)(2,1)} custom-call(bf16[24,1408]{1,0:T(8,128)(2,1)} %resid_ref.1, bf16[1408]{0:T(1024)(128)(2,1)} %gain_ref.3), custom_call_target="tpu_custom_call" | custom-call | tf_op jit(solution)/shard_map/pallas_call | solution.py:444
  22.6 0.0 copy-start.4
  22.6 2.1 %fusion.91 = (bf16[384,3,1,88]{0,3,1,2:T(8,128)(2,1)S(1)}, f32[384,3,1,88]{0,3,1,2:T(8,128)S(1)}) fusion(bf16[384,1408,1]{1,0,2:T(8,128)(2,1)} %bitcast.49, bf16[1408,3,88]{0,2,1:T(8,128)(2,1)} %param.14), kind=kOutput, calls=%fused_computation.114 | convolution fusion | flops 285576192 | bytes 2433024 | tf_op jit(solution)/shard_map/dot_general | solution.py:605
  24.7 0.0 copy-start.3
  24.7 0.0 copy-done.4
  24.7 0.3 fusion.92
  25.0 0.4 copy-done.3
  25.3 0.7 fusion.19
  26.1 2.7 %convolution_convert_fusion.1 = bf16[384,1408]{1,0:T(8,128)(2,1)} fusion(bf16[88,1408]{1,0:T(8,128)(2,1)} %param.15, f32[384,384]{0,1:T(8,128)S(1)} %get-tuple-element.18, f32[384]{0:T(512)} %fusion.19, f32[384]{0:T(512)S(1)} %get-tuple-element.17, bf16[384,3,1,88]{0,3,1,2:T(8,128)(2,1)} %copy-done.3), kind=kOutput, calls=%fused_computation.1 | convolution fusion | flops 122127360 | bytes 1990144 | tf_op jit(solution)/shard_map/dot_general | solution.py:607
  28.7 0.0 copy-done.1
  28.7 0.0 copy-done.2
  28.8 0.6 pad_maximum_fusion.weight_ref
  29.4 51.0 %shard_map.110 = (bf16[24,1408]{1,0:T(8,128)(2,1)}, bf16[16,24,1408]{2,1,0:T(8,128)(2,1)}, bf16[1408,768]{1,0:T(8,128)(2,1)}) custom-call(bf16[16,24,1408]{2,1,0:T(8,128)(2,1)} %bitcast.47, bf16[24,1408]{1,0:T(8,128)(2,1)} %resid_ref.1, bf16[1408]{0:T(1024)(128)(2,1)} %gain_ref.4, bf16[44,768]{1,0:T(8,128)(2,1)} %pad_maximum_fusion.weight_ref), custom_call_target="tpu_custom_call" | custom-call | tf_op jit(solution)/shard_map/pallas_call | solution.py:389
  80.4 5.5 %convolution_convert_fusion = bf16[384,1408]{1,0:T(8,128)(2,1)} fusion(bf16[1408,768]{1,0:T(8,128)(2,1)} %get-tuple-element.10, bf16[384,1408]{1,0:T(8,128)(2,1)} %bitcast.53), kind=kOutput, calls=%fused_computation | convolution fusion | flops 840597504 | bytes 4325376 | tf_op jit(solution)/shard_map/dot_general | solution.py:618
  85.9 30.5 %shard_map.111 = (bf16[24,1408]{1,0:T(8,128)(2,1)}, bf16[16,24,1408]{2,1,0:T(8,128)(2,1)}, bf16[96,5632]{1,0:T(8,128)(2,1)}) custom-call(bf16[16,24,1408]{2,1,0:T(8,128)(2,1)} %bitcast.48, bf16[24,1408]{1,0:T(8,128)(2,1)} %get-tuple-element.11.resid_ref, bf16[1408]{0:T(1024)(128)(2,1)} %gain_ref.5), custom_call_target="tpu_custom_call" | custom-call | tf_op jit(solution)/shard_map/pallas_call | solution.py:298
  116.4 0.1 reshape.83
  116.5 0.1 subtract_reduce_fusion
  116.6 0.2 convert_reduce_fusion
  116.8 0.0 copy-done.5
  116.8 0.1 select_reduce_fusion
  116.9 2.8 %convolution_convert_fusion.2 = bf16[512,256]{1,0:T(8,128)(2,1)} fusion(bf16[96,5632]{1,0:T(8,128)(2,1)} %get-tuple-element.12, bf16[5632,256]{1,0:T(8,128)(2,1)S(1)} %copy-done, s32[96]{0:T(128)S(1)} %multiply_add_fusion), kind=kOutput, calls=%fused_computation.4 | convolution fusion | flops 302194688 | bytes 4227456 | tf_op jit(solution)/shard_map/dot_general | solution.py:577
  119.7 29.2 %shard_map.112 = bf16[32,16,256]{2,1,0:T(8,128)(2,1)} custom-call(bf16[32,16,256]{2,1,0:T(8,128)(2,1)} %bitcast.50), custom_call_target="tpu_custom_call" | custom-call | tf_op jit(solution)/shard_map/pallas_call | solution.py:221
  148.9 1.7 %copy.13 = bf16[512,256]{1,0:T(8,128)(2,1)} copy(bf16[512,256]{1,0:T(8,128)(2,1)} %bitcast.51) | data formatting | bytes 524288
  (5 shorter events, 0.0 us)
Async XLA Ops:
  0.0 116.9 %copy-start = (bf16[5632,256]{1,0:T(8,128)(2,1)S(1)}, bf16[5632,256]{1,0:T(8,128)(2,1)}, u32[]{:S(2)}) copy-start(bf16[5632,256]{1,0:T(8,128)(2,1)} %param.18) | copy-start | bytes 8650756
  22.6 2.1 %copy-start.4 = (s32[384]{0:T(512)S(1)}, s32[384]{0:T(512)}, u32[]{:S(2)}) copy-start(s32[384]{0:T(512)} %param.12) | copy-start | bytes 4612
  24.7 0.7 copy-start.3
  26.1 2.7 %copy-start.1 = (bf16[384,44]{0,1:T(8,128)(2,1)S(1)}, bf16[384,44]{0,1:T(8,128)(2,1)}, u32[]{:S(2)}) copy-start(bf16[384,44]{0,1:T(8,128)(2,1)} %param.17) | copy-start | bytes 101380
  26.1 2.7 %copy-start.2 = (bf16[44,384]{1,0:T(8,128)(2,1)S(1)}, bf16[44,384]{1,0:T(8,128)(2,1)}, u32[]{:S(2)}) copy-start(bf16[44,384]{1,0:T(8,128)(2,1)} %param.16) | copy-start | bytes 101380
  85.9 30.9 %copy-start.5 = (s32[32]{0:T(128)S(1)}, s32[32]{0:T(128)}, u32[]{:S(2)}) copy-start(s32[32]{0:T(128)} %param.13) | copy-start | bytes 388

commit v17 on v15

--- a/solution.py
+++ b/solution.py
@@ -229,14 +229,14 @@
 
 
 def _mix_kernel(n, gain_row, part_ref, resid_ref, gain_ref, resid_out, out_ref, merged_out, held, mine_a,
-                mine_b, scatter_send, scatter_recv, gather_send, gather_recv):
+                mine_b, mine_c, scatter_send, scatter_recv, gather_send, gather_recv):
     me = lax.axis_index("feat")
     tok_index = lax.axis_index("tok")
     peers = [lax.rem(me + d, n) for d in range(1, n)]
     _greet(peers, tok_index)
-    split = 16
-    halves = [(0, split), (split, part_ref.shape[1] - split)]
-    mines = [mine_a, mine_b]
+    piece = part_ref.shape[1] // 3
+    halves = [(0, piece), (piece, piece), (2 * piece, piece)]
+    mines = [mine_a, mine_b, mine_c]
 
     def scatter_copy(half, peer, slot):
         first, size = halves[half]
@@ -254,10 +254,10 @@
             device_id=(tok_index, peer), device_id_type=MESH,
         )
 
-    for half in range(2):
+    for half in range(len(halves)):
         for peer in peers:
             scatter_copy(half, peer, me).start()
-    for half in range(2):
+    for half in range(len(halves)):
         first, size = halves[half]
         total = part_ref[me, first:first + size, :].astype(jnp.float32)
         for peer in peers:
@@ -273,7 +273,7 @@
         out_ref[me, first:first + size, :] = normed
         for peer in peers:
             gather_copy(half, peer, me).start()
-    for half in range(2):
+    for half in range(len(halves)):
         for peer in peers:
             gather_copy(half, peer, peer).wait_recv()
     group = 4
@@ -287,7 +287,7 @@
         merged_out[:, part * width:(part + 1) * width] = jnp.dot(
             pick, rows, preferred_element_type=jnp.float32
         ).astype(jnp.bfloat16)
-    for half in range(2):
+    for half in range(len(halves)):
         for peer in peers:
             scatter_copy(half, peer, me).wait_send()
             gather_copy(half, peer, me).wait_send()
@@ -306,12 +306,13 @@
         out_specs=(pl.BlockSpec(memory_space=pltpu.VMEM),) * 3,
         scratch_shapes=[
             pltpu.VMEM((n, rows, width), parts.dtype),
-            pltpu.VMEM((16, width), jnp.bfloat16),
-            pltpu.VMEM((rows - 16, width), jnp.bfloat16),
-            pltpu.SemaphoreType.DMA((2, n)),
-            pltpu.SemaphoreType.DMA((2, n)),
-            pltpu.SemaphoreType.DMA((2, n)),
-            pltpu.SemaphoreType.DMA((2, n)),
+            pltpu.VMEM((rows // 3, width), jnp.bfloat16),
+            pltpu.VMEM((rows // 3, width), jnp.bfloat16),
+            pltpu.VMEM((rows // 3, width), jnp.bfloat16),
+            pltpu.SemaphoreType.DMA((3, n)),
+            pltpu.SemaphoreType.DMA((3, n)),
+            pltpu.SemaphoreType.DMA((3, n)),
+            pltpu.SemaphoreType.DMA((3, n)),
         ],
         compiler_params=pltpu.CompilerParams(collective_id=collective_id, has_side_effects=True),
     )(parts, resid, gains)

time: 150 us -> 150 us (level)
  no operation moved by 1% of the time
where the time goes in v17:
time: 150 us; the launch traced here: 149 us
  Pallas kernels  132 us (88%)
  matrix products  13.4 us (9%)
  local copies, waits for them, and re-layouts  2.15 us (1%)
  other arithmetic  1.74 us (1%)
    pallas_call x1, Pallas kernels, mix_ring_feat(): pl.pallas_call(functools.partial(_mix_ring_kernel, n, gain_row), out_shap...  50.3 us
    pallas_call x1, Pallas kernels, mix_feat(): pl.pallas_call(functools.partial(_mix_kernel, n, gain_row), out_shape=(ja...  34.6 us
    pallas_call x1, Pallas kernels, route_exchange(): pl.pallas_call(functools.partial(_route_kernel, n), out_shape=jax.ShapeDt...  24.5 us
    pallas_call x1, Pallas kernels, norm_gather_feat(): pl.pallas_call(functools.partial(_norm_gather_kernel, n, gain_row), out_s...  22.6 us
    dot_general x1, matrix products, body(): lax.dot_general(hidden, lower_t, (((1,), (1,)), ((), ())), preferred_elem...  5.52 us

profile of v17, /device:TPU:1, one launch (start us, length us, event | category | flops | bytes accessed | tf_op | source)
XLA Modules:
  0.0 149.4 jit_solution(10579709376207431646)
XLA Ops:
  0.0 0.0 copy-start
  0.0 22.6 %shard_map.109 = bf16[16,24,1408]{2,1,0:T(8,128)(2,1)} custom-call(bf16[24,1408]{1,0:T(8,128)(2,1)} %resid_ref.1, bf16[1408]{0:T(1024)(128)(2,1)} %gain_ref.3), custom_call_target="tpu_custom_call" | custom-call | tf_op jit(solution)/shard_map/pallas_call | solution.py:445
  22.6 0.0 copy-start.4
  22.6 2.1 %fusion.91 = (bf16[384,3,1,88]{0,3,1,2:T(8,128)(2,1)S(1)}, f32[384,3,1,88]{0,3,1,2:T(8,128)S(1)}) fusion(bf16[384,1408,1]{1,0,2:T(8,128)(2,1)} %bitcast.49, bf16[1408,3,88]{0,2,1:T(8,128)(2,1)} %param.14), kind=kOutput, calls=%fused_computation.114 | convolution fusion | flops 285576192 | bytes 2433024 | tf_op jit(solution)/shard_map/dot_general | solution.py:606
  24.7 0.0 copy-start.3
  24.7 0.0 copy-done.4
  24.7 0.3 fusion.92
  25.0 0.4 copy-done.3
  25.3 0.7 fusion.19
  26.1 2.7 %convolution_convert_fusion.1 = bf16[384,1408]{1,0:T(8,128)(2,1)} fusion(bf16[88,1408]{1,0:T(8,128)(2,1)} %param.15, f32[384,384]{0,1:T(8,128)S(1)} %get-tuple-element.18, f32[384]{0:T(512)} %fusion.19, f32[384]{0:T(512)S(1)} %get-tuple-element.17, bf16[384,3,1,88]{0,3,1,2:T(8,128)(2,1)} %copy-done.3), kind=kOutput, calls=%fused_computation.1 | convolution fusion | flops 122127360 | bytes 1990144 | tf_op jit(solution)/shard_map/dot_general | solution.py:608
  28.7 0.0 copy-done.1
  28.7 0.0 copy-done.2
  28.8 0.6 pad_maximum_fusion.weight_ref
  29.4 50.3 %shard_map.110 = (bf16[24,1408]{1,0:T(8,128)(2,1)}, bf16[16,24,1408]{2,1,0:T(8,128)(2,1)}, bf16[1408,768]{1,0:T(8,128)(2,1)}) custom-call(bf16[16,24,1408]{2,1,0:T(8,128)(2,1)} %bitcast.47, bf16[24,1408]{1,0:T(8,128)(2,1)} %resid_ref.1, bf16[1408]{0:T(1024)(128)(2,1)} %gain_ref.4, bf16[44,768]{1,0:T(8,128)(2,1)} %pad_maximum_fusion.weight_ref), custom_call_target="tpu_custom_call" | custom-call | tf_op jit(solution)/shard_map/pallas_call | solution.py:390
  79.7 5.5 %convolution_convert_fusion = bf16[384,1408]{1,0:T(8,128)(2,1)} fusion(bf16[1408,768]{1,0:T(8,128)(2,1)} %get-tuple-element.10, bf16[384,1408]{1,0:T(8,128)(2,1)} %bitcast.53), kind=kOutput, calls=%fused_computation | convolution fusion | flops 840597504 | bytes 4325376 | tf_op jit(solution)/shard_map/dot_general | solution.py:619
  85.3 34.6 %shard_map.111 = (bf16[24,1408]{1,0:T(8,128)(2,1)}, bf16[16,24,1408]{2,1,0:T(8,128)(2,1)}, bf16[96,5632]{1,0:T(8,128)(2,1)}) custom-call(bf16[16,24,1408]{2,1,0:T(8,128)(2,1)} %bitcast.48, bf16[24,1408]{1,0:T(8,128)(2,1)} %get-tuple-element.11.resid_ref, bf16[1408]{0:T(1024)(128)(2,1)} %gain_ref.5), custom_call_target="tpu_custom_call" | custom-call | tf_op jit(solution)/shard_map/pallas_call | solution.py:298
  119.9 0.1 reshape.83
  120.0 0.1 subtract_reduce_fusion
  120.1 0.2 convert_reduce_fusion
  120.3 0.0 copy-done.5
  120.3 0.1 select_reduce_fusion
  120.4 2.8 %convolution_convert_fusion.2 = bf16[512,256]{1,0:T(8,128)(2,1)} fusion(bf16[96,5632]{1,0:T(8,128)(2,1)} %get-tuple-element.12, bf16[5632,256]{1,0:T(8,128)(2,1)S(1)} %copy-done, s32[96]{0:T(128)S(1)} %multiply_add_fusion), kind=kOutput, calls=%fused_computation.4 | convolution fusion | flops 302194688 | bytes 4227456 | tf_op jit(solution)/shard_map/dot_general | solution.py:578
  123.3 24.5 %shard_map.112 = bf16[32,16,256]{2,1,0:T(8,128)(2,1)} custom-call(bf16[32,16,256]{2,1,0:T(8,128)(2,1)} %bitcast.50), custom_call_target="tpu_custom_call" | custom-call | tf_op jit(solution)/shard_map/pallas_call | solution.py:221
  147.8 1.7 %copy.13 = bf16[512,256]{1,0:T(8,128)(2,1)} copy(bf16[512,256]{1,0:T(8,128)(2,1)} %bitcast.51) | data formatting | bytes 524288
  (5 shorter events, 0.0 us)
Async XLA Ops:
  0.0 120.4 %copy-start = (bf16[5632,256]{1,0:T(8,128)(2,1)S(1)}, bf16[5632,256]{1,0:T(8,128)(2,1)}, u32[]{:S(2)}) copy-start(bf16[5632,256]{1,0:T(8,128)(2,1)} %param.18) | copy-start | bytes 8650756
  22.6 2.1 %copy-start.4 = (s32[384]{0:T(512)S(1)}, s32[384]{0:T(512)}, u32[]{:S(2)}) copy-start(s32[384]{0:T(512)} %param.12) | copy-start | bytes 4612
  24.7 0.7 copy-start.3
  26.1 2.7 %copy-start.1 = (bf16[384,44]{0,1:T(8,128)(2,1)S(1)}, bf16[384,44]{0,1:T(8,128)(2,1)}, u32[]{:S(2)}) copy-start(bf16[384,44]{0,1:T(8,128)(2,1)} %param.17) | copy-start | bytes 101380
  26.1 2.7 %copy-start.2 = (bf16[44,384]{1,0:T(8,128)(2,1)S(1)}, bf16[44,384]{1,0:T(8,128)(2,1)}, u32[]{:S(2)}) copy-start(bf16[44,384]{1,0:T(8,128)(2,1)} %param.16) | copy-start | bytes 101380
  85.3 35.0 %copy-start.5 = (s32[32]{0:T(128)S(1)}, s32[32]{0:T(128)}, u32[]{:S(2)}) copy-start(s32[32]{0:T(128)} %param.13) | copy-start | bytes 388

commit v18 on v17

--- a/solution.py
+++ b/solution.py
@@ -193,7 +193,8 @@
 def _route_kernel(n, packed_ref, out_ref, send_sem, recv_sem):
     me = lax.axis_index("tok")
     feat_index = lax.axis_index("feat")
-    peers = [lax.rem(me + d, n) for d in range(1, n)]
+    order = sorted(range(1, n), key=lambda d: -min(d, n - d))
+    peers = [lax.rem(me + d, n) for d in order]
     barrier = pltpu.get_barrier_semaphore()
     for peer in peers:
         pl.semaphore_signal(barrier, inc=1, device_id=(peer, feat_index), device_id_type=MESH)

time: 150 us -> 148 us (0.987)
  Pallas kernels: 132 us -> 130 us
    pallas_call x1, Pallas kernels: 24.5 us -> 22.3 us  [route_exchange(): pl.pallas_call(functools.partial(_route_kernel, n), out_shape=jax.ShapeDt...]
where the time goes in v18:
time: 148 us; the launch traced here: 147 us
  Pallas kernels  130 us (88%)
  matrix products  13.4 us (9%)
  local copies, waits for them, and re-layouts  2.15 us (1%)
  other arithmetic  1.74 us (1%)
    pallas_call x1, Pallas kernels, mix_ring_feat(): pl.pallas_call(functools.partial(_mix_ring_kernel, n, gain_row), out_shap...  50.3 us
    pallas_call x1, Pallas kernels, mix_feat(): pl.pallas_call(functools.partial(_mix_kernel, n, gain_row), out_shape=(ja...  34.6 us
    pallas_call x1, Pallas kernels, norm_gather_feat(): pl.pallas_call(functools.partial(_norm_gather_kernel, n, gain_row), out_s...  22.6 us
    pallas_call x1, Pallas kernels, route_exchange(): pl.pallas_call(functools.partial(_route_kernel, n), out_shape=jax.ShapeDt...  22.3 us
    dot_general x1, matrix products, body(): lax.dot_general(hidden, lower_t, (((1,), (1,)), ((), ())), preferred_elem...  5.52 us

profile of v18, /device:TPU:1, one launch (start us, length us, event | category | flops | bytes accessed | tf_op | source)
XLA Modules:
  0.0 147.2 jit_solution(9057196406546806852)
XLA Ops:
  0.0 0.0 copy-start
  0.0 22.6 %shard_map.109 = bf16[16,24,1408]{2,1,0:T(8,128)(2,1)} custom-call(bf16[24,1408]{1,0:T(8,128)(2,1)} %resid_ref.1, bf16[1408]{0:T(1024)(128)(2,1)} %gain_ref.3), custom_call_target="tpu_custom_call" | custom-call | tf_op jit(solution)/shard_map/pallas_call | solution.py:446
  22.6 0.0 copy-start.4
  22.6 2.1 %fusion.91 = (bf16[384,3,1,88]{0,3,1,2:T(8,128)(2,1)S(1)}, f32[384,3,1,88]{0,3,1,2:T(8,128)S(1)}) fusion(bf16[384,1408,1]{1,0,2:T(8,128)(2,1)} %bitcast.49, bf16[1408,3,88]{0,2,1:T(8,128)(2,1)} %param.14), kind=kOutput, calls=%fused_computation.114 | convolution fusion | flops 285576192 | bytes 2433024 | tf_op jit(solution)/shard_map/dot_general | solution.py:607
  24.7 0.0 copy-start.3
  24.7 0.0 copy-done.4
  24.7 0.3 fusion.92
  25.0 0.4 copy-done.3
  25.3 0.7 fusion.19
  26.1 2.7 %convolution_convert_fusion.1 = bf16[384,1408]{1,0:T(8,128)(2,1)} fusion(bf16[88,1408]{1,0:T(8,128)(2,1)} %param.15, f32[384,384]{0,1:T(8,128)S(1)} %get-tuple-element.18, f32[384]{0:T(512)} %fusion.19, f32[384]{0:T(512)S(1)} %get-tuple-element.17, bf16[384,3,1,88]{0,3,1,2:T(8,128)(2,1)} %copy-done.3), kind=kOutput, calls=%fused_computation.1 | convolution fusion | flops 122127360 | bytes 1990144 | tf_op jit(solution)/shard_map/dot_general | solution.py:609
  28.7 0.0 copy-done.1
  28.7 0.0 copy-done.2
  28.8 0.6 pad_maximum_fusion.weight_ref
  29.4 50.3 %shard_map.110 = (bf16[24,1408]{1,0:T(8,128)(2,1)}, bf16[16,24,1408]{2,1,0:T(8,128)(2,1)}, bf16[1408,768]{1,0:T(8,128)(2,1)}) custom-call(bf16[16,24,1408]{2,1,0:T(8,128)(2,1)} %bitcast.47, bf16[24,1408]{1,0:T(8,128)(2,1)} %resid_ref.1, bf16[1408]{0:T(1024)(128)(2,1)} %gain_ref.4, bf16[44,768]{1,0:T(8,128)(2,1)} %pad_maximum_fusion.weight_ref), custom_call_target="tpu_custom_call" | custom-call | tf_op jit(solution)/shard_map/pallas_call | solution.py:391
  79.7 5.5 %convolution_convert_fusion = bf16[384,1408]{1,0:T(8,128)(2,1)} fusion(bf16[1408,768]{1,0:T(8,128)(2,1)} %get-tuple-element.10, bf16[384,1408]{1,0:T(8,128)(2,1)} %bitcast.53), kind=kOutput, calls=%fused_computation | convolution fusion | flops 840597504 | bytes 4325376 | tf_op jit(solution)/shard_map/dot_general | solution.py:620
  85.3 34.6 %shard_map.111 = (bf16[24,1408]{1,0:T(8,128)(2,1)}, bf16[16,24,1408]{2,1,0:T(8,128)(2,1)}, bf16[96,5632]{1,0:T(8,128)(2,1)}) custom-call(bf16[16,24,1408]{2,1,0:T(8,128)(2,1)} %bitcast.48, bf16[24,1408]{1,0:T(8,128)(2,1)} %get-tuple-element.11.resid_ref, bf16[1408]{0:T(1024)(128)(2,1)} %gain_ref.5), custom_call_target="tpu_custom_call" | custom-call | tf_op jit(solution)/shard_map/pallas_call | solution.py:299
  119.9 0.1 reshape.83
  120.0 0.1 subtract_reduce_fusion
  120.1 0.2 convert_reduce_fusion
  120.3 0.0 copy-done.5
  120.3 0.1 select_reduce_fusion
  120.4 2.8 %convolution_convert_fusion.2 = bf16[512,256]{1,0:T(8,128)(2,1)} fusion(bf16[96,5632]{1,0:T(8,128)(2,1)} %get-tuple-element.12, bf16[5632,256]{1,0:T(8,128)(2,1)S(1)} %copy-done, s32[96]{0:T(128)S(1)} %multiply_add_fusion), kind=kOutput, calls=%fused_computation.4 | convolution fusion | flops 302194688 | bytes 4227456 | tf_op jit(solution)/shard_map/dot_general | solution.py:579
  123.3 22.3 %shard_map.112 = bf16[32,16,256]{2,1,0:T(8,128)(2,1)} custom-call(bf16[32,16,256]{2,1,0:T(8,128)(2,1)} %bitcast.50), custom_call_target="tpu_custom_call" | custom-call | tf_op jit(solution)/shard_map/pallas_call | solution.py:222
  145.5 1.7 %copy.13 = bf16[512,256]{1,0:T(8,128)(2,1)} copy(bf16[512,256]{1,0:T(8,128)(2,1)} %bitcast.51) | data formatting | bytes 524288
  (5 shorter events, 0.0 us)
Async XLA Ops:
  0.0 120.4 %copy-start = (bf16[5632,256]{1,0:T(8,128)(2,1)S(1)}, bf16[5632,256]{1,0:T(8,128)(2,1)}, u32[]{:S(2)}) copy-start(bf16[5632,256]{1,0:T(8,128)(2,1)} %param.18) | copy-start | bytes 8650756
  22.6 2.1 %copy-start.4 = (s32[384]{0:T(512)S(1)}, s32[384]{0:T(512)}, u32[]{:S(2)}) copy-start(s32[384]{0:T(512)} %param.12) | copy-start | bytes 4612
  24.7 0.7 copy-start.3
  26.1 2.7 %copy-start.1 = (bf16[384,44]{0,1:T(8,128)(2,1)S(1)}, bf16[384,44]{0,1:T(8,128)(2,1)}, u32[]{:S(2)}) copy-start(bf16[384,44]{0,1:T(8,128)(2,1)} %param.17) | copy-start | bytes 101380
  26.1 2.7 %copy-start.2 = (bf16[44,384]{1,0:T(8,128)(2,1)S(1)}, bf16[44,384]{1,0:T(8,128)(2,1)}, u32[]{:S(2)}) copy-start(bf16[44,384]{1,0:T(8,128)(2,1)} %param.16) | copy-start | bytes 101380
  85.3 35.0 %copy-start.5 = (s32[32]{0:T(128)S(1)}, s32[32]{0:T(128)}, u32[]{:S(2)}) copy-start(s32[32]{0:T(128)} %param.13) | copy-start | bytes 388

commit v19 on v18

--- a/solution.py
+++ b/solution.py
@@ -7,6 +7,16 @@
 from jax.sharding import PartitionSpec as P
 
 
+def _feat_peers(n, me):
+    side = int(round(n ** 0.5))
+    if side * side != n:
+        return [lax.rem(me + d, n) for d in range(1, n)]
+    offsets = [(dy, dx) for dy in range(side) for dx in range(side) if (dy, dx) != (0, 0)]
+    offsets.sort(key=lambda o: -(min(o[0], side - o[0]) + min(o[1], side - o[1])))
+    row, col = me // side, me % side
+    return [lax.rem(row + dy, side) * side + lax.rem(col + dx, side) for dy, dx in offsets]
+
+
 def _greet(peers, tok_index):
     barrier = pltpu.get_barrier_semaphore()
     for peer in peers:
@@ -17,7 +27,7 @@
 def _gather_kernel(n, row_ref, out_ref, send_sem, recv_sem):
     me = lax.axis_index("feat")
     tok_index = lax.axis_index("tok")
-    peers = [lax.rem(me + d, n) for d in range(1, n)]
+    peers = _feat_peers(n, me)
     _greet(peers, tok_index)
     for peer in peers:
         pltpu.make_async_remote_copy(
@@ -233,7 +243,7 @@
                 mine_b, mine_c, scatter_send, scatter_recv, gather_send, gather_recv):
     me = lax.axis_index("feat")
     tok_index = lax.axis_index("tok")
-    peers = [lax.rem(me + d, n) for d in range(1, n)]
+    peers = _feat_peers(n, me)
     _greet(peers, tok_index)
     piece = part_ref.shape[1] // 3
     halves = [(0, piece), (piece, piece), (2 * piece, piece)]
@@ -418,7 +428,7 @@
 def _norm_gather_kernel(n, gain_row, tok_ref, gain_ref, out_ref, mine, send_sem, recv_sem):
     me = lax.axis_index("feat")
     tok_index = lax.axis_index("tok")
-    peers = [lax.rem(me + d, n) for d in range(1, n)]
+    peers = _feat_peers(n, me)
     _greet(peers, tok_index)
     as_float = tok_ref[...].astype(jnp.float32)
     center = jnp.mean(as_float, axis=-1, keepdims=True)
@@ -460,7 +470,7 @@
 def _scatter_kernel(n, part_ref, out_ref, held, send_sem, recv_sem):
     me = lax.axis_index("feat")
     tok_index = lax.axis_index("tok")
-    peers = [lax.rem(me + d, n) for d in range(1, n)]
+    peers = _feat_peers(n, me)
     _greet(peers, tok_index)
     for peer in peers:
         pltpu.make_async_remote_copy(

time: 148 us -> 145 us (0.980)
  Pallas kernels: 130 us -> 128 us
    pallas_call x1, Pallas kernels: 50.3 us -> 47.3 us  [mix_ring_feat(): pl.pallas_call(functools.partial(_mix_ring_kernel, n, gain_row), out_shap...]
    pallas_call x1, Pallas kernels: 34.6 us -> 36.1 us  [mix_feat(): pl.pallas_call(functools.partial(_mix_kernel, n, gain_row), out_shape=(ja...]
where the time goes in v19:
time: 145 us
  Pallas kernels  128 us (88%)
  matrix products  13.4 us (9%)
  local copies, waits for them, and re-layouts  2.15 us (1%)
  other arithmetic  1.74 us (1%)
    pallas_call x1, Pallas kernels, mix_ring_feat(): pl.pallas_call(functools.partial(_mix_ring_kernel, n, gain_row), out_shap...  47.3 us
    pallas_call x1, Pallas kernels, mix_feat(): pl.pallas_call(functools.partial(_mix_kernel, n, gain_row), out_shape=(ja...  36.1 us
    pallas_call x1, Pallas kernels, norm_gather_feat(): pl.pallas_call(functools.partial(_norm_gather_kernel, n, gain_row), out_s...  22.8 us
    pallas_call x1, Pallas kernels, route_exchange(): pl.pallas_call(functools.partial(_route_kernel, n), out_shape=jax.ShapeDt...  21.3 us
    dot_general x1, matrix products, body(): lax.dot_general(hidden, lower_t, (((1,), (1,)), ((), ())), preferred_elem...  5.52 us

profile of v19, /device:TPU:1, one launch (start us, length us, event | category | flops | bytes accessed | tf_op | source)
XLA Modules:
  0.0 145.0 jit_solution(7316588762141596364)
XLA Ops:
  0.0 0.0 copy-start
  0.0 22.8 %shard_map.109 = bf16[16,24,1408]{2,1,0:T(8,128)(2,1)} custom-call(bf16[24,1408]{1,0:T(8,128)(2,1)} %resid_ref.1, bf16[1408]{0:T(1024)(128)(2,1)} %gain_ref.3), custom_call_target="tpu_custom_call" | custom-call | tf_op jit(solution)/shard_map/pallas_call | solution.py:456
  22.9 0.0 copy-start.4
  22.9 2.1 %fusion.91 = (bf16[384,3,1,88]{0,3,1,2:T(8,128)(2,1)S(1)}, f32[384,3,1,88]{0,3,1,2:T(8,128)S(1)}) fusion(bf16[384,1408,1]{1,0,2:T(8,128)(2,1)} %bitcast.49, bf16[1408,3,88]{0,2,1:T(8,128)(2,1)} %param.14), kind=kOutput, calls=%fused_computation.114 | convolution fusion | flops 285576192 | bytes 2433024 | tf_op jit(solution)/shard_map/dot_general | solution.py:617
  24.9 0.0 copy-start.3
  24.9 0.0 copy-done.4
  24.9 0.3 fusion.92
  25.2 0.4 copy-done.3
  25.6 0.7 fusion.19
  26.3 2.7 %convolution_convert_fusion.1 = bf16[384,1408]{1,0:T(8,128)(2,1)} fusion(bf16[88,1408]{1,0:T(8,128)(2,1)} %param.15, f32[384,384]{0,1:T(8,128)S(1)} %get-tuple-element.18, f32[384]{0:T(512)} %fusion.19, f32[384]{0:T(512)S(1)} %get-tuple-element.17, bf16[384,3,1,88]{0,3,1,2:T(8,128)(2,1)} %copy-done.3), kind=kOutput, calls=%fused_computation.1 | convolution fusion | flops 122127360 | bytes 1990144 | tf_op jit(solution)/shard_map/dot_general | solution.py:619
  29.0 0.0 copy-done.1
  29.0 0.0 copy-done.2
  29.0 0.6 pad_maximum_fusion.weight_ref
  29.7 47.3 %shard_map.110 = (bf16[24,1408]{1,0:T(8,128)(2,1)}, bf16[16,24,1408]{2,1,0:T(8,128)(2,1)}, bf16[1408,768]{1,0:T(8,128)(2,1)}) custom-call(bf16[16,24,1408]{2,1,0:T(8,128)(2,1)} %bitcast.47, bf16[24,1408]{1,0:T(8,128)(2,1)} %resid_ref.1, bf16[1408]{0:T(1024)(128)(2,1)} %gain_ref.4, bf16[44,768]{1,0:T(8,128)(2,1)} %pad_maximum_fusion.weight_ref), custom_call_target="tpu_custom_call" | custom-call | tf_op jit(solution)/shard_map/pallas_call | solution.py:401
  77.0 5.5 %convolution_convert_fusion = bf16[384,1408]{1,0:T(8,128)(2,1)} fusion(bf16[1408,768]{1,0:T(8,128)(2,1)} %get-tuple-element.10, bf16[384,1408]{1,0:T(8,128)(2,1)} %bitcast.53), kind=kOutput, calls=%fused_computation | convolution fusion | flops 840597504 | bytes 4325376 | tf_op jit(solution)/shard_map/dot_general | solution.py:630
  82.5 36.1 %shard_map.111 = (bf16[24,1408]{1,0:T(8,128)(2,1)}, bf16[16,24,1408]{2,1,0:T(8,128)(2,1)}, bf16[96,5632]{1,0:T(8,128)(2,1)}) custom-call(bf16[16,24,1408]{2,1,0:T(8,128)(2,1)} %bitcast.48, bf16[24,1408]{1,0:T(8,128)(2,1)} %get-tuple-element.11.resid_ref, bf16[1408]{0:T(1024)(128)(2,1)} %gain_ref.5), custom_call_target="tpu_custom_call" | custom-call | tf_op jit(solution)/shard_map/pallas_call | solution.py:309
  118.6 0.1 reshape.83
  118.8 0.1 subtract_reduce_fusion
  118.9 0.2 convert_reduce_fusion
  119.0 0.0 copy-done.5
  119.1 0.1 select_reduce_fusion
  119.2 2.8 %convolution_convert_fusion.2 = bf16[512,256]{1,0:T(8,128)(2,1)} fusion(bf16[96,5632]{1,0:T(8,128)(2,1)} %get-tuple-element.12, bf16[5632,256]{1,0:T(8,128)(2,1)S(1)} %copy-done, s32[96]{0:T(128)S(1)} %multiply_add_fusion), kind=kOutput, calls=%fused_computation.4 | convolution fusion | flops 302194688 | bytes 4227456 | tf_op jit(solution)/shard_map/dot_general | solution.py:589
  122.0 21.3 %shard_map.112 = bf16[32,16,256]{2,1,0:T(8,128)(2,1)} custom-call(bf16[32,16,256]{2,1,0:T(8,128)(2,1)} %bitcast.50), custom_call_target="tpu_custom_call" | custom-call | tf_op jit(solution)/shard_map/pallas_call | solution.py:232
  143.3 1.7 %copy.13 = bf16[512,256]{1,0:T(8,128)(2,1)} copy(bf16[512,256]{1,0:T(8,128)(2,1)} %bitcast.51) | data formatting | bytes 524288
  (5 shorter events, 0.0 us)
Async XLA Ops:
  0.0 119.2 %copy-start = (bf16[5632,256]{1,0:T(8,128)(2,1)S(1)}, bf16[5632,256]{1,0:T(8,128)(2,1)}, u32[]{:S(2)}) copy-start(bf16[5632,256]{1,0:T(8,128)(2,1)} %param.18) | copy-start | bytes 8650756
  22.9 2.1 %copy-start.4 = (s32[384]{0:T(512)S(1)}, s32[384]{0:T(512)}, u32[]{:S(2)}) copy-start(s32[384]{0:T(512)} %param.12) | copy-start | bytes 4612
  24.9 0.7 copy-start.3
  26.3 2.7 %copy-start.1 = (bf16[384,44]{0,1:T(8,128)(2,1)S(1)}, bf16[384,44]{0,1:T(8,128)(2,1)}, u32[]{:S(2)}) copy-start(bf16[384,44]{0,1:T(8,128)(2,1)} %param.17) | copy-start | bytes 101380
  26.3 2.7 %copy-start.2 = (bf16[44,384]{1,0:T(8,128)(2,1)S(1)}, bf16[44,384]{1,0:T(8,128)(2,1)}, u32[]{:S(2)}) copy-start(bf16[44,384]{1,0:T(8,128)(2,1)} %param.16) | copy-start | bytes 101380
  82.5 36.6 %copy-start.5 = (s32[32]{0:T(128)S(1)}, s32[32]{0:T(128)}, u32[]{:S(2)}) copy-start(s32[32]{0:T(128)} %param.13) | copy-start | bytes 388

commit v20 on v19

--- a/solution.py
+++ b/solution.py
@@ -383,7 +383,7 @@
             gather_copy(peer, me).start()
 
     _ring_gather(weight_ref, weight_out, send_right, send_left, send_partner, weight_recv, me,
-                 hook=norm_and_send, hook_step=5)
+                 hook=norm_and_send, hook_step=4)
     block_rows = weight_out.shape[1]
     for slot in range(weight_out.shape[0]):
         weight_flat[slot * block_rows:(slot + 1) * block_rows, :] = weight_out[slot]

time: 145 us -> 147 us (1.014)
  Pallas kernels: 128 us -> 130 us
    pallas_call x1, Pallas kernels: 21.3 us -> 23 us  [route_exchange(): pl.pallas_call(functools.partial(_route_kernel, n), out_shape=jax.ShapeDt...]
where the time goes in v20:
time: 147 us
  Pallas kernels  130 us (88%)
  matrix products  13.4 us (9%)
  local copies, waits for them, and re-layouts  2.15 us (1%)
  other arithmetic  1.74 us (1%)
    pallas_call x1, Pallas kernels, mix_ring_feat(): pl.pallas_call(functools.partial(_mix_ring_kernel, n, gain_row), out_shap...  47.3 us
    pallas_call x1, Pallas kernels, mix_feat(): pl.pallas_call(functools.partial(_mix_kernel, n, gain_row), out_shape=(ja...  36.5 us
    pallas_call x1, Pallas kernels, route_exchange(): pl.pallas_call(functools.partial(_route_kernel, n), out_shape=jax.ShapeDt...  23 us
    pallas_call x1, Pallas kernels, norm_gather_feat(): pl.pallas_call(functools.partial(_norm_gather_kernel, n, gain_row), out_s...  22.8 us
    dot_general x1, matrix products, body(): lax.dot_general(hidden, lower_t, (((1,), (1,)), ((), ())), preferred_elem...  5.52 us

profile of v20, /device:TPU:1, one launch (start us, length us, event | category | flops | bytes accessed | tf_op | source)
XLA Modules:
  0.0 147.0 jit_solution(5542001086127818137)
XLA Ops:
  0.0 0.0 copy-start
  0.0 22.8 %shard_map.109 = bf16[16,24,1408]{2,1,0:T(8,128)(2,1)} custom-call(bf16[24,1408]{1,0:T(8,128)(2,1)} %resid_ref.1, bf16[1408]{0:T(1024)(128)(2,1)} %gain_ref.3), custom_call_target="tpu_custom_call" | custom-call | tf_op jit(solution)/shard_map/pallas_call | solution.py:456
  22.9 0.0 copy-start.4
  22.9 2.1 %fusion.91 = (bf16[384,3,1,88]{0,3,1,2:T(8,128)(2,1)S(1)}, f32[384,3,1,88]{0,3,1,2:T(8,128)S(1)}) fusion(bf16[384,1408,1]{1,0,2:T(8,128)(2,1)} %bitcast.49, bf16[1408,3,88]{0,2,1:T(8,128)(2,1)} %param.14), kind=kOutput, calls=%fused_computation.114 | convolution fusion | flops 285576192 | bytes 2433024 | tf_op jit(solution)/shard_map/dot_general | solution.py:617
  24.9 0.0 copy-start.3
  24.9 0.0 copy-done.4
  24.9 0.3 fusion.92
  25.2 0.4 copy-done.3
  25.6 0.7 fusion.19
  26.3 2.7 %convolution_convert_fusion.1 = bf16[384,1408]{1,0:T(8,128)(2,1)} fusion(bf16[88,1408]{1,0:T(8,128)(2,1)} %param.15, f32[384,384]{0,1:T(8,128)S(1)} %get-tuple-element.18, f32[384]{0:T(512)} %fusion.19, f32[384]{0:T(512)S(1)} %get-tuple-element.17, bf16[384,3,1,88]{0,3,1,2:T(8,128)(2,1)} %copy-done.3), kind=kOutput, calls=%fused_computation.1 | convolution fusion | flops 122127360 | bytes 1990144 | tf_op jit(solution)/shard_map/dot_general | solution.py:619
  29.0 0.0 copy-done.1
  29.0 0.6 pad_maximum_fusion.weight_ref
  29.7 47.3 %shard_map.110 = (bf16[24,1408]{1,0:T(8,128)(2,1)}, bf16[16,24,1408]{2,1,0:T(8,128)(2,1)}, bf16[1408,768]{1,0:T(8,128)(2,1)}) custom-call(bf16[16,24,1408]{2,1,0:T(8,128)(2,1)} %bitcast.47, bf16[24,1408]{1,0:T(8,128)(2,1)} %resid_ref.1, bf16[1408]{0:T(1024)(128)(2,1)} %gain_ref.4, bf16[44,768]{1,0:T(8,128)(2,1)} %pad_maximum_fusion.weight_ref), custom_call_target="tpu_custom_call" | custom-call | tf_op jit(solution)/shard_map/pallas_call | solution.py:401
  76.9 5.5 %convolution_convert_fusion = bf16[384,1408]{1,0:T(8,128)(2,1)} fusion(bf16[1408,768]{1,0:T(8,128)(2,1)} %get-tuple-element.10, bf16[384,1408]{1,0:T(8,128)(2,1)} %bitcast.53), kind=kOutput, calls=%fused_computation | convolution fusion | flops 840597504 | bytes 4325376 | tf_op jit(solution)/shard_map/dot_general | solution.py:630
  82.5 36.5 %shard_map.111 = (bf16[24,1408]{1,0:T(8,128)(2,1)}, bf16[16,24,1408]{2,1,0:T(8,128)(2,1)}, bf16[96,5632]{1,0:T(8,128)(2,1)}) custom-call(bf16[16,24,1408]{2,1,0:T(8,128)(2,1)} %bitcast.48, bf16[24,1408]{1,0:T(8,128)(2,1)} %get-tuple-element.11.resid_ref, bf16[1408]{0:T(1024)(128)(2,1)} %gain_ref.5), custom_call_target="tpu_custom_call" | custom-call | tf_op jit(solution)/shard_map/pallas_call | solution.py:309
  118.9 0.1 reshape.83
  119.0 0.1 subtract_reduce_fusion
  119.1 0.2 convert_reduce_fusion
  119.3 0.0 copy-done.5
  119.3 0.1 select_reduce_fusion
  119.4 0.0 copy-done
  119.5 2.8 %convolution_convert_fusion.2 = bf16[512,256]{1,0:T(8,128)(2,1)} fusion(bf16[96,5632]{1,0:T(8,128)(2,1)} %get-tuple-element.12, bf16[5632,256]{1,0:T(8,128)(2,1)S(1)} %copy-done, s32[96]{0:T(128)S(1)} %multiply_add_fusion), kind=kOutput, calls=%fused_computation.4 | convolution fusion | flops 302194688 | bytes 4227456 | tf_op jit(solution)/shard_map/dot_general | solution.py:589
  122.3 23.0 %shard_map.112 = bf16[32,16,256]{2,1,0:T(8,128)(2,1)} custom-call(bf16[32,16,256]{2,1,0:T(8,128)(2,1)} %bitcast.50), custom_call_target="tpu_custom_call" | custom-call | tf_op jit(solution)/shard_map/pallas_call | solution.py:232
  145.3 1.7 %copy.13 = bf16[512,256]{1,0:T(8,128)(2,1)} copy(bf16[512,256]{1,0:T(8,128)(2,1)} %bitcast.51) | data formatting | bytes 524288
  (5 shorter events, 0.0 us)
Async XLA Ops:
  0.0 119.4 %copy-start = (bf16[5632,256]{1,0:T(8,128)(2,1)S(1)}, bf16[5632,256]{1,0:T(8,128)(2,1)}, u32[]{:S(2)}) copy-start(bf16[5632,256]{1,0:T(8,128)(2,1)} %param.18) | copy-start | bytes 8650756
  22.9 2.1 %copy-start.4 = (s32[384]{0:T(512)S(1)}, s32[384]{0:T(512)}, u32[]{:S(2)}) copy-start(s32[384]{0:T(512)} %param.12) | copy-start | bytes 4612
  24.9 0.7 copy-start.3
  26.3 2.7 %copy-start.1 = (bf16[384,44]{0,1:T(8,128)(2,1)S(1)}, bf16[384,44]{0,1:T(8,128)(2,1)}, u32[]{:S(2)}) copy-start(bf16[384,44]{0,1:T(8,128)(2,1)} %param.17) | copy-start | bytes 101380
  26.3 2.7 %copy-start.2 = (bf16[44,384]{1,0:T(8,128)(2,1)S(1)}, bf16[44,384]{1,0:T(8,128)(2,1)}, u32[]{:S(2)}) copy-start(bf16[44,384]{1,0:T(8,128)(2,1)} %param.16) | copy-start | bytes 101380
  82.4 36.9 %copy-start.5 = (s32[32]{0:T(128)S(1)}, s32[32]{0:T(128)}, u32[]{:S(2)}) copy-start(s32[32]{0:T(128)} %param.13) | copy-start | bytes 388
